TPU v7x, 32 devices: a whole 2x2x4 slice. The times are simulated.
32 devices in a mesh: dp: 8 (over z, y), mp: 4 (over x, core).
Axes of the slice: x: 2, y: 2, z: 4, core: 2. Of those that a mesh axis runs over, the one named last changes fastest.
Arguments:
- tokens: bfloat16 [32, 256, 1152], P('dp'), may hold values from -6 to 6
- condition: bfloat16 [32, 1152], P('dp'), may hold values from -6 to 6
- cotangent: bfloat16 [32, 256, 1152], P('dp'), may hold values from -12 to 12
- kept_index: int32 [32, 128], P('dp'), may hold values from 0 to 255, as said below
- skip_index: int32 [32, 128], P('dp'), may hold values from 0 to 255, as said below
- step_count: int32 [1], replicated, may hold values from 1 to 20
- ada_weight: float32 [1152, 6, 1152], P('dp', None, 'mp'), may hold values from -0.1875 to 0.1875
- qkv_weight: float32 [3, 1152, 1152], P(None, 'dp', 'mp'), may hold values from -0.1875 to 0.1875
- proj_weight: float32 [1152, 1152], P('mp', 'dp'), may hold values from -1 to 1
- fc1_weight: float32 [1152, 4608], P('dp', 'mp'), may hold values from -0.1875 to 0.1875
- fc2_weight: float32 [4608, 1152], P('mp', 'dp'), may hold values from -0.09375 to 0.09375
- ada_moment: float32 [1152, 6, 1152], P('dp', None, 'mp'), may hold values from -80 to 80
- qkv_moment: float32 [3, 1152, 1152], P(None, 'dp', 'mp'), may hold values from -80 to 80
- proj_moment: float32 [1152, 1152], P('mp', 'dp'), may hold values from -80 to 80
- fc1_moment: float32 [1152, 4608], P('dp', 'mp'), may hold values from -80 to 80
- fc2_moment: float32 [4608, 1152], P('mp', 'dp'), may hold values from -80 to 80
- ada_average: float32 [1152, 6, 1152], P('dp', None, 'mp'), may hold values from -0.1875 to 0.1875
- qkv_average: float32 [3, 1152, 1152], P(None, 'dp', 'mp'), may hold values from -0.1875 to 0.1875
- proj_average: float32 [1152, 1152], P('mp', 'dp'), may hold values from -1 to 1
- fc1_average: float32 [1152, 4608], P('dp', 'mp'), may hold values from -0.1875 to 0.1875
- fc2_average: float32 [4608, 1152], P('mp', 'dp'), may hold values from -0.09375 to 0.09375
Outputs:
- block_out: bfloat16 [32, 256, 1152], P('dp')
- tokens_grad: float32 [32, 256, 1152], P('dp')
- condition_grad: float32 [32, 1152], P('dp')
- ada_master: float32 [1152, 6, 1152], P('dp', None, 'mp')
- qkv_master: float32 [3, 1152, 1152], P(None, 'dp', 'mp')
- proj_master: float32 [1152, 1152], P('mp', 'dp')
- fc1_master: float32 [1152, 4608], P('dp', 'mp')
- fc2_master: float32 [4608, 1152], P('mp', 'dp')
- ada_momentum: float32 [1152, 6, 1152], P('dp', None, 'mp')
- qkv_momentum: float32 [3, 1152, 1152], P(None, 'dp', 'mp')
- proj_momentum: float32 [1152, 1152], P('mp', 'dp')
- fc1_momentum: float32 [1152, 4608], P('dp', 'mp')
- fc2_momentum: float32 [4608, 1152], P('mp', 'dp')
- ada_ema: float32 [1152, 6, 1152], P('dp', None, 'mp')
- qkv_ema: float32 [3, 1152, 1152], P(None, 'dp', 'mp')
- proj_ema: float32 [1152, 1152], P('mp', 'dp')
- fc1_ema: float32 [1152, 4608], P('dp', 'mp')
- fc2_ema: float32 [4608, 1152], P('mp', 'dp')
Inputs may be any that keep to these rules, and one draw needn't show every extreme that they name: `kept_index`: row b lists 128 distinct positions of image b in increasing order; row b of skip_index lists the other 128 positions in increasing order. `skip_index`: row b lists the positions of image b that kept_index does not, in increasing order.
All inputs are finite; a program needn't handle non-finite values.
Results may differ from a plain program's by a relative error of at most 0.012.
The roundings to bfloat16 on the way count: a program that leaves them out, or rounds other values in their place, can miss the bound.
Values may be sent and summed in bfloat16 or wider, within the bound.
No kernel may reach another device: no remote copies, remote signals or barrier semaphores. Data moves between devices by JAX's collectives and lax.ppermute only.
A program may use at most 192 MiB of HBM per device.

v0:
```python
from functools import partial
import math

import jax
import jax.numpy as jnp
from jax import lax
from jax.experimental import pallas as pl
from jax.experimental.pallas import tpu as pltpu
from jax.sharding import PartitionSpec as P

HEAD_DIM = 72

epsilon = 1e-06
momentum_rate = 0.9

f32 = jnp.float32
bf16 = jnp.bfloat16


def layer_norm(values):
    centered = values - jnp.mean(values, axis=-1, keepdims=True)
    inverse = lax.rsqrt(jnp.mean(centered * centered, axis=-1, keepdims=True) + epsilon)
    return (centered * inverse, inverse)


def norm_back(normed, inverse, gradient):
    return inverse * (
        gradient
        - jnp.mean(gradient, axis=-1, keepdims=True)
        - normed * jnp.mean(gradient * normed, axis=-1, keepdims=True)
    )


def swap_core(values):
    return lax.ppermute(values, "mp", [(j, j ^ 1) for j in range(4)])


def swap_x(values):
    return lax.ppermute(values, "mp", [(j, j ^ 2) for j in range(4)])


def join_pair(own, other, core, axis=0):
    return jnp.where(
        core == 0,
        jnp.concatenate([own, other], axis),
        jnp.concatenate([other, own], axis),
    )


def spread_pair(own, core):
    return join_pair(own, swap_core(own), core)


def swap_dp(values, bit):
    size = lax.axis_size("dp")
    return lax.ppermute(values, "dp", [(i, i ^ bit) for i in range(size)])


def dp_groups():
    size = lax.axis_size("dp")
    return [4] + [2] * (size.bit_length() - 3)


def spread_round(values, axis, level):
    groups = dp_groups()
    step = math.prod(groups[:level])
    others = [swap_dp(values, step * b) for b in range(1, groups[level])]
    return jnp.concatenate([values] + others, axis)


def sum_round(values, axis, level):
    groups = dp_groups()
    step = math.prod(groups[:level])
    blocks = jnp.split(values, groups[level], axis)
    total = blocks[0]
    for b in range(1, groups[level]):
        total = total + swap_dp(blocks[b], step * b)
    return total


def turn_round(values, level):
    groups = dp_groups()
    step = math.prod(groups[:level])
    shape = values.shape
    values = values.reshape((-1, groups[level], step) + shape[1:])
    blocks = [values[:, b] for b in range(groups[level])]
    blocks = [blocks[0]] + [swap_dp(blocks[b], step * b) for b in range(1, groups[level])]
    return jnp.stack(blocks, 1).reshape(shape)


def in_order(values):
    index = lax.axis_index("dp")
    shape = values.shape
    count = shape[0].bit_length() - 1
    values = values.reshape((2,) * count + shape[1:])
    for axis in range(count):
        values = jnp.where((index >> (count - 1 - axis)) & 1, jnp.flip(values, axis), values)
    return values.reshape(shape)


def ring_tables():
    cycle = [0, 2, 4, 6, 7, 5, 3, 1]
    clockwise = [(cycle[i], cycle[(i + 1) % 8]) for i in range(8)]
    return clockwise, [(b, a) for a, b in clockwise]


def ring_place_of(index):
    return jnp.where((index & 1) == 0, index >> 1, 7 - (index >> 1))


def ring_device(place):
    place = lax.rem(place, 8)
    return jnp.where(place < 4, 2 * place, 2 * (7 - place) + 1)


def hop(values, direction):
    clockwise, backward = ring_tables()
    return lax.ppermute(values, "dp", clockwise if direction > 0 else backward)


def ring_device_at(index, distance):
    return ring_device(ring_place_of(index) + distance + 8)


class Gather:
    def __init__(self, shard, lead):
        self.lead = lead
        self.shard = shard
        self.ahead = [shard]
        self.behind = [shard]

    def start(self, sides):
        moving = []
        if "a" in sides:
            moving.append(hop(self.ahead[-1], self.lead))
        if "b" in sides:
            moving.append(hop(self.behind[-1], -self.lead))
        return tuple(moving)

    def finish(self, sides, moved):
        moved = list(moved)
        if "a" in sides:
            self.ahead.append(moved.pop(0))
        if "b" in sides:
            self.behind.append(moved.pop(0))

    def pieces(self):
        rows = self.shard.shape[0]
        distances = [-self.lead * k for k in range(5)] + [self.lead * k for k in range(1, 4)]
        places = [
            partial(lambda distance, index: ring_device_at(index, distance) * rows, distance)
            for distance in distances
        ]
        return self.ahead + self.behind[1:], places


class Scatter:
    def __init__(self, part, lead, first):
        self.part, self.lead = part, lead
        self.rows = part.shape[0] // 8
        self.left = {"a": 4, "b": 3}
        self.added = {"a": False, "b": False}
        self.held = dict(zip("ab", first))

    def signs(self):
        return {"a": self.lead, "b": -self.lead}

    def add(self, values):
        full = {"a": 4, "b": 3}
        adding = [k for k in values if 0 < self.left[k] < full[k] and not self.added[k]]
        if adding:
            signs = self.signs()
            sums = add_blocks(
                self.part,
                [values[k] for k in adding],
                [signs[k] * self.left[k] for k in adding],
            )
            values = {**values, **dict(zip(adding, sums))}
            for k in adding:
                self.added[k] = True
        return values

    def prepare(self, sides):
        values = self.add({k: self.held[k] for k in sides})
        return tuple(values[k] for k in sides)

    def start(self, sides):
        values = self.add({k: self.held[k] for k in sides if k in "ab"})
        signs = self.signs()
        for k in values:
            self.left[k] -= 1
            self.added[k] = False
        values = {k: hop(value, signs[k]) for k, value in values.items()}
        if "+" in sides:
            values = self.add(values)
        return tuple(values.values())

    def finish(self, sides, moved):
        self.held.update(zip(sides, moved))

    def total(self):
        at = ring_device_at(lax.axis_index("dp"), 0)
        block = lax.dynamic_slice_in_dim(self.part, at * self.rows, self.rows, 0)
        return self.held["a"].astype(f32) + self.held["b"].astype(f32) + block.astype(f32)


def gather_plain(shard):
    return lax.all_gather(shard, "dp", axis=0, tiled=True)


def scatter_plain(part):
    return lax.psum_scatter(part.astype(f32), "dp", scatter_dimension=0, tiled=True)


stage = lax.optimization_barrier


def run(kernel, name, outs, args, scratch=None):
    vmem = pl.BlockSpec(memory_space=pltpu.VMEM)
    anywhere = pl.BlockSpec(memory_space=pl.ANY)
    by_copy = scratch is not None
    return pl.pallas_call(
        kernel,
        out_shape=[jax.ShapeDtypeStruct(shape, dtype) for shape, dtype in outs],
        in_specs=[vmem if not by_copy or x.size < 40000 else anywhere for x in args],
        out_specs=[anywhere if by_copy else vmem] * len(outs),
        scratch_shapes=[pltpu.VMEM(shape, dtype) for shape, dtype in scratch]
        + [pltpu.SemaphoreType.DMA((48,))]
        if by_copy
        else [],
        cost_estimate=pl.CostEstimate(flops=0, bytes_accessed=1024, transcendentals=0),
        name=name,
    )(*args)


class Copies:
    def __init__(self, semaphores):
        self.semaphores = semaphores
        self.used = 0

    def start(self, source, target):
        copy = pltpu.make_async_copy(source, target, self.semaphores.at[self.used])
        self.used += 1
        copy.start()
        return copy

    def each(self, sources, targets, count, width):
        first = self.used
        self.used += count * len(sources)

        def copy(k, tile):
            at = pl.ds(pl.multiple_of(tile * width, width), width)
            number = first + k * count + tile
            return pltpu.make_async_copy(
                sources[k].at[:, at], targets[k].at[:, at], self.semaphores.at[number]
            )

        def start(tile):
            for k in range(len(sources)):
                copy(k, tile).start()

        def finish(tile, carry=0):
            for k in range(len(sources)):
                copy(k, tile).wait()
            return carry

        return start, finish

    def place(self, pieces, places, target):
        started = []
        for piece, place in zip(pieces, places):
            if place is None:
                started.append(self.start(piece, target))
            else:
                at = pl.multiple_of(place(lax.axis_index("dp")), 8)
                started.append(self.start(piece, target.at[pl.ds(at, piece.shape[0]), :]))
        return started


    def first_blocks(self, part, lead, outs):
        started = []
        for distance, out in zip((4 * lead, -3 * lead), outs):
            rows = out.shape[0]
            at = pl.multiple_of(ring_device_at(lax.axis_index("dp"), distance) * rows, 8)
            started.append(self.start(part.at[pl.ds(at, rows), :], out))
        return started


def wait(copies):
    for copy in copies:
        copy.wait()


def kernel_add(distances, part, *refs):
    count = len(distances)
    moved, outs, refs = refs[:count], refs[count : 2 * count], refs[2 * count :]
    copies = Copies(refs[-1])
    rows = outs[0].shape[0]
    arriving = []
    for k, distance in enumerate(distances):
        at = pl.multiple_of(ring_device_at(lax.axis_index("dp"), distance) * rows, 8)
        arriving.append(copies.start(moved[k], refs[2 * k]))
        arriving.append(copies.start(part.at[pl.ds(at, rows), :], refs[2 * k + 1]))
    leaving = []
    step = 48 if rows % 48 == 0 else rows
    for k in range(count):
        wait(arriving[2 * k : 2 * k + 2])
        total, block = refs[2 * k], refs[2 * k + 1]

        def add(i, carry):
            at = pl.ds(pl.multiple_of(i * step, step), step)
            total[at, :] = (total[at, :].astype(f32) + block[at, :].astype(f32)).astype(bf16)
            return carry

        lax.fori_loop(0, rows // step, add, 0)
        leaving.append(copies.start(total, outs[k]))
    wait(leaving)


def add_blocks(part, moved, distances):
    shape = moved[0].shape
    return run(
        partial(kernel_add, distances),
        "add_blocks",
        [(shape, bf16)] * len(moved),
        (part, *moved),
        [(shape, bf16)] * (2 * len(moved)),
    )


def dot(a, b):
    return jnp.dot(a, b, preferred_element_type=f32)


def dot_last(a, b):
    return lax.dot_general(a, b, (((1,), (1,)), ((), ())), preferred_element_type=f32)


def dot_first(a, b):
    return lax.dot_general(a, b, (((0,), (0,)), ((), ())), preferred_element_type=f32)


def core_here():
    return lax.axis_index("mp") & 1


def pair_rows(total, pair):
    half = total // 2
    return pl.ds(pl.multiple_of(pair * half, half), half)


def image_rows(rows, image):
    return pl.ds(pl.multiple_of(image * rows, rows), rows)


def tiles(total):
    return total // 384 if total % 384 == 0 else 1


def chosen(index, values):
    shape = (values.shape[0], index.shape[1])
    select = lax.broadcasted_iota(jnp.int32, shape, 0) == index
    return dot_first(select.astype(f32).astype(bf16), values)


def head_values(values, local, depth, head, t):
    return values[:, t * local + head * depth : t * local + (head + 1) * depth]


def stacked_probs(values, local, depth, heads):
    scores = jnp.concatenate(
        [
            dot_last(
                head_values(values, local, depth, head, 0),
                head_values(values, local, depth, head, 1),
            )
            for head in range(heads)
        ],
        0,
    )
    scores = scores * depth ** (-0.5)
    exp_scores = jnp.exp(scores - jnp.max(scores, axis=-1, keepdims=True))
    return exp_scores / jnp.sum(exp_scores, axis=-1, keepdims=True)


def lane_start(columns):
    return columns // 128 * 128


def kernel_mods(cond, weights, out):
    for k in range(out.shape[0]):
        out[k] = dot(cond[...], weights[k].astype(bf16))


def kernel_silu(grads, weights, out):
    total = dot_last(grads[0], weights[0].astype(bf16))
    for k in range(1, grads.shape[0]):
        total = total + dot_last(grads[k], weights[k].astype(bf16))
    out[...] = total


def kernel_norm(tokens, index, own, normed):
    images, rows = index.shape
    core = core_here()

    def norm(image, carry):
        at = image_rows(rows, image)
        values = chosen(index[pl.ds(image, 1), :], tokens[image])
        normed[at, :] = layer_norm(values)[0]

        @pl.when(image // (images // 2) == core)
        def _():
            place = image_rows(rows, image - core * (images // 2))
            own[place, :] = values.astype(bf16)

        return carry

    lax.fori_loop(0, images, norm, 0)


def kernel_project(places, *refs):
    count = len(places)
    pieces, (given, mods) = refs[:count], refs[count : count + 2]
    outs, refs = refs[count + 2 : count + 4], refs[count + 4 :]
    full, normed, hidden, projected, semaphores = refs
    copies = Copies(semaphores)
    images = mods.shape[1]
    total = normed.shape[0]
    rows = total // images
    arriving = [copies.start(given, normed)]
    columns = full.shape[1]
    placed = copies.place([piece.at[:, :columns] for piece in pieces], places, full)
    wait(arriving)

    def norm(image, carry):
        at = image_rows(rows, image)
        scale = mods[1, pl.ds(image, 1), :]
        values = normed[at, :] * (1.0 + scale) + mods[0, pl.ds(image, 1), :]
        hidden[at, :] = values.astype(bf16)
        return carry

    lax.fori_loop(0, images, norm, 0)
    leaving = [copies.start(hidden, outs[0])]
    wait(placed)
    weights = full[:, : projected.shape[1]]

    def project(pair, carry):
        at = pair_rows(total, pair)
        projected[at, :] = dot(hidden[at, :], weights).astype(bf16)
        return carry

    lax.fori_loop(0, 2, project, 0)
    leaving.append(copies.start(projected, outs[1]))
    wait(leaving)


def kernel_attend(places, heads, rows, *refs):
    count = len(places)
    pieces, (given,) = refs[:count], refs[count : count + 1]
    outs, refs = refs[count + 1 : count + 4], refs[count + 4 :]
    full, projected, attended, own, other, semaphores = refs
    copies = Copies(semaphores)
    total = projected.shape[0]
    local = attended.shape[1]
    depth = local // heads
    core = core_here()
    start = lane_start(3 * local)
    arriving = [copies.start(given, projected)]
    placed = copies.place([piece.at[:, start:] for piece in pieces], places, full)
    wait(arriving)

    def attend(image, carry):
        at = image_rows(rows, image)
        values = projected[at, :]
        probs = stacked_probs(values, local, depth, heads).astype(bf16)
        attended[at, :] = jnp.concatenate(
            [
                dot(
                    probs[head * rows : (head + 1) * rows],
                    head_values(values, local, depth, head, 2),
                ).astype(bf16)
                for head in range(heads)
            ],
            1,
        )
        return carry

    lax.fori_loop(0, total // rows, attend, 0)
    leaving = [copies.start(attended, outs[0])]
    wait(placed)
    weights = full[:, 3 * local - start :]
    other[...] = dot_last(attended[pair_rows(total, 1 - core), :], weights).astype(bf16)
    leaving.append(copies.start(other, outs[2]))
    own[...] = dot_last(attended[pair_rows(total, core), :], weights)
    leaving.append(copies.start(own, outs[1]))
    wait(leaving)


def kernel_kept_grad(grads, index, mods, own, mlp_grad):
    core = core_here()
    images, rows = index.shape
    half = images // 2
    for place in range(images):
        pair = core if place < half else 1 - core
        image = pair * half + place % half
        values = chosen(index[pl.ds(image, 1), :], grads[image])
        at = slice(place * rows, (place + 1) * rows)
        if place < half:
            own[at, :] = values.astype(bf16)
        mlp_grad[at, :] = (mods[5, pl.ds(image, 1), :] * values).astype(bf16)


def kernel_second_norm(kept, mods, own, moved, residual, hidden_two):
    core = core_here()
    half = mods.shape[1] // 2
    rows = residual.shape[0] // half
    for image in range(half):
        at = slice(image * rows, (image + 1) * rows)
        where = core * half + image
        gate, shift, scale = [mods[k, pl.ds(where, 1), :] for k in (2, 3, 4)]
        attn_out = own[at, :].astype(f32) + moved[at, :].astype(f32)
        values = kept[at, :].astype(f32) + gate * attn_out
        residual[at, :] = values
        normed, _ = layer_norm(values)
        hidden_two[at, :] = (normed * (1.0 + scale) + shift).astype(bf16)


gelu_rate = math.sqrt(2.0 / math.pi)


def gelu_parts(values):
    tanh = jnp.tanh(gelu_rate * (values + 0.044715 * (values * values * values)))
    return 0.5 * (1.0 + tanh), tanh


def kernel_feed_forward(places, lead, *refs):
    count = len(places)
    pieces, (here, there, mlp) = refs[:count], refs[count : count + 3]
    outs, refs = refs[count + 3 : -7], refs[-7:]
    full, hidden_two, mlp_grad, pre_act, activated, fc2_grad, semaphores = refs
    copies = Copies(semaphores)
    half = here.shape[0]
    arriving = [copies.start(here, hidden_two.at[:half, :])]
    arriving.append(copies.start(there, hidden_two.at[half:, :]))
    arriving += copies.place(pieces, places, full)
    arriving.append(copies.start(mlp, mlp_grad))
    columns = full.shape[1]
    count = tiles(columns)
    width = columns // count
    leave, leave_end = copies.each([pre_act, activated, fc2_grad], outs[:3], count, width)
    wait(arriving)

    def product(tile, carry):
        at = pl.ds(pl.multiple_of(tile * width, width), width)
        values = dot(hidden_two[...], full[:, at])
        pre_act[:, at] = values
        low = (values * gelu_parts(values)[0]).astype(bf16)
        activated[:, at] = low
        fc2_grad[:, at] = dot_first(mlp_grad[...], low).astype(bf16)
        leave(tile)
        return carry

    lax.fori_loop(0, count, product, 0)
    leaving = copies.first_blocks(fc2_grad, lead, outs[3:])
    lax.fori_loop(0, count, leave_end, 0)
    wait(leaving)


def kernel_fc1_grad(lead, here, there, pre, *refs):
    outs, (hidden_two, pre_grad, fc1_grad, semaphores) = refs[:-4], refs[-4:]
    copies = Copies(semaphores)
    half = here.shape[0]
    arriving = [copies.start(here, hidden_two.at[:half, :])]
    arriving.append(copies.start(there, hidden_two.at[half:, :]))
    arriving.append(copies.start(pre, pre_grad))
    wait(arriving)
    columns = fc1_grad.shape[1]
    count = tiles(columns)
    width = columns // count
    leave, leave_end = copies.each([fc1_grad], outs[:1], count, width)

    def product(tile, carry):
        at = pl.ds(pl.multiple_of(tile * width, width), width)
        fc1_grad[:, at] = dot_first(hidden_two[...], pre_grad[:, at]).astype(bf16)
        leave(tile)
        return carry

    lax.fori_loop(0, count, product, 0)
    leaving = copies.first_blocks(fc1_grad, lead, outs[1:])
    lax.fori_loop(0, count, leave_end, 0)
    wait(leaving)


def kernel_feed_back(one_places, two_places, *refs):
    count = len(one_places)
    ones, twos, refs = refs[:count], refs[count : 2 * count], refs[2 * count :]
    (mlp, pre), outs, refs = refs[:2], refs[2:5], refs[5:]
    fc1, fc2, mlp_grad, pre_act, pre_grad, own, other, semaphores = refs
    copies = Copies(semaphores)
    arriving = [copies.start(mlp, mlp_grad)] + copies.place(twos, two_places, fc2)
    columns = fc2.shape[1]
    count = tiles(columns)
    width = columns // count
    values_in = [copies.start(pre, pre_act)]
    later = copies.place(ones, one_places, fc1)
    leave, leave_end = copies.each([pre_grad], outs[:1], count, width)
    wait(arriving + values_in)

    def product(tile, carry):
        at = pl.ds(pl.multiple_of(tile * width, width), width)
        gradient = dot(mlp_grad[...], fc2[:, at])
        values = pre_act[:, at]
        share, tanh = gelu_parts(values)
        slope = share + 0.5 * values * (1.0 - tanh * tanh) * gelu_rate * (
            1.0 + 3.0 * 0.044715 * (values * values)
        )
        pre_grad[:, at] = (gradient * slope).astype(bf16)
        leave(tile)
        return carry

    lax.fori_loop(0, count, product, 0)
    wait(later)
    back_product(copies, pre_grad, fc1, own, other, outs[1:])
    lax.fori_loop(0, count, leave_end, 0)


def back_product(copies, rows, weights, own, other, outs):
    half = own.shape[0]
    depth = weights.shape[0]
    count = tiles(depth)
    width = depth // count
    leave, leave_end = copies.each([own, other], outs, count, width)

    def product(tile, carry):
        at = pl.ds(pl.multiple_of(tile * width, width), width)
        values = dot_last(rows[...], weights[at, :])
        other[:, at] = values[half:].astype(bf16)
        own[:, at] = values[:half]
        leave(tile)
        return carry

    lax.fori_loop(0, count, product, 0)
    lax.fori_loop(0, count, leave_end, 0)


def kernel_feed_out(places, *refs):
    count = len(places)
    pieces, (low,) = refs[:count], refs[count : count + 1]
    outs, (full, activated, own, other, semaphores) = refs[count + 1 : count + 3], refs[count + 3 :]
    copies = Copies(semaphores)
    arriving = [copies.start(low, activated)] + copies.place(pieces, places, full)
    wait(arriving)
    back_product(copies, activated, full, own, other, outs)


def kernel_second_back(
    own, moved, residual, attn_own, attn_moved, grad, mods, residual_grad, attn_grad, sums
):
    core = core_here()
    half = mods.shape[1] // 2
    rows = residual.shape[0] // half
    for image in range(half):
        at = slice(image * rows, (image + 1) * rows)
        where = core * half + image
        gate, scale = [mods[k, pl.ds(where, 1), :] for k in (2, 4)]
        normed, inverse = layer_norm(residual[at, :])
        gradient = own[at, :].astype(f32) + moved[at, :].astype(f32)
        sums[1, pl.ds(image, 1), :] = jnp.sum(gradient, axis=0, keepdims=True)
        sums[2, pl.ds(image, 1), :] = jnp.sum(gradient * normed, axis=0, keepdims=True)
        values = grad[at, :].astype(f32) + norm_back(normed, inverse, gradient * (1.0 + scale))
        residual_grad[at, :] = values
        attn_out = attn_own[at, :].astype(f32) + attn_moved[at, :].astype(f32)
        sums[0, pl.ds(image, 1), :] = jnp.sum(values * attn_out, axis=0, keepdims=True)
        attn_grad[at, :] = (gate * values).astype(bf16)


def kernel_attention_back(places, heads, rows, lead, *refs):
    count = len(places)
    pieces, inputs = refs[:count], refs[count : count + 5]
    outs, refs = refs[count + 5 : -11], refs[-11:]
    here, there, projected_in, attended_in, hidden_in = inputs
    full, out_grad, projected, attended, hidden, back, grads, attn_grad, own, other = refs[:-1]
    copies = Copies(refs[-1])
    core = core_here()
    total = out_grad.shape[0]
    local = attended.shape[1]
    depth = local // heads
    arriving = [
        copies.start(here, out_grad.at[pair_rows(total, core), :]),
        copies.start(there, out_grad.at[pair_rows(total, 1 - core), :]),
    ] + copies.place(pieces, places, full)
    later = [copies.start(projected_in, projected), copies.start(attended_in, attended)]
    last = [copies.start(hidden_in, hidden)]
    wait(arriving)
    back[...] = dot(out_grad[...], full[:, 3 * local :]).astype(bf16)
    wait(later)

    def image_back(image, carry):
        at = image_rows(rows, image)
        values = projected[at, :]
        gradient = back[at, :]
        probs = stacked_probs(values, local, depth, heads)
        prob_grad = jnp.concatenate(
            [
                dot_last(
                    head_values(gradient, local, depth, head, 0),
                    head_values(values, local, depth, head, 2),
                )
                for head in range(heads)
            ],
            0,
        )
        score_grad = probs * (prob_grad - jnp.sum(prob_grad * probs, axis=-1, keepdims=True))
        score_grad = score_grad.astype(bf16)
        probs = probs.astype(bf16)
        parts = []
        for t in range(3):
            for head in range(heads):
                own_rows = slice(head * rows, (head + 1) * rows)
                if t == 0:
                    key = head_values(values, local, depth, head, 1)
                    part = dot(score_grad[own_rows], key) * depth ** (-0.5)
                elif t == 1:
                    query = head_values(values, local, depth, head, 0)
                    part = dot_first(score_grad[own_rows], query) * depth ** (-0.5)
                else:
                    part = dot_first(
                        probs[own_rows], head_values(gradient, local, depth, head, 0)
                    )
                parts.append(part.astype(bf16))
        grads[at, :] = jnp.concatenate(parts, 1)
        return carry

    lax.fori_loop(0, total // rows, image_back, 0)
    weights = full[:, : 3 * local]
    other[...] = dot_last(grads[pair_rows(total, 1 - core), :], weights).astype(bf16)
    leaving = [copies.start(other, outs[2])]
    own[...] = dot_last(grads[pair_rows(total, core), :], weights)
    leaving.append(copies.start(own, outs[1]))
    wait(last)
    attn_grad[:, 3 * local :] = dot_first(out_grad[...], attended[...]).astype(bf16)
    attn_grad[:, : 3 * local] = dot_first(hidden[...], grads[...]).astype(bf16)
    leaving.append(copies.start(attn_grad, outs[0]))
    leaving += copies.first_blocks(attn_grad, lead, outs[3:])
    wait(leaving)


def kernel_output(own, moved, residual, grad, mods, kept_out, sums):
    core = core_here()
    half = mods.shape[1] // 2
    rows = residual.shape[0] // half
    for image in range(half):
        at = slice(image * rows, (image + 1) * rows)
        mlp_out = own[at, :].astype(f32) + moved[at, :].astype(f32)
        gate = mods[5, pl.ds(core * half + image, 1), :]
        kept_out[at, :] = (residual[at, :] + gate * mlp_out).astype(bf16)
        sums[pl.ds(image, 1), :] = jnp.sum(
            grad[at, :].astype(f32) * mlp_out, axis=0, keepdims=True
        )


def kernel_first_back(
    own, moved, residual_grad, kept, mods, late, last, kept_grad, mine, partner
):
    me = lax.axis_index("mp")
    core = me & 1
    half = mods.shape[1] // 2
    rows = residual_grad.shape[0] // half
    local = mine.shape[2]
    lines = [[], []]
    for image in range(half):
        at = slice(image * rows, (image + 1) * rows)
        normed, inverse = layer_norm(kept[at, :].astype(f32))
        gradient = own[at, :].astype(f32) + moved[at, :].astype(f32)
        lines[0].append(jnp.sum(gradient, axis=0, keepdims=True))
        lines[1].append(jnp.sum(gradient * normed, axis=0, keepdims=True))
        scale = mods[1, pl.ds(core * half + image, 1), :]
        values = residual_grad[at, :] + norm_back(normed, inverse, gradient * (1.0 + scale))
        kept_grad[at, :] = values.astype(bf16)
    planes = [jnp.concatenate(line, 0) for line in lines]
    planes += [late[0], late[1], late[2], last[...]]
    for k, plane in enumerate(planes):
        blocks = [plane[:, j * local : (j + 1) * local] for j in range(4)]
        for out, device in ((mine, me), (partner, me ^ 1)):
            picked = blocks[0]
            for j in range(1, 4):
                picked = jnp.where(device == j, blocks[j], picked)
            out[k] = picked.astype(bf16)


def new_state(weight, moment, average, gradient, rate, steps):
    decay = (1.0 + steps) / (10.0 + steps)
    new_moment = momentum_rate * moment + gradient
    master = weight - rate * (gradient + momentum_rate * new_moment)
    return master, new_moment, decay * average + (1.0 - decay) * master


def attention_step(rate, steps, gradient, *refs):
    counts = steps[0].astype(f32)
    qkv, proj, qkv_out, proj_out = refs[:3], refs[3:6], refs[6:9], refs[9:]
    local = proj[0].shape[1]
    for t in range(3):
        values = new_state(
            *[ref[t] for ref in qkv], gradient[:, t * local : (t + 1) * local], rate, counts
        )
        for ref, value in zip(qkv_out, values):
            ref[t] = value
    values = new_state(*[ref[...] for ref in proj], gradient[:, 3 * local :], rate, counts)
    for ref, value in zip(proj_out, values):
        ref[...] = value


def step_attention(qkv, proj, gradient, rate, steps):
    whole = pl.BlockSpec(memory_space=pltpu.VMEM)
    size = qkv[0].size + proj[0].size
    return pl.pallas_call(
        partial(attention_step, rate),
        out_shape=[jax.ShapeDtypeStruct(x.shape, f32) for x in qkv + proj],
        in_specs=[pl.BlockSpec(memory_space=pltpu.SMEM)] + [whole] * 7,
        out_specs=[whole] * 6,
        cost_estimate=pl.CostEstimate(flops=0, bytes_accessed=1024, transcendentals=0),
        name="step_attention",
    )(steps, gradient, *qkv, *proj)


def ada_step(rate, steps, cond, mods, weight, moment, average, master, new_moment, ema):
    counts = steps[0].astype(f32)
    gradient = lax.dot_general(
        cond[...], mods[0], (((0,), (0,)), ((), ())), preferred_element_type=f32
    )
    values = new_state(weight[0], moment[0], average[0], gradient, rate, counts)
    master[0], new_moment[0], ema[0] = values


def step_ada(weight, moment, average, cond, mods, rate, steps):
    count, rows, columns = weight.shape
    spec = pl.BlockSpec((1, rows, columns), lambda k: (k, 0, 0))
    return pl.pallas_call(
        partial(ada_step, rate),
        grid=(count,),
        out_shape=[jax.ShapeDtypeStruct(weight.shape, f32)] * 3,
        in_specs=[
            pl.BlockSpec(memory_space=pltpu.SMEM),
            pl.BlockSpec(cond.shape, lambda k: (0, 0)),
            pl.BlockSpec((1,) + mods.shape[1:], lambda k: (k, 0, 0)),
        ]
        + [spec] * 3,
        out_specs=[spec] * 3,
        cost_estimate=pl.CostEstimate(flops=0, bytes_accessed=1024, transcendentals=0),
        name="step_ada",
    )(steps, cond, mods, weight, moment, average)


def per_device(
    tokens,
    condition,
    cotangent,
    kept_index,
    skip_index,
    step_count,
    ada_weight,
    qkv_weight,
    proj_weight,
    fc1_weight,
    fc2_weight,
    ada_moment,
    qkv_moment,
    proj_moment,
    fc1_moment,
    fc2_moment,
    ada_average,
    qkv_average,
    proj_average,
    fc1_average,
    fc2_average,
):
    images, seq, width = tokens.shape
    kept_count = kept_index.shape[1]
    own_d = ada_weight.shape[0]
    mods = ada_weight.shape[1]
    local = ada_weight.shape[2]
    units = fc1_weight.shape[1]
    local_heads = local // HEAD_DIM
    total = images * kept_count
    half = total // 2
    core = lax.axis_index("mp") % 2
    chip = lax.axis_index("mp") // 2
    dp_size = lax.axis_size("dp")
    index = lax.axis_index("dp")
    ring = dp_size == 8

    def tick(extras, *hops):
        hops = [(one, sides) for one, sides in hops if one is not None]
        moving = tuple(one.start(sides) for one, sides in hops)
        held, moved = stage((tuple(extras()), moving))
        for (one, sides), values in zip(hops, moved):
            one.finish(sides, values)
        return held

    attn_low = jnp.concatenate(
        [qkv_weight[0], qkv_weight[1], qkv_weight[2], proj_weight.T], 1
    ).astype(bf16)
    fc1_low = fc1_weight.astype(bf16)
    fc2_low = fc2_weight.T.astype(bf16)
    if ring:
        attn_ring, fc1_ring, fc2_ring = Gather(attn_low, 1), Gather(fc1_low, 1), Gather(fc2_low, -1)
    else:
        attn_ring = fc1_ring = fc2_ring = None
        attn_pieces, attn_places = [gather_plain(attn_low)], [None]
        fc1_pieces, fc1_places = [gather_plain(fc1_low)], [None]
        fc2_pieces, fc2_places = [gather_plain(fc2_low)], [None]
    block = [((width // 8, units), bf16)] * 2 if ring else []
    attn_block = [((width // 8, 4 * local), bf16)] * 2 if ring else []

    cond_float = condition.astype(f32)
    silu_cond = jax.nn.silu(cond_float).astype(bf16)
    small = silu_cond.reshape(images, dp_size, own_d)
    levels = len(dp_groups())
    def first_norm():
        return spread_round(small, 0, 0), *run(
            kernel_norm,
            "first_norm",
            [((half, width), bf16), ((total, width), f32)],
            (tokens, kept_index),
        )

    small, kept_own, normed = tick(first_norm, (attn_ring, "ab"))
    ada_state = [jnp.moveaxis(x, 1, 0) for x in (ada_weight, ada_moment, ada_average)]

    def rest_of_cond():
        values = small
        for level in range(1, levels):
            values = spread_round(values, 0, level)
        return (values,)

    (small,) = tick(rest_of_cond, (attn_ring, "ab"))

    def sum_of_mods():
        own = lax.dynamic_index_in_dim(small, index, 1, keepdims=False)
        (values,) = run(
            kernel_mods, "mods", [((mods, dp_size * images, local), f32)], (own, ada_state[0])
        )
        for level in reversed(range(1, levels)):
            values = sum_round(values, 1, level)
        return own, values

    cond_own, small = tick(sum_of_mods, (attn_ring, "ab"))
    (mod_local,) = tick(lambda: (sum_round(small, 1, 0),), (attn_ring, "a"))
    if ring:
        attn_pieces, attn_places = attn_ring.pieces()

    def all_mods():
        at_core = swap_core(mod_local)
        at_x = swap_x(mod_local)
        at_both = lax.ppermute(mod_local, "mp", [(j, j ^ 3) for j in range(4)])
        pairs = [join_pair(mod_local, at_core, core, 2), join_pair(at_x, at_both, core, 2)]
        return (
            jnp.where(chip == 0, jnp.concatenate(pairs, 2), jnp.concatenate(pairs[::-1], 2)),
        )

    (modulation,) = tick(all_mods, (fc1_ring, "ab"))


    def project():
        outs = [((total, width), bf16), ((total, 3 * local), bf16)]
        lanes = -(-3 * local // 128) * 128
        return run(
            partial(kernel_project, attn_places),
            "project",
            outs,
            (*attn_pieces, normed, modulation),
            [((width, lanes), bf16), ((total, width), f32)] + outs,
        )

    hidden, projected = tick(project, (fc2_ring, "ab"))

    def add_low(own, other):
        return (own + other.astype(f32)).astype(bf16)

    def attend():
        outs = [((total, local), bf16), ((half, width), f32), ((half, width), bf16)]
        lanes = 4 * local - lane_start(3 * local)
        return run(
            partial(kernel_attend, attn_places, local_heads, kept_count),
            "attend",
            outs,
            (*attn_pieces, projected),
            [((width, lanes), bf16), ((total, 3 * local), bf16)] + outs,
        )

    attended, own_part, other_part = tick(attend, (fc1_ring, "ab"))

    def attention_sums():
        own = add_low(own_part, swap_core(other_part))
        return own, swap_x(own), *kept_grads()


    def kept_grads():
        return run(
            kernel_kept_grad,
            "kept_grad",
            [((half, width), bf16), ((total, width), bf16)],
            (cotangent, kept_index, modulation),
        )

    attn_own, attn_moved, grad_own, mlp_grad = tick(
        attention_sums, (fc1_ring, "ab"), (fc2_ring, "ab")
    )

    def second_norm():
        values, low = run(
            kernel_second_norm,
            "second_norm",
            [((half, width), f32), ((half, width), bf16)],
            (kept_own, modulation, attn_own, attn_moved),
        )
        return values, low, swap_core(low)

    residual, hidden_here, hidden_there = tick(second_norm, (fc1_ring, "a"), (fc2_ring, "a"))
    if ring:
        fc1_pieces, fc1_places = fc1_ring.pieces()

    def feed_forward():
        outs = [((total, units), f32), ((total, units), bf16), ((width, units), bf16)]
        return run(
            partial(kernel_feed_forward, fc1_places, -1),
            "feed_forward",
            outs + block,
            (*fc1_pieces, hidden_here, hidden_there, mlp_grad),
            [((width, units), bf16), ((total, width), bf16), ((total, width), bf16)] + outs,
        )

    pre_act, activated, fc2_grad, *first = tick(feed_forward, (fc2_ring, "ba"))
    if ring:
        fc2_pieces, fc2_places = fc2_ring.pieces()
        fc2_sums = Scatter(fc2_grad, -1, first)
    else:
        fc2_sums = fc1_sums = attn_sums = None

    def feed_back():
        outs = [((total, units), bf16), ((half, width), f32), ((half, width), bf16)]
        return run(
            partial(kernel_feed_back, fc1_places, fc2_places),
            "feed_back",
            outs,
            (*fc1_pieces, *fc2_pieces, mlp_grad, pre_act),
            [
                ((width, units), bf16),
                ((width, units), bf16),
                ((total, width), bf16),
                ((total, units), f32),
            ]
            + outs,
        )

    pre_grad, own_part, other_part = tick(feed_back, (fc2_sums, "ab"))
    moving = []

    def products():
        own_low = add_low(own_part, swap_core(other_part))
        outs = [((width, units), bf16)]
        grad, *first = run(
            partial(kernel_fc1_grad, -1),
            "fc1_grad",
            outs + block,
            (hidden_here, hidden_there, pre_grad),
            [((total, width), bf16), ((total, units), bf16)] + outs,
        )
        if ring:
            moving.append(Scatter(grad, -1, first))
            first = moving[0].start("ab")
        outs = [((half, width), f32), ((half, width), bf16)]
        sums = run(
            partial(kernel_feed_out, fc2_places),
            "feed_out",
            outs,
            (*fc2_pieces, activated),
            [((width, units), bf16), ((total, units), bf16)] + outs,
        )
        return own_low, swap_x(own_low), grad, *sums, *first

    hidden_own, hidden_moved, fc1_grad, own_mlp, other_mlp, *first = tick(
        products, (fc2_sums, "ab+")
    )
    if ring:
        (fc1_sums,) = moving
        fc1_sums.part = fc1_grad
        fc1_sums.finish("ab", first)

    def second_back():
        sums = run(
            kernel_second_back,
            "second_back",
            [((half, width), f32), ((half, width), bf16), ((3, images // 2, width), f32)],
            (
                hidden_own,
                hidden_moved,
                residual,
                attn_own,
                attn_moved,
                grad_own,
                modulation,
            ),
        )
        return *sums, *(fc1_sums.prepare("ab") if ring else ())

    residual_grad, out_here, late_mods, *sums = tick(second_back, (fc2_sums, "ab"))
    if ring:
        fc1_sums.finish("ab", sums)
    out_here, out_there, mlp_own = tick(
        lambda: (out_here, swap_core(out_here), add_low(own_mlp, swap_core(other_mlp)))
    )

    def attention_back():
        outs = [((width, 4 * local), bf16), ((half, width), f32), ((half, width), bf16)]
        back = run(
            partial(kernel_attention_back, attn_places, local_heads, kept_count, 1),
            "attention_back",
            outs + attn_block,
            (*attn_pieces, out_here, out_there, projected, attended, hidden),
            [
                ((width, 4 * local), bf16),
                ((total, width), bf16),
                ((total, 3 * local), bf16),
                ((total, local), bf16),
                ((total, width), bf16),
                ((total, local), bf16),
                ((total, 3 * local), bf16),
            ]
            + outs,
        )
        return swap_x(mlp_own), *back

    mlp_moved, attn_grad, own_part, other_part, *first = tick(attention_back, (fc1_sums, "ab"))
    if ring:
        attn_sums = Scatter(attn_grad, 1, first)

    def output():
        return run(
            kernel_output,
            "output",
            [((half, width), bf16), ((images // 2, width), f32)],
            (mlp_own, mlp_moved, residual, grad_own, modulation),
        )

    def attention_back_sums():
        own = add_low(own_part, swap_core(other_part))
        return own, swap_x(own), *output()

    back_own, back_moved, kept_out, last_mods = tick(
        attention_back_sums, (attn_sums, "ab+"), (fc1_sums, "ab")
    )

    def first_back():
        kept, mine, partner = run(
            kernel_first_back,
            "first_back",
            [
                ((half, width), bf16),
                ((mods, images // 2, local), bf16),
                ((mods, images // 2, local), bf16),
            ],
            (
                back_own,
                back_moved,
                residual_grad,
                kept_own,
                modulation,
                late_mods,
                last_mods,
            ),
        )
        return kept, join_pair(mine, swap_core(partner), core, 1)

    kept_grad, small = tick(first_back, (attn_sums, "ab"))

    def spreads():
        values = spread_round(small, 1, 0)
        return values, spread_pair(kept_grad, core), spread_pair(kept_out, core)

    small, kept_grad, kept_out = tick(spreads, (attn_sums, "ab"))
    kept_grad, kept_out = [x.reshape(images, kept_count, width) for x in (kept_grad, kept_out)]

    rate = 0.02 / math.sqrt(images * dp_size * kept_count)
    steps = step_count[0].astype(f32)
    positions = lax.broadcasted_iota(jnp.int32, (images, seq, kept_count), 1)
    select = (kept_index[:, None, :] == positions).astype(bf16)
    is_kept = jnp.any(kept_index[:, None, :] == positions, axis=2)[:, :, None]

    def outputs():
        values = small
        for level in range(1, levels):
            values = spread_round(values, 1, level)
        placed = jnp.einsum("bsi,bid->bsd", select, kept_grad, preferred_element_type=f32)
        grads = jnp.where(is_kept, placed, cotangent.astype(f32))
        placed = jnp.einsum("bsi,bid->bsd", select, kept_out, preferred_element_type=f32)
        out = jnp.where(is_kept, placed.astype(bf16), tokens)
        last = (fc2_sums.held["a"], fc2_sums.held["b"]) if ring else ()
        return values, grads, out, *last

    mod_grad_all, tokens_grad, block_out, *last = tick(
        outputs, (attn_sums, "a"), (fc1_sums, "a")
    )
    if ring:
        fc2_sums.finish("ab", last)
    (silu_part,) = run(
        kernel_silu, "silu", [((dp_size * images, own_d), f32)], (mod_grad_all, ada_state[0])
    )
    silu_part = silu_part + swap_core(silu_part)
    silu_part = silu_part + swap_x(silu_part)
    ada_new = step_ada(*ada_state, cond_own, mod_grad_all, rate, step_count)
    ada_master, ada_momentum, ada_ema = [jnp.moveaxis(x, 0, 1) for x in ada_new]
    attn_shard = attn_sums.total() if ring else scatter_plain(attn_grad)
    fc1_shard = fc1_sums.total() if ring else scatter_plain(fc1_grad)
    if ring:
        fc2_sums.finish("a", fc2_sums.start("a"))
        fc2_shard = fc2_sums.total()
    else:
        fc2_shard = scatter_plain(fc2_grad)
    fc2_master, fc2_momentum, fc2_ema = new_state(
        fc2_weight.T, fc2_moment.T, fc2_average.T, fc2_shard, rate, steps
    )
    silu_blocks = silu_part.reshape(dp_size, images, own_d)
    attn_new = step_attention(
        (qkv_weight, qkv_moment, qkv_average),
        (proj_weight.T, proj_moment.T, proj_average.T),
        attn_shard,
        rate,
        step_count,
    )
    for level in reversed(range(levels)):
        silu_blocks = turn_round(silu_blocks, level)
    silu_blocks = in_order(silu_blocks)
    qkv_master, qkv_momentum, qkv_ema, proj_master, proj_momentum, proj_ema = attn_new
    fc1_master, fc1_momentum, fc1_ema = new_state(
        fc1_weight, fc1_moment, fc1_average, fc1_shard, rate, steps
    )
    silu_grad = jnp.moveaxis(silu_blocks, 0, 1).reshape(images, width)
    silu_value, silu_pull = jax.vjp(jax.nn.silu, cond_float)
    condition_grad = silu_pull(silu_grad)[0]
    return (
        block_out,
        tokens_grad,
        condition_grad,
        ada_master,
        qkv_master,
        proj_master.T,
        fc1_master,
        fc2_master.T,
        ada_momentum,
        qkv_momentum,
        proj_momentum.T,
        fc1_momentum,
        fc2_momentum.T,
        ada_ema,
        qkv_ema,
        proj_ema.T,
        fc1_ema,
        fc2_ema.T,
    )


def solution(mesh):
    weights = (
        P("dp", None, "mp"),
        P(None, "dp", "mp"),
        P("mp", "dp"),
        P("dp", "mp"),
        P("mp", "dp"),
    )
    rows = P("dp", None, None)
    pairs = P("dp", None)
    return jax.shard_map(
        per_device,
        mesh=mesh,
        in_specs=(rows, pairs, rows, pairs, pairs, P()) + weights * 3,
        out_specs=(rows, rows, pairs) + weights * 3,
        check_vma=False,
    )
```

profile of v0, /device:TPU:0, one launch (start us, length us, event | category | flops | bytes accessed | tf_op | source)
XLA Modules:
  0.0 303.4 jit_solution(16396978884174173537)
XLA Ops:
  2.2 3.1 %collective-permute-start.3 = (bf16[144,1152]{1,0:T(8,128)(2,1)S(1)}, bf16[144,1152]{1,0:T(8,128)(2,1)S(1)}, u32[]{:S(2)}, u32[]{:S(2)}) collective-permute-start(bf16[144,1152]{1,0:T(8,128)(2,1)S(1)} %concatenate.53.refs_0_), channel_id=1, source_target_pairs={{0,8},{8,16},{16,24},{24,28},{28,20},{20,12},{12,4},{4,0},{1,9},{9... | collective-permute-start | bytes 995336 | tf_op jit(solution)/shard_map/ppermute | solution.py:118
  9.0 5.3 %first_norm.1 = (bf16[256,1152]{1,0:T(8,128)(2,1)}, f32[512,1152]{1,0:T(8,128)}) custom-call(bf16[4,256,1152]{2,1,0:T(8,128)(2,1)} %tokens.1, s32[4,128]{1,0:T(4,128)} %index.3), custom_call_target="tpu_custom_call" | custom-call | bytes 1024 | tf_op jit(solution)/shard_map/first_norm/pallas_call | solution.py:222
  17.2 2.6 collective-permute-start.5
  19.8 8.7 %collective-permute-done.5 = bf16[16,8,144]{2,0,1:T(8,128)(2,1)S(1)} collective-permute-done((bf16[16,8,144]{2,0,1:T(8,128)(2,1)S(1)}, bf16[16,8,144]{2,0,1:T(8,128)(2,1)S(1)}, u32[]{:S(2)}, u32[]{:S(2)}) %collective-permute-start.5) | collective-permute-done | bytes 36896 | tf_op jit(solution)/shard_map/ppermute | solution.py:56
  34.8 7.1 %collective-permute-done.8 = f32[6,16,288]{2,1,0:T(8,128)S(1)} collective-permute-done((f32[6,16,288]{2,1,0:T(8,128)S(1)}, f32[6,16,288]{2,1,0:T(8,128)S(1)}, u32[]{:S(2)}, u32[]{:S(2)}) %collective-permute-start.8) | collective-permute-done | bytes 110624 | tf_op jit(solution)/shard_map/ppermute | solution.py:56
  42.9 3.5 %collective-permute-start.14 = (bf16[144,1152]{1,0:T(8,128)(2,1)S(1)}, bf16[144,1152]{1,0:T(8,128)(2,1)S(1)}, u32[]{:S(2)}, u32[]{:S(2)}) collective-permute-start(bf16[144,1152]{1,0:T(8,128)(2,1)S(1)} %collective-permute-done.9.refs_3_), channel_id=1, source_target_pairs={{0,8},{8,16},{16,24},{24,28},{28,20},{20,12},{12,4},{4,0},{1,9},{9... | collective-permute-start | bytes 995336 | tf_op jit(solution)/shard_map/ppermute | solution.py:118
  47.0 2.9 collective-permute-start.13
  66.0 6.1 %project.1 = (bf16[512,1152]{1,0:T(8,128)(2,1)}, bf16[512,864]{1,0:T(8,128)(2,1)}) custom-call(bf16[144,1152]{1,0:T(8,128)(2,1)} %copy-done.3, bf16[144,1152]{1,0:T(8,128)(2,1)} %copy-done.7, bf16[144,1152]{1,0:T(8,128)(2,1)} %copy-done.9, bf16[144,1152]{1,0:T(8,128)(2,1)} %copy-done.12, bf16[144,1152]{1,0:T(8,128)(2,1)} %copy-done.13, ...), custom_call_target="tpu_custom_call" | custom-call | bytes 1024 | tf_op jit(solution)/shard_map/project/pallas_call | solution.py:222
  72.4 7.2 %attend.1 = (bf16[512,288]{1,0:T(8,128)(2,1)}, f32[256,1152]{1,0:T(8,128)}, bf16[256,1152]{1,0:T(8,128)(2,1)}) custom-call(bf16[144,1152]{1,0:T(8,128)(2,1)} %copy-done.3, bf16[144,1152]{1,0:T(8,128)(2,1)} %copy-done.7, bf16[144,1152]{1,0:T(8,128)(2,1)} %copy-done.9, bf16[144,1152]{1,0:T(8,128)(2,1)} %copy-done.12, bf16[144,1152]{1,0:T(8,128)(2,1)} %copy-done.13, ...), custom_call_target="tpu_custom_call" | custom-call | bytes 1024 | tf_op jit(solution)/shard_map/attend/pallas_call | solution.py:222
  89.4 3.3 %kept_grad.1 = (bf16[256,1152]{1,0:T(8,128)(2,1)}, bf16[512,1152]{1,0:T(8,128)(2,1)}) custom-call(bf16[4,256,1152]{2,1,0:T(8,128)(2,1)} %grads.1, s32[4,128]{1,0:T(4,128)} %index.3, f32[6,4,1152]{2,1,0:T(4,128)} %maximum_select_fusion.2.refs_9_.mods), custom_call_target="tpu_custom_call" | custom-call | bytes 1024 | tf_op jit(solution)/shard_map/kept_grad/pallas_call | solution.py:222
  92.7 3.4 %collective-permute-done.28.refs_10_.refs_2_ = bf16[144,1152]{1,0:T(8,128)(2,1)} collective-permute-done((bf16[144,1152]{1,0:T(8,128)(2,1)S(1)}, bf16[144,1152]{1,0:T(8,128)(2,1)}, u32[]{:S(2)}, u32[]{:S(2)}) %collective-permute-start.28) | collective-permute-done | bytes 331808 | tf_op jit(solution)/shard_map/ppermute | solution.py:118
  98.1 5.6 %collective-permute-done.26.refs_3_ = bf16[144,1152]{1,0:T(8,128)(2,1)S(1)} collective-permute-done((bf16[144,1152]{1,0:T(8,128)(2,1)S(1)}, bf16[144,1152]{1,0:T(8,128)(2,1)S(1)}, u32[]{:S(2)}, u32[]{:S(2)}) %collective-permute-start.26) | collective-permute-done | bytes 331808 | tf_op jit(solution)/shard_map/ppermute | solution.py:118
  104.5 3.0 second_norm.1
  109.8 8.3 %collective-permute-done.31.refs_4_ = bf16[144,1152]{1,0:T(8,128)(2,1)S(1)} collective-permute-done((bf16[144,1152]{1,0:T(8,128)(2,1)S(1)}, bf16[144,1152]{1,0:T(8,128)(2,1)S(1)}, u32[]{:S(2)}, u32[]{:S(2)}) %collective-permute-start.31) | collective-permute-done | bytes 331808 | tf_op jit(solution)/shard_map/ppermute | solution.py:118
  119.7 8.8 %feed_forward.1 = (f32[512,1152]{1,0:T(8,128)}, bf16[512,1152]{1,0:T(8,128)(2,1)}, bf16[1152,1152]{1,0:T(8,128)(2,1)}, bf16[144,1152]{1,0:T(8,128)(2,1)}, bf16[144,1152]{1,0:T(8,128)(2,1)}) custom-call(bf16[144,1152]{1,0:T(8,128)(2,1)} %copy-done.5, bf16[144,1152]{1,0:T(8,128)(2,1)} %copy-done.23, bf16[144,1152]{1,0:T(8,128)(2,1)} %copy-done.25, ...), custom_call_target="tpu_custom_call" | custom-call | bytes 1024 | tf_op jit(solution)/shard_map/feed_forward/pallas_call | solution.py:222
  130.7 9.8 %feed_back.1 = (bf16[512,1152]{1,0:T(8,128)(2,1)}, f32[256,1152]{1,0:T(8,128)}, bf16[256,1152]{1,0:T(8,128)(2,1)}) custom-call(bf16[144,1152]{1,0:T(8,128)(2,1)} %copy-done.5, bf16[144,1152]{1,0:T(8,128)(2,1)} %copy-done.23, bf16[144,1152]{1,0:T(8,128)(2,1)} %copy-done.25, bf16[144,1152]{1,0:T(8,128)(2,1)} %copy-done.27, bf16[144,1152]{1,0:T(8,128)(2,1)} %copy-done.29, ...), custom_call_target="tpu_custom_call" | custom-call | bytes 1024 | tf_op jit(solution)/shard_map/feed_back/pallas_call | solution.py:222
  144.7 2.5 add_blocks.9
  149.3 5.6 %fc1_grad.1 = (bf16[1152,1152]{1,0:T(8,128)(2,1)}, bf16[144,1152]{1,0:T(8,128)(2,1)}, bf16[144,1152]{1,0:T(8,128)(2,1)}) custom-call(bf16[256,1152]{1,0:T(8,128)(2,1)} %get-tuple-element.219.refs_8_.here, bf16[256,1152]{1,0:T(8,128)(2,1)} %copy-done.19, bf16[512,1152]{1,0:T(8,128)(2,1)} %get-tuple-element.238.pre), custom_call_target="tpu_custom_call" | custom-call | bytes 1024 | tf_op jit(solution)/shard_map/fc1_grad/pallas_call | solution.py:222
  157.0 5.7 %feed_out.1 = (f32[256,1152]{1,0:T(8,128)}, bf16[256,1152]{1,0:T(8,128)(2,1)}) custom-call(bf16[144,1152]{1,0:T(8,128)(2,1)} %copy-done.6, bf16[144,1152]{1,0:T(8,128)(2,1)} %copy-done.30, bf16[144,1152]{1,0:T(8,128)(2,1)} %collective-permute-done.28.refs_10_.refs_2_, bf16[144,1152]{1,0:T(8,128)(2,1)} %copy-done.33, bf16[144,1152]{1,0:T(8,128)(2,1)} %copy-done.35, ...), custom_call_target="tpu_custom_call" | custom-call | bytes 1024 | tf_op jit(solution)/shard_map/feed_out/pallas_call | solution.py:222
  172.0 4.7 %second_back.1 = (f32[256,1152]{1,0:T(8,128)}, bf16[256,1152]{1,0:T(8,128)(2,1)}, f32[3,2,1152]{2,1,0:T(2,128)}) custom-call(bf16[256,1152]{1,0:T(8,128)(2,1)} %copy-done.20, bf16[256,1152]{1,0:T(8,128)(2,1)} %copy-done.42, f32[256,1152]{1,0:T(8,128)} %get-tuple-element.254.residual, bf16[256,1152]{1,0:T(8,128)(2,1)} %copy-done.2, ...), custom_call_target="tpu_custom_call" | custom-call | bytes 1024 | tf_op jit(solution)/shard_map/second_back/pallas_call | solution.py:222
  184.4 12.1 %attention_back.1 = (bf16[1152,1152]{1,0:T(8,128)(2,1)}, f32[256,1152]{1,0:T(8,128)}, bf16[256,1152]{1,0:T(8,128)(2,1)}, bf16[144,1152]{1,0:T(8,128)(2,1)}, bf16[144,1152]{1,0:T(8,128)(2,1)}) custom-call(bf16[144,1152]{1,0:T(8,128)(2,1)} %copy-done.3, bf16[144,1152]{1,0:T(8,128)(2,1)} %copy-done.7, bf16[144,1152]{1,0:T(8,128)(2,1)} %copy-done.9, ...), custom_call_target="tpu_custom_call" | custom-call | bytes 1024 | tf_op jit(solution)/shard_map/attention_back/pallas_call | solution.py:222
  208.0 3.0 output.1
  221.2 3.8 %first_back.1 = (bf16[256,1152]{1,0:T(8,128)(2,1)}, bf16[6,2,288]{2,1,0:T(2,128)(2,1)}, bf16[6,2,288]{2,1,0:T(2,128)(2,1)}) custom-call(bf16[256,1152]{1,0:T(8,128)(2,1)} %copy-done.22, bf16[256,1152]{1,0:T(8,128)(2,1)} %copy-done.47, f32[256,1152]{1,0:T(8,128)} %get-tuple-element.297.residual_grad, bf16[256,1152]{1,0:T(8,128)(2,1)} %get-tuple-element.210.kept, ...), custom_call_target="tpu_custom_call" | custom-call | bytes 1024 | tf_op jit(solution)/shard_map/first_back/pallas_call | solution.py:222
  243.4 4.7 %collective-permute-done.64.refs_0_ = bf16[144,1152]{1,0:T(8,128)(2,1)} collective-permute-done((bf16[144,1152]{1,0:T(8,128)(2,1)}, bf16[144,1152]{1,0:T(8,128)(2,1)}, u32[]{:S(2)}, u32[]{:S(2)}) %collective-permute-start.64) | collective-permute-done | bytes 331808 | tf_op jit(solution)/shard_map/ppermute | solution.py:118
  248.1 6.1 %collective-permute-done.65 = bf16[144,1152]{1,0:T(8,128)(2,1)} collective-permute-done((bf16[144,1152]{1,0:T(8,128)(2,1)}, bf16[144,1152]{1,0:T(8,128)(2,1)}, u32[]{:S(2)}, u32[]{:S(2)}) %collective-permute-start.65) | collective-permute-done | bytes 331808 | tf_op jit(solution)/shard_map/ppermute | solution.py:118
  258.3 3.8 %convolution_select_fusion = f32[4,256,1152]{2,1,0:T(8,128)} fusion(bf16[4,128,1152]{2,1,0:T(8,128)(2,1)S(1)} %bitcast.73, bf16[4,256,1152]{2,1,0:T(8,128)(2,1)S(1)} %copy-done, pred[4,256]{1,0:T(4,128)(4,1)} %fusion.3, s32[4,128]{1,0:T(4,128)S(1)} %copy-done.67), kind=kOutput, calls=%fused_computation | convolution fusion | flops 304480256 | bytes 8260608 | tf_op jit(solution)/shard_map/bsi,bid->bsd/dot_general | solution.py:1194
  271.3 3.0 collective-permute-done.70
  274.3 3.4 %collective-permute-start.71 = (f32[1,4,4,144]{3,2,1,0:T(4,128)S(1)}, f32[1,4,4,144]{3,2,1,0:T(4,128)S(1)}, u32[]{:S(2)}, u32[]{:S(2)}) collective-permute-start(f32[1,4,4,144]{3,2,1,0:T(4,128)S(1)} %get-tuple-element.355), channel_id=1, source_target_pairs={{0,16},{4,20},{8,24},{12,28},{16,0},{20,4},{24,8},{28,12},{1,17},{... | collective-permute-start | bytes 27656 | tf_op jit(solution)/shard_map/ppermute | solution.py:56
  286.1 3.1 %multiply_add_fusion = (f32[144,1152]{1,0:T(8,128)}, f32[144,1152]{1,0:T(8,128)}, f32[144,1152]{1,0:T(8,128)}, f32[144,1152]{1,0:T(8,128)}) fusion(f32[144,1152]{1,0:T(8,128)S(1)} %copy-done.38, f32[]{:T(128)S(6)} %sub.34, f32[]{:T(128)} %bitcast.33, f32[144,1152]{1,0:T(8,128)S(1)} %copy-done.15, bf16[1152,1152]{1,0:T(8,128)(2,1)} %get-tuple-element.259.part, ...), kind=kLoop, calls=%fused_computation.14 | loop fusion | flops 3151872 | bytes 6635532 | tf_op jit(solution)/shard_map/add | solution.py:795
  289.3 6.4 %step_ada.1 = (f32[6,144,288]{2,1,0:T(8,128)}, f32[6,144,288]{2,1,0:T(8,128)}, f32[6,144,288]{2,1,0:T(8,128)}) custom-call(s32[1]{0:T(128)S(6)} %copy.49.steps, bf16[32,144]{1,0:T(8,128)(2,1)} %dynamic-slice_bitcast_fusion.cond, bf16[6,32,288]{2,1,0:T(8,128)(2,1)} %pad_maximum_fusion.grads.mods, f32[6,144,288]{2,1,0:T(8,128)} %bitcast.72, ...), custom_call_target="tpu_custom_call" | custom-call | bytes 1024 | tf_op jit(solution)/shard_map/step_ada/pallas_call | solution.py:838
  295.7 4.2 %step_attention.1 = (f32[3,144,288]{2,1,0:T(8,128)}, f32[3,144,288]{2,1,0:T(8,128)}, f32[3,144,288]{2,1,0:T(8,128)}, f32[144,288]{1,0:T(8,128)}, f32[144,288]{1,0:T(8,128)}, /*index=5*/f32[144,288]{1,0:T(8,128)}) custom-call(s32[1]{0:T(128)S(6)} %copy.49.steps, f32[144,1152]{1,0:T(8,128)} %get-tuple-element.356.gradient, f32[3,144,288]{2,1,0:T(8,128)} %refs_0_.1, ...), custom_call_target="tpu_custom_call" | custom-call | bytes 1024 | tf_op jit(solution)/shard_map/step_attention/pallas_call | solution.py:816
  300.8 2.6 fusion.1
  (335 shorter events, 137.6 us)
Async XLA Ops:
  2.2 12.9 %collective-permute-start.3 = (bf16[144,1152]{1,0:T(8,128)(2,1)S(1)}, bf16[144,1152]{1,0:T(8,128)(2,1)S(1)}, u32[]{:S(2)}, u32[]{:S(2)}) collective-permute-start(bf16[144,1152]{1,0:T(8,128)(2,1)S(1)} %concatenate.53.refs_0_), channel_id=1, source_target_pairs={{0,8},{8,16},{16,24},{24,28},{28,20},{20,12},{12,4},{4,0},{1,9},{9... | collective-permute-start | bytes 995336 | tf_op jit(solution)/shard_map/ppermute | solution.py:118
  15.1 13.4 %collective-permute-start.6 = (bf16[144,1152]{1,0:T(8,128)(2,1)S(1)}, bf16[144,1152]{1,0:T(8,128)(2,1)S(1)}, u32[]{:S(2)}, u32[]{:S(2)}) collective-permute-start(bf16[144,1152]{1,0:T(8,128)(2,1)S(1)} %collective-permute-done.3.refs_1_), channel_id=1, source_target_pairs={{0,8},{8,16},{16,24},{24,28},{28,20},{20,12},{12,4},{4,0},{1,9},{9... | collective-permute-start | bytes 995336 | tf_op jit(solution)/shard_map/ppermute | solution.py:118
  16.8 11.8 %collective-permute-start.7 = (bf16[144,1152]{1,0:T(8,128)(2,1)S(1)}, bf16[144,1152]{1,0:T(8,128)(2,1)S(1)}, u32[]{:S(2)}, u32[]{:S(2)}) collective-permute-start(bf16[144,1152]{1,0:T(8,128)(2,1)S(1)} %collective-permute-done.4.refs_5_), channel_id=1, source_target_pairs={{8,0},{16,8},{24,16},{28,24},{20,28},{12,20},{4,12},{0,4},{9,1},{1... | collective-permute-start | bytes 995336 | tf_op jit(solution)/shard_map/ppermute | solution.py:118
  42.9 13.6 %collective-permute-start.14 = (bf16[144,1152]{1,0:T(8,128)(2,1)S(1)}, bf16[144,1152]{1,0:T(8,128)(2,1)S(1)}, u32[]{:S(2)}, u32[]{:S(2)}) collective-permute-start(bf16[144,1152]{1,0:T(8,128)(2,1)S(1)} %collective-permute-done.9.refs_3_), channel_id=1, source_target_pairs={{0,8},{8,16},{16,24},{24,28},{28,20},{20,12},{12,4},{4,0},{1,9},{9... | collective-permute-start | bytes 995336 | tf_op jit(solution)/shard_map/ppermute | solution.py:118
  50.0 13.7 %collective-permute-start.18 = (bf16[144,1152]{1,0:T(8,128)(2,1)S(1)}, bf16[144,1152]{1,0:T(8,128)(2,1)S(1)}, u32[]{:S(2)}, u32[]{:S(2)}) collective-permute-start(bf16[144,1152]{1,0:T(8,128)(2,1)S(1)} %convert_element_type.75.refs_0_), channel_id=1, source_target_pairs={{0,8},{8,16},{16,24},{24,28},{28,20},{20,12},{12,4},{4,0},{1,9},{9... | collective-permute-start | bytes 995336 | tf_op jit(solution)/shard_map/ppermute | solution.py:118
  56.7 15.4 %collective-permute-start.20 = (bf16[144,1152]{1,0:T(8,128)(2,1)S(1)}, bf16[144,1152]{1,0:T(8,128)(2,1)S(1)}, u32[]{:S(2)}, u32[]{:S(2)}) collective-permute-start(bf16[144,1152]{1,0:T(8,128)(2,1)S(1)} %bitcast_convert_fusion.refs_8_.refs_0_), channel_id=1, source_target_pairs={{8,0},{16,8},{24,16},{28,24},{20,28},{12,20},{4,12},{0,4},{9,1},{1... | collective-permute-start | bytes 995336 | tf_op jit(solution)/shard_map/ppermute | solution.py:118
  63.6 16.0 %collective-permute-start.22 = (bf16[144,1152]{1,0:T(8,128)(2,1)S(1)}, bf16[144,1152]{1,0:T(8,128)(2,1)S(1)}, u32[]{:S(2)}, u32[]{:S(2)}) collective-permute-start(bf16[144,1152]{1,0:T(8,128)(2,1)S(1)} %collective-permute-done.18.refs_1_), channel_id=1, source_target_pairs={{0,8},{8,16},{16,24},{24,28},{28,20},{20,12},{12,4},{4,0},{1,9},{9... | collective-permute-start | bytes 995336 | tf_op jit(solution)/shard_map/ppermute | solution.py:118
  64.9 14.7 %collective-permute-start.23 = (bf16[144,1152]{1,0:T(8,128)(2,1)S(1)}, bf16[144,1152]{1,0:T(8,128)(2,1)S(1)}, u32[]{:S(2)}, u32[]{:S(2)}) collective-permute-start(bf16[144,1152]{1,0:T(8,128)(2,1)S(1)} %collective-permute-done.19.refs_5_), channel_id=1, source_target_pairs={{8,0},{16,8},{24,16},{28,24},{20,28},{12,20},{4,12},{0,4},{9,1},{1... | collective-permute-start | bytes 995336 | tf_op jit(solution)/shard_map/ppermute | solution.py:118
  83.3 20.4 %collective-permute-start.25 = (bf16[256,1152]{1,0:T(8,128)(2,1)S(1)}, bf16[256,1152]{1,0:T(8,128)(2,1)S(1)}, u32[]{:S(2)}, u32[]{:S(2)}) collective-permute-start(bf16[256,1152]{1,0:T(8,128)(2,1)S(1)} %add_convert_fusion.3.own.attn_own), channel_id=1, source_target_pairs={{0,2},{1,3},{2,0},{3,1},{4,6},{5,7},{6,4},{7,5},{8,10},{9,11},{10,... | collective-permute-start | bytes 1769480 | tf_op jit(solution)/shard_map/ppermute | solution.py:39
  87.3 16.4 %collective-permute-start.26 = (bf16[144,1152]{1,0:T(8,128)(2,1)S(1)}, bf16[144,1152]{1,0:T(8,128)(2,1)S(1)}, u32[]{:S(2)}, u32[]{:S(2)}) collective-permute-start(bf16[144,1152]{1,0:T(8,128)(2,1)S(1)} %collective-permute-done.22.refs_2_), channel_id=1, source_target_pairs={{0,8},{8,16},{16,24},{24,28},{28,20},{20,12},{12,4},{4,0},{1,9},{9... | collective-permute-start | bytes 995336 | tf_op jit(solution)/shard_map/ppermute | solution.py:118
  88.3 15.3 %collective-permute-start.27 = (bf16[144,1152]{1,0:T(8,128)(2,1)S(1)}, bf16[144,1152]{1,0:T(8,128)(2,1)S(1)}, u32[]{:S(2)}, u32[]{:S(2)}) collective-permute-start(bf16[144,1152]{1,0:T(8,128)(2,1)S(1)} %collective-permute-done.23.refs_6_), channel_id=1, source_target_pairs={{8,0},{16,8},{24,16},{28,24},{20,28},{12,20},{4,12},{0,4},{9,1},{1... | collective-permute-start | bytes 995336 | tf_op jit(solution)/shard_map/ppermute | solution.py:118
  109.5 19.0 %collective-permute-start.34 = (bf16[144,1152]{1,0:T(8,128)(2,1)}, bf16[144,1152]{1,0:T(8,128)(2,1)S(1)}, u32[]{:S(2)}, u32[]{:S(2)}) collective-permute-start(bf16[144,1152]{1,0:T(8,128)(2,1)} %collective-permute-done.29.refs_14_.refs_6_), channel_id=1, source_target_pairs={{0,8},{8,16},{16,24},{24,28},{28,20},{20,12},{12,4},{4,0},{1,9},{9... | collective-permute-start | bytes 995336 | tf_op jit(solution)/shard_map/ppermute | solution.py:118
  128.6 11.9 %collective-permute-start.35 = (bf16[144,1152]{1,0:T(8,128)(2,1)}, bf16[144,1152]{1,0:T(8,128)(2,1)S(1)}, u32[]{:S(2)}, u32[]{:S(2)}) collective-permute-start(bf16[144,1152]{1,0:T(8,128)(2,1)} %get-tuple-element.234), channel_id=1, source_target_pairs={{8,0},{16,8},{24,16},{28,24},{20,28},{12,20},{4,12},{0,4},{9,1},{1... | collective-permute-start | bytes 995336 | tf_op jit(solution)/shard_map/ppermute | solution.py:118
  144.2 22.5 %collective-permute-start.38 = (bf16[256,1152]{1,0:T(8,128)(2,1)S(1)}, bf16[256,1152]{1,0:T(8,128)(2,1)S(1)}, u32[]{:S(2)}, u32[]{:S(2)}) collective-permute-start(bf16[256,1152]{1,0:T(8,128)(2,1)S(1)} %add_convert_fusion.2.own), channel_id=1, source_target_pairs={{0,2},{1,3},{2,0},{3,1},{4,6},{5,7},{6,4},{7,5},{8,10},{9,11},{10,... | collective-permute-start | bytes 1769480 | tf_op jit(solution)/shard_map/ppermute | solution.py:39
  147.2 15.5 %collective-permute-start.41 = (bf16[144,1152]{1,0:T(8,128)(2,1)}, bf16[144,1152]{1,0:T(8,128)(2,1)S(1)}, u32[]{:S(2)}, u32[]{:S(2)}) collective-permute-start(bf16[144,1152]{1,0:T(8,128)(2,1)} %get-tuple-element.248), channel_id=1, source_target_pairs={{8,0},{16,8},{24,16},{28,24},{20,28},{12,20},{4,12},{0,4},{9,1},{1... | collective-permute-start | bytes 995336 | tf_op jit(solution)/shard_map/ppermute | solution.py:118
  148.0 14.7 %collective-permute-start.42 = (bf16[144,1152]{1,0:T(8,128)(2,1)}, bf16[144,1152]{1,0:T(8,128)(2,1)S(1)}, u32[]{:S(2)}, u32[]{:S(2)}) collective-permute-start(bf16[144,1152]{1,0:T(8,128)(2,1)} %get-tuple-element.249), channel_id=1, source_target_pairs={{0,8},{8,16},{16,24},{24,28},{28,20},{20,12},{12,4},{4,0},{1,9},{9... | collective-permute-start | bytes 995336 | tf_op jit(solution)/shard_map/ppermute | solution.py:118
  154.9 11.8 %collective-permute-start.39 = (bf16[144,1152]{1,0:T(8,128)(2,1)}, bf16[144,1152]{1,0:T(8,128)(2,1)S(1)}, u32[]{:S(2)}, u32[]{:S(2)}) collective-permute-start(bf16[144,1152]{1,0:T(8,128)(2,1)} %get-tuple-element.243), channel_id=1, source_target_pairs={{8,0},{16,8},{24,16},{28,24},{20,28},{12,20},{4,12},{0,4},{9,1},{1... | collective-permute-start | bytes 995336 | tf_op jit(solution)/shard_map/ppermute | solution.py:118
  166.7 11.7 %collective-permute-start.46 = (bf16[256,1152]{1,0:T(8,128)(2,1)}, bf16[256,1152]{1,0:T(8,128)(2,1)S(1)}, u32[]{:S(2)}, u32[]{:S(2)}) collective-permute-start(bf16[256,1152]{1,0:T(8,128)(2,1)} %get-tuple-element.268), channel_id=1, source_target_pairs={{0,1},{1,0},{2,3},{3,2},{4,5},{5,4},{6,7},{7,6},{8,9},{9,8},{10,11... | collective-permute-start | bytes 1769480 | tf_op jit(solution)/shard_map/ppermute | solution.py:35
  180.7 15.9 %collective-permute-start.47 = (bf16[256,1152]{1,0:T(8,128)(2,1)S(1)}, bf16[256,1152]{1,0:T(8,128)(2,1)S(1)}, u32[]{:S(2)}, u32[]{:S(2)}) collective-permute-start(bf16[256,1152]{1,0:T(8,128)(2,1)S(1)} %add_convert_fusion.1.own), channel_id=1, source_target_pairs={{0,2},{1,3},{2,0},{3,1},{4,6},{5,7},{6,4},{7,5},{8,10},{9,11},{10,... | collective-permute-start | bytes 1769480 | tf_op jit(solution)/shard_map/ppermute | solution.py:39
  182.3 14.1 %collective-permute-start.48 = (bf16[144,1152]{1,0:T(8,128)(2,1)}, bf16[144,1152]{1,0:T(8,128)(2,1)S(1)}, u32[]{:S(2)}, u32[]{:S(2)}) collective-permute-start(bf16[144,1152]{1,0:T(8,128)(2,1)} %get-tuple-element.279), channel_id=1, source_target_pairs={{8,0},{16,8},{24,16},{28,24},{20,28},{12,20},{4,12},{0,4},{9,1},{1... | collective-permute-start | bytes 995336 | tf_op jit(solution)/shard_map/ppermute | solution.py:118
  182.9 13.6 %collective-permute-start.49 = (bf16[144,1152]{1,0:T(8,128)(2,1)}, bf16[144,1152]{1,0:T(8,128)(2,1)S(1)}, u32[]{:S(2)}, u32[]{:S(2)}) collective-permute-start(bf16[144,1152]{1,0:T(8,128)(2,1)} %get-tuple-element.280), channel_id=1, source_target_pairs={{0,8},{8,16},{16,24},{24,28},{28,20},{20,12},{12,4},{4,0},{1,9},{9... | collective-permute-start | bytes 995336 | tf_op jit(solution)/shard_map/ppermute | solution.py:118
  200.2 18.8 %collective-permute-start.51 = (bf16[256,1152]{1,0:T(8,128)(2,1)S(1)}, bf16[256,1152]{1,0:T(8,128)(2,1)S(1)}, u32[]{:S(2)}, u32[]{:S(2)}) collective-permute-start(bf16[256,1152]{1,0:T(8,128)(2,1)S(1)} %add_convert_fusion.own), channel_id=1, source_target_pairs={{0,2},{1,3},{2,0},{3,1},{4,6},{5,7},{6,4},{7,5},{8,10},{9,11},{10,... | collective-permute-start | bytes 1769480 | tf_op jit(solution)/shard_map/ppermute | solution.py:39
  206.0 13.1 %collective-permute-start.54 = (bf16[144,1152]{1,0:T(8,128)(2,1)}, bf16[144,1152]{1,0:T(8,128)(2,1)S(1)}, u32[]{:S(2)}, u32[]{:S(2)}) collective-permute-start(bf16[144,1152]{1,0:T(8,128)(2,1)} %get-tuple-element.293), channel_id=1, source_target_pairs={{8,0},{16,8},{24,16},{28,24},{20,28},{12,20},{4,12},{0,4},{9,1},{1... | collective-permute-start | bytes 995336 | tf_op jit(solution)/shard_map/ppermute | solution.py:118
  206.6 12.5 %collective-permute-start.55 = (bf16[144,1152]{1,0:T(8,128)(2,1)}, bf16[144,1152]{1,0:T(8,128)(2,1)S(1)}, u32[]{:S(2)}, u32[]{:S(2)}) collective-permute-start(bf16[144,1152]{1,0:T(8,128)(2,1)} %get-tuple-element.294), channel_id=1, source_target_pairs={{0,8},{8,16},{16,24},{24,28},{28,20},{20,12},{12,4},{4,0},{1,9},{9... | collective-permute-start | bytes 995336 | tf_op jit(solution)/shard_map/ppermute | solution.py:118
  221.2 20.3 %collective-permute-start.63 = (bf16[256,1152]{1,0:T(8,128)(2,1)S(1)}, bf16[256,1152]{1,0:T(8,128)(2,1)S(1)}, u32[]{:S(2)}, u32[]{:S(2)}) collective-permute-start(bf16[256,1152]{1,0:T(8,128)(2,1)S(1)} %copy-done.44), channel_id=1, source_target_pairs={{0,1},{1,0},{2,3},{3,2},{4,5},{5,4},{6,7},{7,6},{8,9},{9,8},{10,11... | collective-permute-start | bytes 1769480 | tf_op jit(solution)/shard_map/ppermute | solution.py:35
  228.2 14.7 %collective-permute-start.62 = (bf16[256,1152]{1,0:T(8,128)(2,1)}, bf16[256,1152]{1,0:T(8,128)(2,1)S(1)}, u32[]{:S(2)}, u32[]{:S(2)}) collective-permute-start(bf16[256,1152]{1,0:T(8,128)(2,1)} %get-tuple-element.306), channel_id=1, source_target_pairs={{0,1},{1,0},{2,3},{3,2},{4,5},{5,4},{6,7},{7,6},{8,9},{9,8},{10,11... | collective-permute-start | bytes 1769480 | tf_op jit(solution)/shard_map/ppermute | solution.py:35
  237.4 28.3 %collective-permute-start.68 = (bf16[144,1152]{1,0:T(8,128)(2,1)}, bf16[144,1152]{1,0:T(8,128)(2,1)}, u32[]{:S(2)}, u32[]{:S(2)}) collective-permute-start(bf16[144,1152]{1,0:T(8,128)(2,1)} %add_blocks.16), channel_id=1, source_target_pairs={{8,0},{16,8},{24,16},{28,24},{20,28},{12,20},{4,12},{0,4},{9,1},{1... | collective-permute-start | bytes 995336 | tf_op jit(solution)/shard_map/ppermute | solution.py:118
  239.5 14.8 %collective-permute-start.65 = (bf16[144,1152]{1,0:T(8,128)(2,1)}, bf16[144,1152]{1,0:T(8,128)(2,1)}, u32[]{:S(2)}, u32[]{:S(2)}) collective-permute-start(bf16[144,1152]{1,0:T(8,128)(2,1)} %get-tuple-element.311), channel_id=1, source_target_pairs={{8,0},{16,8},{24,16},{28,24},{20,28},{12,20},{4,12},{0,4},{9,1},{1... | collective-permute-start | bytes 995336 | tf_op jit(solution)/shard_map/ppermute | solution.py:118
  280.9 19.8 %collective-permute-start.75 = (bf16[144,1152]{1,0:T(8,128)(2,1)}, bf16[144,1152]{1,0:T(8,128)(2,1)S(1)}, u32[]{:S(2)}, u32[]{:S(2)}) collective-permute-start(bf16[144,1152]{1,0:T(8,128)(2,1)} %add_blocks.17), channel_id=1, source_target_pairs={{8,0},{16,8},{24,16},{28,24},{20,28},{12,20},{4,12},{0,4},{9,1},{1... | collective-permute-start | bytes 995336 | tf_op jit(solution)/shard_map/ppermute | solution.py:118
  282.6 17.3 %collective-permute-start.72 = (f32[2,1,4,144]{3,2,0,1:T(4,128)S(1)}, f32[2,1,4,144]{3,2,0,1:T(4,128)S(1)}, u32[]{:S(2)}, u32[]{:S(2)}) collective-permute-start(f32[2,1,4,144]{3,2,0,1:T(4,128)S(1)} %get-tuple-element.351), channel_id=1, source_target_pairs={{0,4},{4,0},{8,12},{12,8},{16,20},{20,16},{24,28},{28,24},{1,5},{5... | collective-permute-start | bytes 13832 | tf_op jit(solution)/shard_map/ppermute | solution.py:56
  284.0 15.9 %collective-permute-start.73 = (f32[2,1,4,144]{3,2,0,1:T(4,128)S(1)}, f32[2,1,4,144]{3,2,0,1:T(4,128)S(1)}, u32[]{:S(2)}, u32[]{:S(2)}) collective-permute-start(f32[2,1,4,144]{3,2,0,1:T(4,128)S(1)} %get-tuple-element.353), channel_id=1, source_target_pairs={{0,8},{4,12},{8,0},{12,4},{16,24},{20,28},{24,16},{28,20},{1,9},{5... | collective-permute-start | bytes 13832 | tf_op jit(solution)/shard_map/ppermute | solution.py:56
  286.1 13.8 %collective-permute-start.74 = (f32[2,1,4,144]{3,2,0,1:T(4,128)S(1)}, f32[2,1,4,144]{3,2,0,1:T(4,128)S(1)}, u32[]{:S(2)}, u32[]{:S(2)}) collective-permute-start(f32[2,1,4,144]{3,2,0,1:T(4,128)S(1)} %get-tuple-element.352), channel_id=1, source_target_pairs={{0,12},{4,8},{8,4},{12,0},{16,28},{20,24},{24,20},{28,16},{1,13},{... | collective-permute-start | bytes 13832 | tf_op jit(solution)/shard_map/ppermute | solution.py:56
  (115 other events, 938.0 us)
where the time goes:
time: 305 us; the launch traced here: 303 us
  Pallas kernels  116 us (38%)
  starting transfers between devices  76.3 us (25%)
  waiting for transfers between devices  75.4 us (25%)
  other arithmetic  19.6 us (6%)
  local copies, waits for them, and re-layouts  7.61 us (2%)
  matrix products  6.04 us (2%)
    pallas_call x24, Pallas kernels, run(): pl.pallas_call(kernel, out_shape=[jax.ShapeDtypeStruct(shape, dtype) for...  105 us
    ppermute x42, starting transfers between devices, hop(): return lax.ppermute(values, 'dp', clockwise if direction > 0 else backward)  45.6 us
    ppermute x42, waiting for transfers between devices, hop(): return lax.ppermute(values, 'dp', clockwise if direction > 0 else backward)  37.2 us
    ppermute x16, waiting for transfers between devices, swap_dp(): return lax.ppermute(values, 'dp', [(i, i ^ bit) for i in range(size)])  23 us
    ppermute x16, starting transfers between devices, swap_dp(): return lax.ppermute(values, 'dp', [(i, i ^ bit) for i in range(size)])  21.5 us
    ppermute x11, waiting for transfers between devices, swap_core(): return lax.ppermute(values, 'mp', [(j, j ^ 1) for j in range(4)])  10.5 us
    ppermute x6, starting transfers between devices, swap_x(): return lax.ppermute(values, 'mp', [(j, j ^ 2) for j in range(4)])  7.67 us
    pallas_call x1, Pallas kernels, step_ada(): pl.pallas_call(partial(ada_step, rate), grid=(count,), out_shape=[jax.Sha...  6.38 us
  transfers between devices with their start and end apart: 76, of which 29 were waited for; matrix products, arithmetic and copies ran while one was open for 6% of the time, Pallas kernels for 36%

commit v1 on v0

--- a/solution.py
+++ b/solution.py
@@ -198,10 +198,8 @@
     def finish(self, sides, moved):
         self.held.update(zip(sides, moved))
 
-    def total(self):
-        at = ring_device_at(lax.axis_index("dp"), 0)
-        block = lax.dynamic_slice_in_dim(self.part, at * self.rows, self.rows, 0)
-        return self.held["a"].astype(f32) + self.held["b"].astype(f32) + block.astype(f32)
+    def given(self):
+        return self.held["a"], self.held["b"], self.part
 
 
 def gather_plain(shard):
@@ -228,6 +226,7 @@
         + [pltpu.SemaphoreType.DMA((48,))]
         if by_copy
         else [],
+        compiler_params=pltpu.CompilerParams(vmem_limit_bytes=20 << 20),
         cost_estimate=pl.CostEstimate(flops=0, bytes_accessed=1024, transcendentals=0),
         name=name,
     )(*args)
@@ -293,39 +292,40 @@
 
 def kernel_add(distances, part, *refs):
     count = len(distances)
-    moved, outs, refs = refs[:count], refs[count : 2 * count], refs[2 * count :]
-    copies = Copies(refs[-1])
+    moved, outs, blocks, semaphores = refs[:count], refs[count : 2 * count], refs[2 * count], refs[-1]
+    copies = Copies(semaphores)
     rows = outs[0].shape[0]
     arriving = []
     for k, distance in enumerate(distances):
         at = pl.multiple_of(ring_device_at(lax.axis_index("dp"), distance) * rows, 8)
-        arriving.append(copies.start(moved[k], refs[2 * k]))
-        arriving.append(copies.start(part.at[pl.ds(at, rows), :], refs[2 * k + 1]))
-    leaving = []
+        arriving.append(copies.start(part.at[pl.ds(at, rows), :], blocks.at[k]))
     step = 48 if rows % 48 == 0 else rows
     for k in range(count):
-        wait(arriving[2 * k : 2 * k + 2])
-        total, block = refs[2 * k], refs[2 * k + 1]
+        arriving[k].wait()
+        total, block, out = moved[k], blocks.at[k], outs[k]
 
         def add(i, carry):
             at = pl.ds(pl.multiple_of(i * step, step), step)
-            total[at, :] = (total[at, :].astype(f32) + block[at, :].astype(f32)).astype(bf16)
+            out[at, :] = (total[at, :].astype(f32) + block[at, :].astype(f32)).astype(bf16)
             return carry
 
         lax.fori_loop(0, rows // step, add, 0)
-        leaving.append(copies.start(total, outs[k]))
-    wait(leaving)
 
 
 def add_blocks(part, moved, distances):
     shape = moved[0].shape
-    return run(
+    count = len(moved)
+    vmem = pl.BlockSpec(memory_space=pltpu.VMEM)
+    return pl.pallas_call(
         partial(kernel_add, distances),
-        "add_blocks",
-        [(shape, bf16)] * len(moved),
-        (part, *moved),
-        [(shape, bf16)] * (2 * len(moved)),
-    )
+        out_shape=[jax.ShapeDtypeStruct(shape, bf16)] * count,
+        in_specs=[pl.BlockSpec(memory_space=pl.ANY)] + [vmem] * count,
+        out_specs=[vmem] * count,
+        scratch_shapes=[pltpu.VMEM((count,) + shape, bf16), pltpu.SemaphoreType.DMA((count,))],
+        compiler_params=pltpu.CompilerParams(vmem_limit_bytes=8 << 20),
+        cost_estimate=pl.CostEstimate(flops=0, bytes_accessed=1024, transcendentals=0),
+        name="add_blocks",
+    )(part, *moved)
 
 
 def dot(a, b):
@@ -743,6 +743,37 @@
     leaving.append(copies.start(attn_grad, outs[0]))
     leaving += copies.first_blocks(attn_grad, lead, outs[3:])
     wait(leaving)
+
+
+def kernel_place(here, there, base, index, out):
+    image = pl.program_id(0)
+    rows = index.shape[2]
+    half = here.shape[0] // rows
+    pair = image // half
+    at = image_rows(rows, image - pair * half)
+    same = pair == core_here()
+    values = jnp.where(same, here[at, :], there[at, :])
+    select = lax.broadcasted_iota(jnp.int32, (base.shape[1], rows), 0) == index[0]
+    select = select.astype(f32)
+    kept = jnp.sum(select, axis=1, keepdims=True) > 0.5
+    placed = dot(select.astype(bf16), values)
+    out[0] = jnp.where(kept, placed, base[0].astype(f32)).astype(out.dtype)
+
+
+def place_kept(here, there, base, index, dtype):
+    images, seq, width = base.shape
+    count = index.shape[1]
+    whole = pl.BlockSpec(here.shape, lambda i: (0, 0))
+    spec = pl.BlockSpec((1, seq, width), lambda i: (i, 0, 0))
+    return pl.pallas_call(
+        kernel_place,
+        grid=(images,),
+        out_shape=jax.ShapeDtypeStruct(base.shape, dtype),
+        in_specs=[whole, whole, spec, pl.BlockSpec((1, 1, count), lambda i: (i, 0, 0))],
+        out_specs=spec,
+        cost_estimate=pl.CostEstimate(flops=0, bytes_accessed=1024, transcendentals=0),
+        name="place_kept",
+    )(here, there, base, index.reshape(images, 1, count))
 
 
 def kernel_output(own, moved, residual, grad, mods, kept_out, sums):
@@ -795,7 +826,23 @@
     return master, new_moment, decay * average + (1.0 - decay) * master
 
 
-def attention_step(rate, steps, gradient, *refs):
+def summed(given):
+    total = given[0][...].astype(f32)
+    for ref in given[1:]:
+        total = total + ref[...].astype(f32)
+    return total
+
+
+def one_step(rate, count, index, steps, *refs):
+    given, refs = refs[:count], refs[count:]
+    values = new_state(*[ref[...] for ref in refs[:3]], summed(given), rate, steps[0].astype(f32))
+    for ref, value in zip(refs[3:], values):
+        ref[...] = value
+
+
+def attention_step(rate, count, index, steps, *refs):
+    given, refs = refs[:count], refs[count:]
+    gradient = summed(given)
     counts = steps[0].astype(f32)
     qkv, proj, qkv_out, proj_out = refs[:3], refs[3:6], refs[6:9], refs[9:]
     local = proj[0].shape[1]
@@ -810,39 +857,51 @@
         ref[...] = value
 
 
-def step_attention(qkv, proj, gradient, rate, steps):
-    whole = pl.BlockSpec(memory_space=pltpu.VMEM)
-    size = qkv[0].size + proj[0].size
+def step_weights(kernel, name, state, given, rate, steps):
+    rows = given[0].shape[0]
+    block = 48 if rows % 48 == 0 else rows
+    count = rows // block
+
+    def spec(x):
+        if x.ndim == 3:
+            return pl.BlockSpec((x.shape[0], block, x.shape[2]), lambda i, index: (0, i, 0))
+        return pl.BlockSpec((block, x.shape[1]), lambda i, index: (i, 0))
+
+    own = pl.BlockSpec((block, given[0].shape[1]), lambda i, index: (index[0] * count + i, 0))
+    specs = [spec(x) for x in given[:2]] + [own] * (len(given) - 2)
     return pl.pallas_call(
-        partial(attention_step, rate),
-        out_shape=[jax.ShapeDtypeStruct(x.shape, f32) for x in qkv + proj],
-        in_specs=[pl.BlockSpec(memory_space=pltpu.SMEM)] + [whole] * 7,
-        out_specs=[whole] * 6,
+        partial(kernel, rate, len(given)),
+        grid_spec=pltpu.PrefetchScalarGridSpec(
+            num_scalar_prefetch=1,
+            grid=(count,),
+            in_specs=[pl.BlockSpec(memory_space=pltpu.SMEM)] + specs + [spec(x) for x in state],
+            out_specs=[spec(x) for x in state],
+        ),
+        out_shape=[jax.ShapeDtypeStruct(x.shape, f32) for x in state],
         cost_estimate=pl.CostEstimate(flops=0, bytes_accessed=1024, transcendentals=0),
-        name="step_attention",
-    )(steps, gradient, *qkv, *proj)
+        name=name,
+    )(lax.axis_index("dp").astype(jnp.int32).reshape(1), steps, *given, *state)
 
 
 def ada_step(rate, steps, cond, mods, weight, moment, average, master, new_moment, ema):
     counts = steps[0].astype(f32)
-    gradient = lax.dot_general(
-        cond[...], mods[0], (((0,), (0,)), ((), ())), preferred_element_type=f32
-    )
-    values = new_state(weight[0], moment[0], average[0], gradient, rate, counts)
-    master[0], new_moment[0], ema[0] = values
+    for k in range(weight.shape[0]):
+        gradient = dot_first(cond[...], mods[k])
+        values = new_state(weight[k], moment[k], average[k], gradient, rate, counts)
+        master[k], new_moment[k], ema[k] = values
 
 
 def step_ada(weight, moment, average, cond, mods, rate, steps):
     count, rows, columns = weight.shape
-    spec = pl.BlockSpec((1, rows, columns), lambda k: (k, 0, 0))
+    spec = pl.BlockSpec((2, rows, columns), lambda k: (k, 0, 0))
     return pl.pallas_call(
         partial(ada_step, rate),
-        grid=(count,),
+        grid=(count // 2,),
         out_shape=[jax.ShapeDtypeStruct(weight.shape, f32)] * 3,
         in_specs=[
             pl.BlockSpec(memory_space=pltpu.SMEM),
             pl.BlockSpec(cond.shape, lambda k: (0, 0)),
-            pl.BlockSpec((1,) + mods.shape[1:], lambda k: (k, 0, 0)),
+            pl.BlockSpec((2,) + mods.shape[1:], lambda k: (k, 0, 0)),
         ]
         + [spec] * 3,
         out_specs=[spec] * 3,
@@ -889,13 +948,23 @@
     index = lax.axis_index("dp")
     ring = dp_size == 8
 
+    live = []
+
     def tick(extras, *hops):
         hops = [(one, sides) for one, sides in hops if one is not None]
+        busy = [one for one, _ in hops]
+        idle = [one for one in live if one not in busy]
         moving = tuple(one.start(sides) for one, sides in hops)
-        held, moved = stage((tuple(extras()), moving))
+        work = tuple(extras())
+        resting = tuple((one.held["a"], one.held["b"]) for one in idle)
+        held, moved, resting = stage((work, moving, resting))
         for (one, sides), values in zip(hops, moved):
             one.finish(sides, values)
+        for one, values in zip(idle, resting):
+            one.finish("ab", values)
         return held
+
+    rate = 0.02 / math.sqrt(images * dp_size * kept_count)
 
     attn_low = jnp.concatenate(
         [qkv_weight[0], qkv_weight[1], qkv_weight[2], proj_weight.T], 1
@@ -1014,9 +1083,10 @@
             [((half, width), f32), ((half, width), bf16)],
             (kept_own, modulation, attn_own, attn_moved),
         )
-        return values, low, swap_core(low)
-
-    residual, hidden_here, hidden_there = tick(second_norm, (fc1_ring, "a"), (fc2_ring, "a"))
+        return values, low
+
+    residual, hidden_here = tick(second_norm, (fc1_ring, "a"), (fc2_ring, "a"))
+    hidden_here, hidden_there = tick(lambda: (hidden_here, swap_core(hidden_here)))
     if ring:
         fc1_pieces, fc1_places = fc1_ring.pieces()
 
@@ -1034,6 +1104,7 @@
     if ring:
         fc2_pieces, fc2_places = fc2_ring.pieces()
         fc2_sums = Scatter(fc2_grad, -1, first)
+        live.append(fc2_sums)
     else:
         fc2_sums = fc1_sums = attn_sums = None
 
@@ -1069,26 +1140,19 @@
         if ring:
             moving.append(Scatter(grad, -1, first))
             first = moving[0].start("ab")
-        outs = [((half, width), f32), ((half, width), bf16)]
-        sums = run(
-            partial(kernel_feed_out, fc2_places),
-            "feed_out",
-            outs,
-            (*fc2_pieces, activated),
-            [((width, units), bf16), ((total, units), bf16)] + outs,
-        )
-        return own_low, swap_x(own_low), grad, *sums, *first
-
-    hidden_own, hidden_moved, fc1_grad, own_mlp, other_mlp, *first = tick(
+        return own_low, swap_x(own_low), grad, activated, *first
+
+    hidden_own, hidden_moved, fc1_grad, activated, *first = tick(
         products, (fc2_sums, "ab+")
     )
     if ring:
         (fc1_sums,) = moving
         fc1_sums.part = fc1_grad
         fc1_sums.finish("ab", first)
+        live.append(fc1_sums)
 
     def second_back():
-        sums = run(
+        values, low, lines = run(
             kernel_second_back,
             "second_back",
             [((half, width), f32), ((half, width), bf16), ((3, images // 2, width), f32)],
@@ -1102,14 +1166,35 @@
                 modulation,
             ),
         )
-        return *sums, *(fc1_sums.prepare("ab") if ring else ())
-
-    residual_grad, out_here, late_mods, *sums = tick(second_back, (fc2_sums, "ab"))
+        outs = [((half, width), f32), ((half, width), bf16)]
+        mlp = run(
+            partial(kernel_feed_out, fc2_places),
+            "feed_out",
+            outs,
+            (*fc2_pieces, activated),
+            [((width, units), bf16), ((total, units), bf16)] + outs,
+        )
+        sums = ()
+        if ring:
+            held = stage((fc1_sums.held["a"], fc1_sums.held["b"], low))
+            fc1_sums.finish("ab", held[:2])
+            sums = fc1_sums.prepare("ab")
+        return values, low, lines, *mlp, *sums
+
+    residual_grad, out_here, late_mods, own_mlp, other_mlp, *sums = tick(
+        second_back, (fc2_sums, "ab")
+    )
     if ring:
         fc1_sums.finish("ab", sums)
-    out_here, out_there, mlp_own = tick(
-        lambda: (out_here, swap_core(out_here), add_low(own_mlp, swap_core(other_mlp)))
-    )
+
+    def between():
+        sums = fc2_sums.prepare("a") if ring else ()
+        low = add_low(own_mlp, swap_core(other_mlp))
+        return out_here, swap_core(out_here), low, *sums
+
+    out_here, out_there, mlp_own, *sums = tick(between)
+    if ring:
+        fc2_sums.finish("a", sums)
 
     def attention_back():
         outs = [((width, 4 * local), bf16), ((half, width), f32), ((half, width), bf16)]
@@ -1131,9 +1216,12 @@
         )
         return swap_x(mlp_own), *back
 
-    mlp_moved, attn_grad, own_part, other_part, *first = tick(attention_back, (fc1_sums, "ab"))
+    mlp_moved, attn_grad, own_part, other_part, *first = tick(
+        attention_back, (fc1_sums, "ab"), (fc2_sums, "a")
+    )
     if ring:
         attn_sums = Scatter(attn_grad, 1, first)
+        live.append(attn_sums)
 
     def output():
         return run(
@@ -1143,11 +1231,19 @@
             (mlp_own, mlp_moved, residual, grad_own, modulation),
         )
 
+    back_own, mlp_moved = tick(
+        lambda: (add_low(own_part, swap_core(other_part)), mlp_moved)
+    )
+
     def attention_back_sums():
-        own = add_low(own_part, swap_core(other_part))
-        return own, swap_x(own), *output()
-
-    back_own, back_moved, kept_out, last_mods = tick(
+        given = fc2_sums.given() if ring else (scatter_plain(fc2_grad),)
+        state = (fc2_weight.T, fc2_moment.T, fc2_average.T)
+        new = step_weights(one_step, "step_fc2", state, given, rate, step_count)
+        return swap_x(back_own), *output(), *new
+
+    if ring:
+        live.remove(fc2_sums)
+    back_moved, kept_out, last_mods, fc2_master, fc2_momentum, fc2_ema = tick(
         attention_back_sums, (attn_sums, "ab+"), (fc1_sums, "ab")
     )
 
@@ -1170,71 +1266,62 @@
                 last_mods,
             ),
         )
-        return kept, join_pair(mine, swap_core(partner), core, 1)
-
-    kept_grad, small = tick(first_back, (attn_sums, "ab"))
-
-    def spreads():
-        values = spread_round(small, 1, 0)
-        return values, spread_pair(kept_grad, core), spread_pair(kept_out, core)
-
-    small, kept_grad, kept_out = tick(spreads, (attn_sums, "ab"))
-    kept_grad, kept_out = [x.reshape(images, kept_count, width) for x in (kept_grad, kept_out)]
-
-    rate = 0.02 / math.sqrt(images * dp_size * kept_count)
-    steps = step_count[0].astype(f32)
-    positions = lax.broadcasted_iota(jnp.int32, (images, seq, kept_count), 1)
-    select = (kept_index[:, None, :] == positions).astype(bf16)
-    is_kept = jnp.any(kept_index[:, None, :] == positions, axis=2)[:, :, None]
-
-    def outputs():
+        return kept, join_pair(mine, swap_core(partner), core, 1), swap_core(kept_out)
+
+    kept_grad, small, kept_there = tick(first_back, (attn_sums, "ab"))
+
+    def first_spread():
+        sums = fc1_sums.prepare("a") if ring else ()
+        return spread_round(small, 1, 0), kept_there, kept_grad, *sums
+
+    small, kept_there, kept_grad, *sums = tick(first_spread, (attn_sums, "ab"))
+    if ring:
+        fc1_sums.finish("a", sums)
+
+    def last_spread():
         values = small
         for level in range(1, levels):
             values = spread_round(values, 1, level)
-        placed = jnp.einsum("bsi,bid->bsd", select, kept_grad, preferred_element_type=f32)
-        grads = jnp.where(is_kept, placed, cotangent.astype(f32))
-        placed = jnp.einsum("bsi,bid->bsd", select, kept_out, preferred_element_type=f32)
-        out = jnp.where(is_kept, placed.astype(bf16), tokens)
-        last = (fc2_sums.held["a"], fc2_sums.held["b"]) if ring else ()
-        return values, grads, out, *last
-
-    mod_grad_all, tokens_grad, block_out, *last = tick(
-        outputs, (attn_sums, "a"), (fc1_sums, "a")
+        out = place_kept(kept_out, kept_there, tokens, kept_index, bf16)
+        return values, kept_grad, swap_core(kept_grad), out
+
+    mod_grad_all, kept_grad, grad_there, block_out = tick(
+        last_spread, (attn_sums, "a"), (fc1_sums, "a")
     )
-    if ring:
-        fc2_sums.finish("ab", last)
-    (silu_part,) = run(
-        kernel_silu, "silu", [((dp_size * images, own_d), f32)], (mod_grad_all, ada_state[0])
-    )
-    silu_part = silu_part + swap_core(silu_part)
-    silu_part = silu_part + swap_x(silu_part)
-    ada_new = step_ada(*ada_state, cond_own, mod_grad_all, rate, step_count)
+
+    def silu_first():
+        (part,) = run(
+            kernel_silu, "silu", [((dp_size * images, own_d), f32)], (mod_grad_all, ada_state[0])
+        )
+        return part + swap_core(part), mod_grad_all, kept_grad
+
+    silu_part, mod_grad_all, kept_grad = tick(silu_first)
+
+    def silu_second():
+        given = fc1_sums.given() if ring else (scatter_plain(fc1_grad),)
+        state = (fc1_weight, fc1_moment, fc1_average)
+        new = step_weights(one_step, "step_fc1", state, given, rate, step_count)
+        new += step_ada(*ada_state, cond_own, mod_grad_all, rate, step_count)
+        return silu_part + swap_x(silu_part), *new
+
+    silu_part, fc1_master, fc1_momentum, fc1_ema, *ada_new = tick(silu_second)
+    silu_blocks = silu_part.reshape(dp_size, images, own_d)
+
+    def silu_third():
+        blocks = silu_blocks
+        for level in reversed(range(1, levels)):
+            blocks = turn_round(blocks, level)
+        given = attn_sums.given() if ring else (scatter_plain(attn_grad),)
+        state = (qkv_weight, qkv_moment, qkv_average)
+        state += (proj_weight.T, proj_moment.T, proj_average.T)
+        new = step_weights(attention_step, "step_attention", state, given, rate, step_count)
+        return blocks, kept_grad, *new
+
+    silu_blocks, kept_grad, *attn_new = tick(silu_third)
+    qkv_master, qkv_momentum, qkv_ema, proj_master, proj_momentum, proj_ema = attn_new
+    tokens_grad = place_kept(kept_grad, grad_there, cotangent, kept_index, f32)
+    silu_blocks = in_order(turn_round(silu_blocks, 0))
     ada_master, ada_momentum, ada_ema = [jnp.moveaxis(x, 0, 1) for x in ada_new]
-    attn_shard = attn_sums.total() if ring else scatter_plain(attn_grad)
-    fc1_shard = fc1_sums.total() if ring else scatter_plain(fc1_grad)
-    if ring:
-        fc2_sums.finish("a", fc2_sums.start("a"))
-        fc2_shard = fc2_sums.total()
-    else:
-        fc2_shard = scatter_plain(fc2_grad)
-    fc2_master, fc2_momentum, fc2_ema = new_state(
-        fc2_weight.T, fc2_moment.T, fc2_average.T, fc2_shard, rate, steps
-    )
-    silu_blocks = silu_part.reshape(dp_size, images, own_d)
-    attn_new = step_attention(
-        (qkv_weight, qkv_moment, qkv_average),
-        (proj_weight.T, proj_moment.T, proj_average.T),
-        attn_shard,
-        rate,
-        step_count,
-    )
-    for level in reversed(range(levels)):
-        silu_blocks = turn_round(silu_blocks, level)
-    silu_blocks = in_order(silu_blocks)
-    qkv_master, qkv_momentum, qkv_ema, proj_master, proj_momentum, proj_ema = attn_new
-    fc1_master, fc1_momentum, fc1_ema = new_state(
-        fc1_weight, fc1_moment, fc1_average, fc1_shard, rate, steps
-    )
     silu_grad = jnp.moveaxis(silu_blocks, 0, 1).reshape(images, width)
     silu_value, silu_pull = jax.vjp(jax.nn.silu, cond_float)
     condition_grad = silu_pull(silu_grad)[0]

time: 305 us -> 266 us (0.87)
  Pallas kernels: 116 us -> 89.3 us
  other arithmetic: 19.6 us -> 3.86 us
  waiting for transfers between devices: 75.4 us -> 86.2 us
  matrix products: 6.04 us -> 0 us
  starting transfers between devices: 76.3 us -> 71.1 us
  local copies, waits for them, and re-layouts: 7.61 us -> 12.3 us
    pallas_call x24 -> x15, Pallas kernels: 105 us -> 54.6 us  [run(): pl.pallas_call(kernel, out_shape=[jax.ShapeDtypeStruct(shape, dtype) for...]
    pallas_call x2 -> x15, Pallas kernels: 10.6 us -> 34.7 us  [the longest x3 13 us: step_weights(): pl.pallas_call(partial(kernel, rate, len(given)), grid_spec=pltpu.Prefetc...]
    ppermute x16, waiting for transfers between devices: 23 us -> 31 us  [swap_dp(): return lax.ppermute(values, 'dp', [(i, i ^ bit) for i in range(size)])]
    unnamed x143 -> x91, local copies, waits for them, and re-layouts: 5.35 us -> 11.6 us
    ppermute x42, waiting for transfers between devices: 37.2 us -> 43.4 us  [hop(): return lax.ppermute(values, 'dp', clockwise if direction > 0 else backward)]
    dot_general x2 -> x0, matrix products: 6.04 us -> none  [the longest x1 3.78 us: outputs(): jnp.einsum('bsi,bid->bsd', select, kept_grad, preferred_element_type=f32)]
    add x3 -> x2, other arithmetic: 3.9 us -> 0.01 us  [the longest x1 0.01 us: silu_second(): return (silu_part + swap_x(silu_part), *new)]
  transfers between devices with their start and end apart: 76 -> 76, of which waited for: 29 -> 33; matrix products, arithmetic and copies ran while one was open for 6% -> 0% of each run, Pallas kernels for 36% -> 33%
where the time goes in v1:
time: 266 us; the launch traced here: 265 us
  Pallas kernels  89.3 us (34%)
  waiting for transfers between devices  86.2 us (32%)
  starting transfers between devices  71.1 us (27%)
  local copies, waits for them, and re-layouts  12.3 us (5%)
  other arithmetic  3.86 us (1%)
    pallas_call x15, Pallas kernels, run(): pl.pallas_call(kernel, out_shape=[jax.ShapeDtypeStruct(shape, dtype) for...  54.6 us
    ppermute x42, waiting for transfers between devices, hop(): return lax.ppermute(values, 'dp', clockwise if direction > 0 else backward)  43.4 us
    ppermute x42, starting transfers between devices, hop(): return lax.ppermute(values, 'dp', clockwise if direction > 0 else backward)  43.3 us
    ppermute x16, waiting for transfers between devices, swap_dp(): return lax.ppermute(values, 'dp', [(i, i ^ bit) for i in range(size)])  31 us
    ppermute x16, starting transfers between devices, swap_dp(): return lax.ppermute(values, 'dp', [(i, i ^ bit) for i in range(size)])  18.6 us
    pallas_call x3, Pallas kernels, step_weights(): pl.pallas_call(partial(kernel, rate, len(given)), grid_spec=pltpu.Prefetc...  13 us
    unnamed x91, local copies, waits for them, and re-layouts  11.6 us
    ppermute x11, waiting for transfers between devices, swap_core(): return lax.ppermute(values, 'mp', [(j, j ^ 1) for j in range(4)])  10.2 us
  transfers between devices with their start and end apart: 76, of which 33 were waited for; matrix products, arithmetic and copies ran while one was open for 0% of the time, Pallas kernels for 33%

profile of v1, /device:TPU:0, one launch (start us, length us, event | category | flops | bytes accessed | tf_op | source)
XLA Modules:
  0.0 265.1 jit_solution(3877940230809579422)
XLA Ops:
  2.2 3.1 %collective-permute-start.3 = (bf16[144,1152]{1,0:T(8,128)(2,1)S(1)}, bf16[144,1152]{1,0:T(8,128)(2,1)S(1)}, u32[]{:S(2)}, u32[]{:S(2)}) collective-permute-start(bf16[144,1152]{1,0:T(8,128)(2,1)S(1)} %concatenate.41.refs_0_), channel_id=1, source_target_pairs={{0,8},{8,16},{16,24},{24,28},{28,20},{20,12},{12,4},{4,0},{1,9},{9... | collective-permute-start | bytes 995336 | tf_op jit(solution)/shard_map/ppermute | solution.py:118
  5.4 2.0 collective-permute-start
  10.7 2.1 first_norm.1
  17.2 2.9 %collective-permute-start.5 = (bf16[16,8,144]{2,0,1:T(8,128)(2,1)S(1)}, bf16[16,8,144]{2,0,1:T(8,128)(2,1)S(1)}, u32[]{:S(2)}, u32[]{:S(2)}) collective-permute-start(bf16[16,8,144]{2,0,1:T(8,128)(2,1)S(1)} %pad_maximum_fusion.3), channel_id=1, source_target_pairs={{0,16},{4,20},{8,24},{12,28},{16,0},{20,4},{24,8},{28,12},{1,17},{... | collective-permute-start | bytes 110600 | tf_op jit(solution)/shard_map/ppermute | solution.py:56
  20.2 8.8 %collective-permute-done.5 = bf16[16,8,144]{2,0,1:T(8,128)(2,1)S(1)} collective-permute-done((bf16[16,8,144]{2,0,1:T(8,128)(2,1)S(1)}, bf16[16,8,144]{2,0,1:T(8,128)(2,1)S(1)}, u32[]{:S(2)}, u32[]{:S(2)}) %collective-permute-start.5) | collective-permute-done | bytes 36896 | tf_op jit(solution)/shard_map/ppermute | solution.py:56
  30.5 2.2 collective-permute-start.9
  32.6 6.0 %collective-permute-done.8 = f32[6,16,288]{2,1,0:T(8,128)S(1)} collective-permute-done((f32[6,16,288]{2,1,0:T(8,128)S(1)}, f32[6,16,288]{2,1,0:T(8,128)S(1)}, u32[]{:S(2)}, u32[]{:S(2)}) %collective-permute-start.8) | collective-permute-done | bytes 110624 | tf_op jit(solution)/shard_map/ppermute | solution.py:56
  39.3 3.3 %collective-permute-done.9.refs_3_ = bf16[144,1152]{1,0:T(8,128)(2,1)S(1)} collective-permute-done((bf16[144,1152]{1,0:T(8,128)(2,1)S(1)}, bf16[144,1152]{1,0:T(8,128)(2,1)S(1)}, u32[]{:S(2)}, u32[]{:S(2)}) %collective-permute-start.9) | collective-permute-done | bytes 331808 | tf_op jit(solution)/shard_map/ppermute | solution.py:118
  47.4 5.2 %collective-permute-done.11 = f32[6,4,288]{2,1,0:T(4,128)S(1)} collective-permute-done((f32[6,4,288]{2,1,0:T(4,128)S(1)}, f32[6,4,288]{2,1,0:T(4,128)S(1)}, u32[]{:S(2)}, u32[]{:S(2)}) %collective-permute-start.11) | collective-permute-done | bytes 27680 | tf_op jit(solution)/shard_map/ppermute | solution.py:56
  65.9 3.2 %project.1 = (bf16[512,1152]{1,0:T(8,128)(2,1)S(1)}, bf16[512,864]{1,0:T(8,128)(2,1)S(1)}) custom-call(bf16[144,1152]{1,0:T(8,128)(2,1)S(1)} %concatenate.41.refs_0_, bf16[144,1152]{1,0:T(8,128)(2,1)S(1)} %collective-permute-done.3.refs_1_, bf16[144,1152]{1,0:T(8,128)(2,1)S(1)} %collective-permute-done.6.refs_2_, ...), custom_call_target="tpu_custom_call" | custom-call | bytes 1024 | tf_op jit(solution)/shard_map/project/pallas_call | solution.py:220
  69.2 6.0 %attend.1 = (bf16[512,288]{1,0:T(8,128)(2,1)S(1)}, f32[256,1152]{1,0:T(8,128)S(1)}, bf16[256,1152]{1,0:T(8,128)(2,1)S(1)}) custom-call(bf16[144,1152]{1,0:T(8,128)(2,1)S(1)} %concatenate.41.refs_0_, bf16[144,1152]{1,0:T(8,128)(2,1)S(1)} %collective-permute-done.3.refs_1_, bf16[144,1152]{1,0:T(8,128)(2,1)S(1)} %collective-permute-done.6.refs_2_, ...), custom_call_target="tpu_custom_call" | custom-call | bytes 1024 | tf_op jit(solution)/shard_map/attend/pallas_call | solution.py:220
  83.8 6.3 %collective-permute-done.28.refs_10_.refs_2_ = bf16[144,1152]{1,0:T(8,128)(2,1)S(1)} collective-permute-done((bf16[144,1152]{1,0:T(8,128)(2,1)}, bf16[144,1152]{1,0:T(8,128)(2,1)S(1)}, u32[]{:S(2)}, u32[]{:S(2)}) %collective-permute-start.28) | collective-permute-done | bytes 331808 | tf_op jit(solution)/shard_map/ppermute | solution.py:118
  91.7 5.7 %collective-permute-done.26.refs_3_ = bf16[144,1152]{1,0:T(8,128)(2,1)S(1)} collective-permute-done((bf16[144,1152]{1,0:T(8,128)(2,1)S(1)}, bf16[144,1152]{1,0:T(8,128)(2,1)S(1)}, u32[]{:S(2)}, u32[]{:S(2)}) %collective-permute-start.26) | collective-permute-done | bytes 331808 | tf_op jit(solution)/shard_map/ppermute | solution.py:118
  100.0 5.8 %collective-permute-done.30.refs_4_ = bf16[144,1152]{1,0:T(8,128)(2,1)S(1)} collective-permute-done((bf16[144,1152]{1,0:T(8,128)(2,1)S(1)}, bf16[144,1152]{1,0:T(8,128)(2,1)S(1)}, u32[]{:S(2)}, u32[]{:S(2)}) %collective-permute-start.30) | collective-permute-done | bytes 331808 | tf_op jit(solution)/shard_map/ppermute | solution.py:118
  108.4 7.8 %feed_forward.1 = (f32[512,1152]{1,0:T(8,128)S(1)}, bf16[512,1152]{1,0:T(8,128)(2,1)S(1)}, bf16[1152,1152]{1,0:T(8,128)(2,1)S(1)}, bf16[144,1152]{1,0:T(8,128)(2,1)S(1)}, bf16[144,1152]{1,0:T(8,128)(2,1)S(1)}) custom-call(bf16[144,1152]{1,0:T(8,128)(2,1)S(1)} %convert_element_type.37.refs_0_, bf16[144,1152]{1,0:T(8,128)(2,1)} %collective-permute-done.18.refs_1_, ...), custom_call_target="tpu_custom_call" | custom-call | bytes 1024 | tf_op jit(solution)/shard_map/feed_forward/pallas_call | solution.py:220
  119.6 8.4 %feed_back.1 = (bf16[512,1152]{1,0:T(8,128)(2,1)S(1)}, f32[256,1152]{1,0:T(8,128)S(1)}, bf16[256,1152]{1,0:T(8,128)(2,1)S(1)}) custom-call(bf16[144,1152]{1,0:T(8,128)(2,1)S(1)} %convert_element_type.37.refs_0_, bf16[144,1152]{1,0:T(8,128)(2,1)} %collective-permute-done.18.refs_1_, bf16[144,1152]{1,0:T(8,128)(2,1)S(1)} %collective-permute-done.22.refs_2_, ...), custom_call_target="tpu_custom_call" | custom-call | bytes 1024 | tf_op jit(solution)/shard_map/feed_back/pallas_call | solution.py:220
  133.3 3.9 %fc1_grad.1 = (bf16[1152,1152]{1,0:T(8,128)(2,1)S(1)}, bf16[144,1152]{1,0:T(8,128)(2,1)S(1)}, bf16[144,1152]{1,0:T(8,128)(2,1)S(1)}) custom-call(bf16[256,1152]{1,0:T(8,128)(2,1)S(1)} %get-tuple-element.273.refs_8_.here, bf16[256,1152]{1,0:T(8,128)(2,1)S(1)} %collective-permute-done.32.refs_9_.there, bf16[512,1152]{1,0:T(8,128)(2,1)S(1)} %get-tuple-element.292.pre), custom_call_target="tpu_custom_call" | custom-call | bytes 1024 | tf_op jit(solution)/shard_map/fc1_grad/pallas_call | solution.py:220
  139.3 2.7 %collective-permute-done.41.refs_0_ = bf16[144,1152]{1,0:T(8,128)(2,1)S(1)} collective-permute-done((bf16[144,1152]{1,0:T(8,128)(2,1)S(1)}, bf16[144,1152]{1,0:T(8,128)(2,1)S(1)}, u32[]{:S(2)}, u32[]{:S(2)}) %collective-permute-start.41) | collective-permute-done | bytes 331808 | tf_op jit(solution)/shard_map/ppermute | solution.py:118
  143.3 4.7 %collective-permute-done.39.refs_0_ = bf16[144,1152]{1,0:T(8,128)(2,1)S(1)} collective-permute-done((bf16[144,1152]{1,0:T(8,128)(2,1)S(1)}, bf16[144,1152]{1,0:T(8,128)(2,1)S(1)}, u32[]{:S(2)}, u32[]{:S(2)}) %collective-permute-start.39) | collective-permute-done | bytes 331808 | tf_op jit(solution)/shard_map/ppermute | solution.py:118
  152.9 4.4 %feed_out.1 = (f32[256,1152]{1,0:T(8,128)S(1)}, bf16[256,1152]{1,0:T(8,128)(2,1)S(1)}) custom-call(bf16[144,1152]{1,0:T(8,128)(2,1)S(1)} %bitcast_convert_fusion.refs_8_.refs_0_, bf16[144,1152]{1,0:T(8,128)(2,1)} %collective-permute-done.20.refs_9_.refs_1_, bf16[144,1152]{1,0:T(8,128)(2,1)S(1)} %collective-permute-done.28.refs_10_.refs_2_, ...), custom_call_target="tpu_custom_call" | custom-call | bytes 1024 | tf_op jit(solution)/shard_map/feed_out/pallas_call | solution.py:220
  165.3 12.1 %attention_back.1 = (bf16[1152,1152]{1,0:T(8,128)(2,1)S(1)}, f32[256,1152]{1,0:T(8,128)S(1)}, bf16[256,1152]{1,0:T(8,128)(2,1)S(1)}, bf16[144,1152]{1,0:T(8,128)(2,1)}, bf16[144,1152]{1,0:T(8,128)(2,1)}) custom-call(bf16[144,1152]{1,0:T(8,128)(2,1)S(1)} %concatenate.41.refs_0_, bf16[144,1152]{1,0:T(8,128)(2,1)S(1)} %copy-done.10, ...), custom_call_target="tpu_custom_call" | custom-call | bytes 1024 | tf_op jit(solution)/shard_map/attention_back/pallas_call | solution.py:220
  189.7 4.1 %step_fc2.1 = (f32[144,1152]{1,0:T(8,128)}, f32[144,1152]{1,0:T(8,128)}, f32[144,1152]{1,0:T(8,128)}) custom-call(s32[1]{0:T(128)} %bitcast.7.index, s32[1]{0:T(128)S(6)} %copy.50.steps, bf16[144,1152]{1,0:T(8,128)(2,1)} %copy-done.42, bf16[144,1152]{1,0:T(8,128)(2,1)} %copy-done.41, bf16[1152,1152]{1,0:T(8,128)(2,1)} %copy-done.4, f32[144,1152]{1,0:T(8,128)} %bitcast.59, ...), custom_call_target="tpu_custom_call" | custom-call | bytes 1024 | tf_op jit(solution)/shard_map/step_fc2/pallas_call | solution.py:872
  198.0 2.3 collective-permute-done.55.refs_0_
  202.4 3.2 %first_back.1 = (bf16[256,1152]{1,0:T(8,128)(2,1)}, bf16[6,2,288]{2,1,0:T(2,128)(2,1)S(1)}, bf16[6,2,288]{2,1,0:T(2,128)(2,1)S(1)}) custom-call(bf16[256,1152]{1,0:T(8,128)(2,1)} %add_convert_fusion.own, bf16[256,1152]{1,0:T(8,128)(2,1)} %collective-permute-done.52.moved, f32[256,1152]{1,0:T(8,128)S(1)} %copy-done.30, bf16[256,1152]{1,0:T(8,128)(2,1)S(1)} %copy-done.27, ...), custom_call_target="tpu_custom_call" | custom-call | bytes 1024 | tf_op jit(solution)/shard_map/first_back/pallas_call | solution.py:220
  206.9 3.7 %collective-permute-done.59.refs_0_ = bf16[144,1152]{1,0:T(8,128)(2,1)S(1)} collective-permute-done((bf16[144,1152]{1,0:T(8,128)(2,1)S(1)}, bf16[144,1152]{1,0:T(8,128)(2,1)S(1)}, u32[]{:S(2)}, u32[]{:S(2)}) %collective-permute-start.59) | collective-permute-done | bytes 331808 | tf_op jit(solution)/shard_map/ppermute | solution.py:118
  218.9 2.9 %collective-permute-done.61 = bf16[6,4,288]{2,1,0:T(4,128)(2,1)S(1)} collective-permute-done((bf16[6,4,288]{2,1,0:T(4,128)(2,1)S(1)}, bf16[6,4,288]{2,1,0:T(4,128)(2,1)S(1)}, u32[]{:S(2)}, u32[]{:S(2)}) %collective-permute-start.61) | collective-permute-done | bytes 13856 | tf_op jit(solution)/shard_map/ppermute | solution.py:56
  226.6 4.9 %place_kept.2 = bf16[4,256,1152]{2,1,0:T(8,128)(2,1)} custom-call(bf16[256,1152]{1,0:T(8,128)(2,1)} %copy-done.31, bf16[256,1152]{1,0:T(8,128)(2,1)} %copy-done.39, bf16[4,256,1152]{2,1,0:T(8,128)(2,1)} %base.2, s32[4,1,128]{2,1,0:T(1,128)} %bitcast.57), custom_call_target="tpu_custom_call" | custom-call | bytes 1024 | tf_op jit(solution)/shard_map/place_kept/pallas_call | solution.py:768
  231.5 6.2 %collective-permute-done.66 = bf16[6,16,288]{2,1,0:T(8,128)(2,1)S(1)} collective-permute-done((bf16[6,16,288]{2,1,0:T(8,128)(2,1)S(1)}, bf16[6,16,288]{2,1,0:T(8,128)(2,1)S(1)}, u32[]{:S(2)}, u32[]{:S(2)}) %collective-permute-start.66) | collective-permute-done | bytes 55328 | tf_op jit(solution)/shard_map/ppermute | solution.py:56
  240.9 5.3 %step_ada.1 = (f32[6,144,288]{2,1,0:T(8,128)}, f32[6,144,288]{2,1,0:T(8,128)}, f32[6,144,288]{2,1,0:T(8,128)}) custom-call(s32[1]{0:T(128)S(6)} %copy.50.steps, bf16[32,144]{1,0:T(8,128)(2,1)} %copy-done.33, bf16[6,32,288]{2,1,0:T(8,128)(2,1)} %copy-done.28, f32[6,144,288]{2,1,0:T(8,128)} %bitcast.54, f32[6,144,288]{2,1,0:T(8,128)} %bitcast.60, ...), custom_call_target="tpu_custom_call" | custom-call | bytes 1024 | tf_op jit(solution)/shard_map/step_ada/pallas_call | solution.py:897
  246.2 4.0 %step_fc1.1 = (f32[144,1152]{1,0:T(8,128)}, f32[144,1152]{1,0:T(8,128)}, f32[144,1152]{1,0:T(8,128)}) custom-call(s32[1]{0:T(128)} %bitcast.7.index, s32[1]{0:T(128)S(6)} %copy.50.steps, bf16[144,1152]{1,0:T(8,128)(2,1)} %copy-done.43, bf16[144,1152]{1,0:T(8,128)(2,1)} %collective-permute-done.56.refs_1_, bf16[1152,1152]{1,0:T(8,128)(2,1)} %copy-done, ...), custom_call_target="tpu_custom_call" | custom-call | bytes 1024 | tf_op jit(solution)/shard_map/step_fc1/pallas_call | solution.py:872
  250.4 4.9 %step_attention.1 = (f32[3,144,288]{2,1,0:T(8,128)}, f32[3,144,288]{2,1,0:T(8,128)}, f32[3,144,288]{2,1,0:T(8,128)}, f32[144,288]{1,0:T(8,128)}, f32[144,288]{1,0:T(8,128)}, /*index=5*/f32[144,288]{1,0:T(8,128)}) custom-call(s32[1]{0:T(128)} %bitcast.7.index, s32[1]{0:T(128)S(6)} %copy.50.steps, bf16[144,1152]{1,0:T(8,128)(2,1)} %collective-permute-done.68.refs_0_, ...), custom_call_target="tpu_custom_call" | custom-call | bytes 1024 | tf_op jit(solution)/shard_map/step_attention/pallas_call | solution.py:872
  258.8 5.3 %place_kept.3 = f32[4,256,1152]{2,1,0:T(8,128)} custom-call(bf16[256,1152]{1,0:T(8,128)(2,1)} %get-tuple-element.426.here, bf16[256,1152]{1,0:T(8,128)(2,1)} %copy-done.38, bf16[4,256,1152]{2,1,0:T(8,128)(2,1)} %base.3, s32[4,1,128]{2,1,0:T(1,128)} %bitcast.58), custom_call_target="tpu_custom_call" | custom-call | bytes 1024 | tf_op jit(solution)/shard_map/place_kept/pallas_call | solution.py:768
  (281 shorter events, 109.6 us)
Async XLA Ops:
  2.2 12.9 %collective-permute-start.3 = (bf16[144,1152]{1,0:T(8,128)(2,1)S(1)}, bf16[144,1152]{1,0:T(8,128)(2,1)S(1)}, u32[]{:S(2)}, u32[]{:S(2)}) collective-permute-start(bf16[144,1152]{1,0:T(8,128)(2,1)S(1)} %concatenate.41.refs_0_), channel_id=1, source_target_pairs={{0,8},{8,16},{16,24},{24,28},{28,20},{20,12},{12,4},{4,0},{1,9},{9... | collective-permute-start | bytes 995336 | tf_op jit(solution)/shard_map/ppermute | solution.py:118
  15.2 13.8 %collective-permute-start.6 = (bf16[144,1152]{1,0:T(8,128)(2,1)S(1)}, bf16[144,1152]{1,0:T(8,128)(2,1)S(1)}, u32[]{:S(2)}, u32[]{:S(2)}) collective-permute-start(bf16[144,1152]{1,0:T(8,128)(2,1)S(1)} %collective-permute-done.3.refs_1_), channel_id=1, source_target_pairs={{0,8},{8,16},{16,24},{24,28},{28,20},{20,12},{12,4},{4,0},{1,9},{9... | collective-permute-start | bytes 995336 | tf_op jit(solution)/shard_map/ppermute | solution.py:118
  17.1 11.9 %collective-permute-start.7 = (bf16[144,1152]{1,0:T(8,128)(2,1)S(1)}, bf16[144,1152]{1,0:T(8,128)(2,1)S(1)}, u32[]{:S(2)}, u32[]{:S(2)}) collective-permute-start(bf16[144,1152]{1,0:T(8,128)(2,1)S(1)} %collective-permute-done.4.refs_5_), channel_id=1, source_target_pairs={{8,0},{16,8},{24,16},{28,24},{20,28},{12,20},{4,12},{0,4},{9,1},{1... | collective-permute-start | bytes 995336 | tf_op jit(solution)/shard_map/ppermute | solution.py:118
  17.2 11.7 %collective-permute-start.5 = (bf16[16,8,144]{2,0,1:T(8,128)(2,1)S(1)}, bf16[16,8,144]{2,0,1:T(8,128)(2,1)S(1)}, u32[]{:S(2)}, u32[]{:S(2)}) collective-permute-start(bf16[16,8,144]{2,0,1:T(8,128)(2,1)S(1)} %pad_maximum_fusion.3), channel_id=1, source_target_pairs={{0,16},{4,20},{8,24},{12,28},{16,0},{20,4},{24,8},{28,12},{1,17},{... | collective-permute-start | bytes 110600 | tf_op jit(solution)/shard_map/ppermute | solution.py:56
  30.5 12.1 %collective-permute-start.9 = (bf16[144,1152]{1,0:T(8,128)(2,1)S(1)}, bf16[144,1152]{1,0:T(8,128)(2,1)S(1)}, u32[]{:S(2)}, u32[]{:S(2)}) collective-permute-start(bf16[144,1152]{1,0:T(8,128)(2,1)S(1)} %collective-permute-done.6.refs_2_), channel_id=1, source_target_pairs={{0,8},{8,16},{16,24},{24,28},{28,20},{20,12},{12,4},{4,0},{1,9},{9... | collective-permute-start | bytes 995336 | tf_op jit(solution)/shard_map/ppermute | solution.py:118
  42.6 11.4 %collective-permute-start.14 = (bf16[144,1152]{1,0:T(8,128)(2,1)S(1)}, bf16[144,1152]{1,0:T(8,128)(2,1)S(1)}, u32[]{:S(2)}, u32[]{:S(2)}) collective-permute-start(bf16[144,1152]{1,0:T(8,128)(2,1)S(1)} %collective-permute-done.9.refs_3_), channel_id=1, source_target_pairs={{0,8},{8,16},{16,24},{24,28},{28,20},{20,12},{12,4},{4,0},{1,9},{9... | collective-permute-start | bytes 995336 | tf_op jit(solution)/shard_map/ppermute | solution.py:118
  46.5 13.9 %collective-permute-start.18 = (bf16[144,1152]{1,0:T(8,128)(2,1)S(1)}, bf16[144,1152]{1,0:T(8,128)(2,1)}, u32[]{:S(2)}, u32[]{:S(2)}) collective-permute-start(bf16[144,1152]{1,0:T(8,128)(2,1)S(1)} %convert_element_type.37.refs_0_), channel_id=1, source_target_pairs={{0,8},{8,16},{16,24},{24,28},{28,20},{20,12},{12,4},{4,0},{1,9},{9... | collective-permute-start | bytes 995336 | tf_op jit(solution)/shard_map/ppermute | solution.py:118
  54.1 15.0 %collective-permute-start.20 = (bf16[144,1152]{1,0:T(8,128)(2,1)S(1)}, bf16[144,1152]{1,0:T(8,128)(2,1)}, u32[]{:S(2)}, u32[]{:S(2)}) collective-permute-start(bf16[144,1152]{1,0:T(8,128)(2,1)S(1)} %bitcast_convert_fusion.refs_8_.refs_0_), channel_id=1, source_target_pairs={{8,0},{16,8},{24,16},{28,24},{20,28},{12,20},{4,12},{0,4},{9,1},{1... | collective-permute-start | bytes 995336 | tf_op jit(solution)/shard_map/ppermute | solution.py:118
  58.2 10.9 %collective-permute-start.21 = (bf16[144,1152]{1,0:T(8,128)(2,1)S(1)}, bf16[144,1152]{1,0:T(8,128)(2,1)S(1)}, u32[]{:S(2)}, u32[]{:S(2)}) collective-permute-start(bf16[144,1152]{1,0:T(8,128)(2,1)S(1)} %bitcast_convert_fusion.refs_8_.refs_0_), channel_id=1, source_target_pairs={{0,8},{8,16},{16,24},{24,28},{28,20},{20,12},{12,4},{4,0},{1,9},{9... | collective-permute-start | bytes 995336 | tf_op jit(solution)/shard_map/ppermute | solution.py:118
  62.2 13.0 %collective-permute-start.22 = (bf16[144,1152]{1,0:T(8,128)(2,1)}, bf16[144,1152]{1,0:T(8,128)(2,1)S(1)}, u32[]{:S(2)}, u32[]{:S(2)}) collective-permute-start(bf16[144,1152]{1,0:T(8,128)(2,1)} %collective-permute-done.18.refs_1_), channel_id=1, source_target_pairs={{0,8},{8,16},{16,24},{24,28},{28,20},{20,12},{12,4},{4,0},{1,9},{9... | collective-permute-start | bytes 995336 | tf_op jit(solution)/shard_map/ppermute | solution.py:118
  62.2 13.0 %collective-permute-start.23 = (bf16[144,1152]{1,0:T(8,128)(2,1)}, bf16[144,1152]{1,0:T(8,128)(2,1)S(1)}, u32[]{:S(2)}, u32[]{:S(2)}) collective-permute-start(bf16[144,1152]{1,0:T(8,128)(2,1)} %collective-permute-done.19.refs_5_), channel_id=1, source_target_pairs={{8,0},{16,8},{24,16},{28,24},{20,28},{12,20},{4,12},{0,4},{9,1},{1... | collective-permute-start | bytes 995336 | tf_op jit(solution)/shard_map/ppermute | solution.py:118
  77.5 19.9 %collective-permute-start.25 = (bf16[256,1152]{1,0:T(8,128)(2,1)S(1)}, bf16[256,1152]{1,0:T(8,128)(2,1)S(1)}, u32[]{:S(2)}, u32[]{:S(2)}) collective-permute-start(bf16[256,1152]{1,0:T(8,128)(2,1)S(1)} %add_convert_fusion.3.own.attn_own), channel_id=1, source_target_pairs={{0,2},{1,3},{2,0},{3,1},{4,6},{5,7},{6,4},{7,5},{8,10},{9,11},{10,... | collective-permute-start | bytes 1769480 | tf_op jit(solution)/shard_map/ppermute | solution.py:39
  79.2 10.9 %collective-permute-start.28 = (bf16[144,1152]{1,0:T(8,128)(2,1)}, bf16[144,1152]{1,0:T(8,128)(2,1)S(1)}, u32[]{:S(2)}, u32[]{:S(2)}) collective-permute-start(bf16[144,1152]{1,0:T(8,128)(2,1)} %collective-permute-done.20.refs_9_.refs_1_), channel_id=1, source_target_pairs={{8,0},{16,8},{24,16},{28,24},{20,28},{12,20},{4,12},{0,4},{9,1},{1... | collective-permute-start | bytes 995336 | tf_op jit(solution)/shard_map/ppermute | solution.py:118
  81.2 16.1 %collective-permute-start.26 = (bf16[144,1152]{1,0:T(8,128)(2,1)S(1)}, bf16[144,1152]{1,0:T(8,128)(2,1)S(1)}, u32[]{:S(2)}, u32[]{:S(2)}) collective-permute-start(bf16[144,1152]{1,0:T(8,128)(2,1)S(1)} %collective-permute-done.22.refs_2_), channel_id=1, source_target_pairs={{0,8},{8,16},{16,24},{24,28},{28,20},{20,12},{12,4},{4,0},{1,9},{9... | collective-permute-start | bytes 995336 | tf_op jit(solution)/shard_map/ppermute | solution.py:118
  83.1 14.2 %collective-permute-start.27 = (bf16[144,1152]{1,0:T(8,128)(2,1)S(1)}, bf16[144,1152]{1,0:T(8,128)(2,1)S(1)}, u32[]{:S(2)}, u32[]{:S(2)}) collective-permute-start(bf16[144,1152]{1,0:T(8,128)(2,1)S(1)} %collective-permute-done.23.refs_6_), channel_id=1, source_target_pairs={{8,0},{16,8},{24,16},{28,24},{20,28},{12,20},{4,12},{0,4},{9,1},{1... | collective-permute-start | bytes 995336 | tf_op jit(solution)/shard_map/ppermute | solution.py:118
  130.2 18.3 %collective-permute-start.38 = (bf16[256,1152]{1,0:T(8,128)(2,1)S(1)}, bf16[256,1152]{1,0:T(8,128)(2,1)S(1)}, u32[]{:S(2)}, u32[]{:S(2)}) collective-permute-start(bf16[256,1152]{1,0:T(8,128)(2,1)S(1)} %add_convert_fusion.2.own), channel_id=1, source_target_pairs={{0,2},{1,3},{2,0},{3,1},{4,6},{5,7},{6,4},{7,5},{8,10},{9,11},{10,... | collective-permute-start | bytes 1769480 | tf_op jit(solution)/shard_map/ppermute | solution.py:39
  137.2 10.7 %collective-permute-start.39 = (bf16[144,1152]{1,0:T(8,128)(2,1)S(1)}, bf16[144,1152]{1,0:T(8,128)(2,1)S(1)}, u32[]{:S(2)}, u32[]{:S(2)}) collective-permute-start(bf16[144,1152]{1,0:T(8,128)(2,1)S(1)} %get-tuple-element.295), channel_id=1, source_target_pairs={{8,0},{16,8},{24,16},{28,24},{20,28},{12,20},{4,12},{0,4},{9,1},{1... | collective-permute-start | bytes 995336 | tf_op jit(solution)/shard_map/ppermute | solution.py:118
  160.7 18.3 %collective-permute-start.47 = (bf16[256,1152]{1,0:T(8,128)(2,1)S(1)}, bf16[256,1152]{1,0:T(8,128)(2,1)S(1)}, u32[]{:S(2)}, u32[]{:S(2)}) collective-permute-start(bf16[256,1152]{1,0:T(8,128)(2,1)S(1)} %add_convert_fusion.1.own), channel_id=1, source_target_pairs={{0,2},{1,3},{2,0},{3,1},{4,6},{5,7},{6,4},{7,5},{8,10},{9,11},{10,... | collective-permute-start | bytes 1769480 | tf_op jit(solution)/shard_map/ppermute | solution.py:39
  162.2 16.7 %collective-permute-start.48 = (bf16[144,1152]{1,0:T(8,128)(2,1)S(1)}, bf16[144,1152]{1,0:T(8,128)(2,1)S(1)}, u32[]{:S(2)}, u32[]{:S(2)}) collective-permute-start(bf16[144,1152]{1,0:T(8,128)(2,1)S(1)} %get-tuple-element.340), channel_id=1, source_target_pairs={{8,0},{16,8},{24,16},{28,24},{20,28},{12,20},{4,12},{0,4},{9,1},{1... | collective-permute-start | bytes 995336 | tf_op jit(solution)/shard_map/ppermute | solution.py:118
  163.3 15.7 %collective-permute-start.49 = (bf16[144,1152]{1,0:T(8,128)(2,1)S(1)}, bf16[144,1152]{1,0:T(8,128)(2,1)S(1)}, u32[]{:S(2)}, u32[]{:S(2)}) collective-permute-start(bf16[144,1152]{1,0:T(8,128)(2,1)S(1)} %get-tuple-element.341), channel_id=1, source_target_pairs={{0,8},{8,16},{16,24},{24,28},{28,20},{20,12},{12,4},{4,0},{1,9},{9... | collective-permute-start | bytes 995336 | tf_op jit(solution)/shard_map/ppermute | solution.py:118
  164.2 14.7 %collective-permute-start.50 = (bf16[144,1152]{1,0:T(8,128)(2,1)S(1)}, bf16[144,1152]{1,0:T(8,128)(2,1)S(1)}, u32[]{:S(2)}, u32[]{:S(2)}) collective-permute-start(bf16[144,1152]{1,0:T(8,128)(2,1)S(1)} %add_blocks.12), channel_id=1, source_target_pairs={{8,0},{16,8},{24,16},{28,24},{20,28},{12,20},{4,12},{0,4},{9,1},{1... | collective-permute-start | bytes 995336 | tf_op jit(solution)/shard_map/ppermute | solution.py:118
  182.0 18.3 %collective-permute-start.52 = (bf16[256,1152]{1,0:T(8,128)(2,1)}, bf16[256,1152]{1,0:T(8,128)(2,1)}, u32[]{:S(2)}, u32[]{:S(2)}) collective-permute-start(bf16[256,1152]{1,0:T(8,128)(2,1)} %add_convert_fusion.own), channel_id=1, source_target_pairs={{0,2},{1,3},{2,0},{3,1},{4,6},{5,7},{6,4},{7,5},{8,10},{9,11},{10,... | collective-permute-start | bytes 1769480 | tf_op jit(solution)/shard_map/ppermute | solution.py:39
  182.5 11.3 %collective-permute-start.53 = (bf16[144,1152]{1,0:T(8,128)(2,1)}, bf16[144,1152]{1,0:T(8,128)(2,1)}, u32[]{:S(2)}, u32[]{:S(2)}) collective-permute-start(bf16[144,1152]{1,0:T(8,128)(2,1)} %get-tuple-element.362), channel_id=1, source_target_pairs={{0,8},{8,16},{16,24},{24,28},{28,20},{20,12},{12,4},{4,0},{1,9},{9... | collective-permute-start | bytes 995336 | tf_op jit(solution)/shard_map/ppermute | solution.py:118
  183.6 11.0 %collective-permute-start.54 = (bf16[144,1152]{1,0:T(8,128)(2,1)}, bf16[144,1152]{1,0:T(8,128)(2,1)}, u32[]{:S(2)}, u32[]{:S(2)}) collective-permute-start(bf16[144,1152]{1,0:T(8,128)(2,1)} %get-tuple-element.363), channel_id=1, source_target_pairs={{8,0},{16,8},{24,16},{28,24},{20,28},{12,20},{4,12},{0,4},{9,1},{1... | collective-permute-start | bytes 995336 | tf_op jit(solution)/shard_map/ppermute | solution.py:118
  185.8 14.5 %collective-permute-start.55 = (bf16[144,1152]{1,0:T(8,128)(2,1)}, bf16[144,1152]{1,0:T(8,128)(2,1)}, u32[]{:S(2)}, u32[]{:S(2)}) collective-permute-start(bf16[144,1152]{1,0:T(8,128)(2,1)} %get-tuple-element.368), channel_id=1, source_target_pairs={{8,0},{16,8},{24,16},{28,24},{20,28},{12,20},{4,12},{0,4},{9,1},{1... | collective-permute-start | bytes 995336 | tf_op jit(solution)/shard_map/ppermute | solution.py:118
  186.8 13.5 %collective-permute-start.56 = (bf16[144,1152]{1,0:T(8,128)(2,1)}, bf16[144,1152]{1,0:T(8,128)(2,1)}, u32[]{:S(2)}, u32[]{:S(2)}) collective-permute-start(bf16[144,1152]{1,0:T(8,128)(2,1)} %get-tuple-element.369), channel_id=1, source_target_pairs={{0,8},{8,16},{16,24},{24,28},{28,20},{20,12},{12,4},{4,0},{1,9},{9... | collective-permute-start | bytes 995336 | tf_op jit(solution)/shard_map/ppermute | solution.py:118
  200.3 11.1 %collective-permute-start.58 = (bf16[256,1152]{1,0:T(8,128)(2,1)S(1)}, bf16[256,1152]{1,0:T(8,128)(2,1)S(1)}, u32[]{:S(2)}, u32[]{:S(2)}) collective-permute-start(bf16[256,1152]{1,0:T(8,128)(2,1)S(1)} %copy-done.32), channel_id=1, source_target_pairs={{0,1},{1,0},{2,3},{3,2},{4,5},{5,4},{6,7},{7,6},{8,9},{9,8},{10,11... | collective-permute-start | bytes 1769480 | tf_op jit(solution)/shard_map/ppermute | solution.py:35
  222.5 15.3 %collective-permute-start.67 = (bf16[256,1152]{1,0:T(8,128)(2,1)}, bf16[256,1152]{1,0:T(8,128)(2,1)S(1)}, u32[]{:S(2)}, u32[]{:S(2)}) collective-permute-start(bf16[256,1152]{1,0:T(8,128)(2,1)} %get-tuple-element.426.here), channel_id=1, source_target_pairs={{0,1},{1,0},{2,3},{3,2},{4,5},{5,4},{6,7},{7,6},{8,9},{9,8},{10,11... | collective-permute-start | bytes 1769480 | tf_op jit(solution)/shard_map/ppermute | solution.py:35
  223.2 14.5 %collective-permute-start.68 = (bf16[144,1152]{1,0:T(8,128)(2,1)S(1)}, bf16[144,1152]{1,0:T(8,128)(2,1)}, u32[]{:S(2)}, u32[]{:S(2)}) collective-permute-start(bf16[144,1152]{1,0:T(8,128)(2,1)S(1)} %add_blocks.17), channel_id=1, source_target_pairs={{0,8},{8,16},{16,24},{24,28},{28,20},{20,12},{12,4},{4,0},{1,9},{9... | collective-permute-start | bytes 995336 | tf_op jit(solution)/shard_map/ppermute | solution.py:118
  225.0 12.8 %collective-permute-start.69 = (bf16[144,1152]{1,0:T(8,128)(2,1)S(1)}, bf16[144,1152]{1,0:T(8,128)(2,1)S(1)}, u32[]{:S(2)}, u32[]{:S(2)}) collective-permute-start(bf16[144,1152]{1,0:T(8,128)(2,1)S(1)} %add_blocks.15), channel_id=1, source_target_pairs={{8,0},{16,8},{24,16},{28,24},{20,28},{12,20},{4,12},{0,4},{9,1},{1... | collective-permute-start | bytes 995336 | tf_op jit(solution)/shard_map/ppermute | solution.py:118
  225.2 12.5 %collective-permute-start.66 = (bf16[6,16,288]{2,1,0:T(8,128)(2,1)S(1)}, bf16[6,16,288]{2,1,0:T(8,128)(2,1)S(1)}, u32[]{:S(2)}, u32[]{:S(2)}) collective-permute-start(bf16[6,16,288]{2,1,0:T(8,128)(2,1)S(1)} %pad_maximum_fusion.2), channel_id=1, source_target_pairs={{0,16},{4,20},{8,24},{12,28},{16,0},{20,4},{24,8},{28,12},{1,17},{... | collective-permute-start | bytes 165896 | tf_op jit(solution)/shard_map/ppermute | solution.py:56
  239.4 10.8 %collective-permute-start.71 = (f32[32,144]{1,0:T(8,128)S(1)}, f32[32,144]{1,0:T(8,128)S(1)}, u32[]{:S(2)}, u32[]{:S(2)}) collective-permute-start(f32[32,144]{1,0:T(8,128)S(1)} %add.56), channel_id=1, source_target_pairs={{0,2},{1,3},{2,0},{3,1},{4,6},{5,7},{6,4},{7,5},{8,10},{9,11},{10,... | collective-permute-start | bytes 55304 | tf_op jit(solution)/shard_map/ppermute | solution.py:39
  (89 other events, 948.5 us)

commit v2 on v1

--- a/solution.py
+++ b/solution.py
@@ -485,7 +485,7 @@
         )
         return carry
 
-    lax.fori_loop(0, total // rows, attend, 0)
+    lax.fori_loop(0, total // rows, attend, 0, unroll=True)
     leaving = [copies.start(attended, outs[0])]
     wait(placed)
     weights = full[:, 3 * local - start :]
@@ -731,7 +731,7 @@
         grads[at, :] = jnp.concatenate(parts, 1)
         return carry
 
-    lax.fori_loop(0, total // rows, image_back, 0)
+    lax.fori_loop(0, total // rows, image_back, 0, unroll=True)
     weights = full[:, : 3 * local]
     other[...] = dot_last(grads[pair_rows(total, 1 - core), :], weights).astype(bf16)
     leaving = [copies.start(other, outs[2])]
@@ -771,6 +771,7 @@
         out_shape=jax.ShapeDtypeStruct(base.shape, dtype),
         in_specs=[whole, whole, spec, pl.BlockSpec((1, 1, count), lambda i: (i, 0, 0))],
         out_specs=spec,
+        compiler_params=pltpu.CompilerParams(vmem_limit_bytes=14 << 20),
         cost_estimate=pl.CostEstimate(flops=0, bytes_accessed=1024, transcendentals=0),
         name="place_kept",
     )(here, there, base, index.reshape(images, 1, count))
@@ -857,7 +858,7 @@
         ref[...] = value
 
 
-def step_weights(kernel, name, state, given, rate, steps):
+def step_weights(kernel, name, state, given, rate, steps, limit=None):
     rows = given[0].shape[0]
     block = 48 if rows % 48 == 0 else rows
     count = rows // block
@@ -878,6 +879,7 @@
             out_specs=[spec(x) for x in state],
         ),
         out_shape=[jax.ShapeDtypeStruct(x.shape, f32) for x in state],
+        compiler_params=pltpu.CompilerParams(vmem_limit_bytes=limit),
         cost_estimate=pl.CostEstimate(flops=0, bytes_accessed=1024, transcendentals=0),
         name=name,
     )(lax.axis_index("dp").astype(jnp.int32).reshape(1), steps, *given, *state)
@@ -1238,7 +1240,7 @@
     def attention_back_sums():
         given = fc2_sums.given() if ring else (scatter_plain(fc2_grad),)
         state = (fc2_weight.T, fc2_moment.T, fc2_average.T)
-        new = step_weights(one_step, "step_fc2", state, given, rate, step_count)
+        new = step_weights(one_step, "step_fc2", state, given, rate, step_count, 12 << 20)
         return swap_x(back_own), *output(), *new
 
     if ring:
@@ -1266,61 +1268,61 @@
                 last_mods,
             ),
         )
-        return kept, join_pair(mine, swap_core(partner), core, 1), swap_core(kept_out)
-
-    kept_grad, small, kept_there = tick(first_back, (attn_sums, "ab"))
-
-    def first_spread():
+        values = spread_round(join_pair(mine, swap_core(partner), core, 1), 1, 0)
+        return kept, values, kept_out
+
+    kept_grad, small, kept_out = tick(first_back, (attn_sums, "ab"))
+
+    def last_spread():
         sums = fc1_sums.prepare("a") if ring else ()
-        return spread_round(small, 1, 0), kept_there, kept_grad, *sums
-
-    small, kept_there, kept_grad, *sums = tick(first_spread, (attn_sums, "ab"))
-    if ring:
-        fc1_sums.finish("a", sums)
-
-    def last_spread():
         values = small
         for level in range(1, levels):
             values = spread_round(values, 1, level)
-        out = place_kept(kept_out, kept_there, tokens, kept_index, bf16)
-        return values, kept_grad, swap_core(kept_grad), out
-
-    mod_grad_all, kept_grad, grad_there, block_out = tick(
-        last_spread, (attn_sums, "a"), (fc1_sums, "a")
-    )
-
-    def silu_first():
+        there = swap_core(kept_grad), swap_core(kept_out)
+        return values, kept_grad, kept_out, *there, *sums
+
+    mod_grad_all, kept_grad, kept_out, grad_there, kept_there, *sums = tick(
+        last_spread, (attn_sums, "ab")
+    )
+    if ring:
+        fc1_sums.finish("a", sums)
+
+    def silu_sums():
         (part,) = run(
             kernel_silu, "silu", [((dp_size * images, own_d), f32)], (mod_grad_all, ada_state[0])
         )
-        return part + swap_core(part), mod_grad_all, kept_grad
-
-    silu_part, mod_grad_all, kept_grad = tick(silu_first)
-
-    def silu_second():
-        given = fc1_sums.given() if ring else (scatter_plain(fc1_grad),)
-        state = (fc1_weight, fc1_moment, fc1_average)
-        new = step_weights(one_step, "step_fc1", state, given, rate, step_count)
-        new += step_ada(*ada_state, cond_own, mod_grad_all, rate, step_count)
-        return silu_part + swap_x(silu_part), *new
-
-    silu_part, fc1_master, fc1_momentum, fc1_ema, *ada_new = tick(silu_second)
-    silu_blocks = silu_part.reshape(dp_size, images, own_d)
-
-    def silu_third():
-        blocks = silu_blocks
-        for level in reversed(range(1, levels)):
-            blocks = turn_round(blocks, level)
+        grads = place_kept(kept_grad, grad_there, cotangent, kept_index, f32)
+        out = place_kept(kept_out, kept_there, tokens, kept_index, bf16)
+        return part + swap_core(part), grads, out, mod_grad_all
+
+    silu_part, tokens_grad, block_out, mod_grad_all = tick(
+        silu_sums, (attn_sums, "a"), (fc1_sums, "a")
+    )
+
+    def step_beside_x():
         given = attn_sums.given() if ring else (scatter_plain(attn_grad),)
         state = (qkv_weight, qkv_moment, qkv_average)
         state += (proj_weight.T, proj_moment.T, proj_average.T)
         new = step_weights(attention_step, "step_attention", state, given, rate, step_count)
-        return blocks, kept_grad, *new
-
-    silu_blocks, kept_grad, *attn_new = tick(silu_third)
+        return silu_part + swap_x(silu_part), mod_grad_all, *new
+
+    silu_part, mod_grad_all, *attn_new = tick(step_beside_x)
+    silu_blocks = silu_part.reshape(dp_size, images, own_d)
+
+    def step_beside_turn():
+        blocks = silu_blocks
+        for level in reversed(range(1, levels)):
+            blocks = turn_round(blocks, level)
+        return blocks, *step_ada(*ada_state, cond_own, mod_grad_all, rate, step_count)
+
+    silu_blocks, *ada_new = tick(step_beside_turn)
+    silu_blocks = in_order(turn_round(silu_blocks, 0))
+    given = fc1_sums.given() if ring else (scatter_plain(fc1_grad),)
+    state = (fc1_weight, fc1_moment, fc1_average)
+    fc1_master, fc1_momentum, fc1_ema = step_weights(
+        one_step, "step_fc1", state, given, rate, step_count
+    )
     qkv_master, qkv_momentum, qkv_ema, proj_master, proj_momentum, proj_ema = attn_new
-    tokens_grad = place_kept(kept_grad, grad_there, cotangent, kept_index, f32)
-    silu_blocks = in_order(turn_round(silu_blocks, 0))
     ada_master, ada_momentum, ada_ema = [jnp.moveaxis(x, 0, 1) for x in ada_new]
     silu_grad = jnp.moveaxis(silu_blocks, 0, 1).reshape(images, width)
     silu_value, silu_pull = jax.vjp(jax.nn.silu, cond_float)

time: 266 us -> 256 us (0.962)
  Pallas kernels: 89.3 us -> 75.7 us
  waiting for transfers between devices: 86.2 us -> 93.8 us
  local copies, waits for them, and re-layouts: 12.3 us -> 7.99 us
    ppermute x42, waiting for transfers between devices: 43.4 us -> 48.1 us  [hop(): return lax.ppermute(values, 'dp', clockwise if direction > 0 else backward)]
    pallas_call x2, Pallas kernels: 10.2 us -> 5.69 us  [place_kept(): pl.pallas_call(kernel_place, grid=(images,), out_shape=jax.ShapeDtypeStru...]
    unnamed x91 -> x79, local copies, waits for them, and re-layouts: 11.6 us -> 7.26 us
    ppermute x16, waiting for transfers between devices: 31 us -> 35 us  [swap_dp(): return lax.ppermute(values, 'dp', [(i, i ^ bit) for i in range(size)])]
    pallas_call x15, Pallas kernels: 54.6 us -> 50.8 us  [run(): pl.pallas_call(kernel, out_shape=[jax.ShapeDtypeStruct(shape, dtype) for...]
    pallas_call x9, Pallas kernels: 6.27 us -> 3.25 us  [add_blocks(): pl.pallas_call(partial(kernel_add, distances), out_shape=[jax.ShapeDtypeS...]
  transfers between devices with their start and end apart: 76 -> 76, of which waited for: 33 -> 36; matrix products, arithmetic and copies ran while one was open for 0% -> 0% of each run, Pallas kernels for 33% -> 29%
where the time goes in v2:
time: 256 us; the launch traced here: 255 us
  waiting for transfers between devices  93.8 us (37%)
  Pallas kernels  75.7 us (30%)
  starting transfers between devices  72.2 us (28%)
  local copies, waits for them, and re-layouts  7.99 us (3%)
  other arithmetic  3.03 us (1%)
    pallas_call x15, Pallas kernels, run(): pl.pallas_call(kernel, out_shape=[jax.ShapeDtypeStruct(shape, dtype) for...  50.8 us
    ppermute x42, waiting for transfers between devices, hop(): return lax.ppermute(values, 'dp', clockwise if direction > 0 else backward)  48.1 us
    ppermute x42, starting transfers between devices, hop(): return lax.ppermute(values, 'dp', clockwise if direction > 0 else backward)  43 us
    ppermute x16, waiting for transfers between devices, swap_dp(): return lax.ppermute(values, 'dp', [(i, i ^ bit) for i in range(size)])  35 us
    ppermute x16, starting transfers between devices, swap_dp(): return lax.ppermute(values, 'dp', [(i, i ^ bit) for i in range(size)])  19.5 us
    pallas_call x3, Pallas kernels, step_weights(): pl.pallas_call(partial(kernel, rate, len(given)), grid_spec=pltpu.Prefetc...  10.7 us
    ppermute x11, waiting for transfers between devices, swap_core(): return lax.ppermute(values, 'mp', [(j, j ^ 1) for j in range(4)])  9.09 us
    ppermute x6, starting transfers between devices, swap_x(): return lax.ppermute(values, 'mp', [(j, j ^ 2) for j in range(4)])  7.51 us
  transfers between devices with their start and end apart: 76, of which 36 were waited for; matrix products, arithmetic and copies ran while one was open for 0% of the time, Pallas kernels for 29%

profile of v2, /device:TPU:0, one launch (start us, length us, event | category | flops | bytes accessed | tf_op | source)
XLA Modules:
  0.0 255.2 jit_solution(11850322541380515658)
XLA Ops:
  2.2 3.1 %collective-permute-start.3 = (bf16[144,1152]{1,0:T(8,128)(2,1)S(1)}, bf16[144,1152]{1,0:T(8,128)(2,1)S(1)}, u32[]{:S(2)}, u32[]{:S(2)}) collective-permute-start(bf16[144,1152]{1,0:T(8,128)(2,1)S(1)} %concatenate.41.refs_0_), channel_id=1, source_target_pairs={{0,8},{8,16},{16,24},{24,28},{28,20},{20,12},{12,4},{4,0},{1,9},{9... | collective-permute-start | bytes 995336 | tf_op jit(solution)/shard_map/ppermute | solution.py:118
  5.4 2.0 collective-permute-start
  10.7 2.1 first_norm.1
  17.2 2.9 %collective-permute-start.5 = (bf16[16,8,144]{2,0,1:T(8,128)(2,1)S(1)}, bf16[16,8,144]{2,0,1:T(8,128)(2,1)S(1)}, u32[]{:S(2)}, u32[]{:S(2)}) collective-permute-start(bf16[16,8,144]{2,0,1:T(8,128)(2,1)S(1)} %pad_maximum_fusion.3), channel_id=1, source_target_pairs={{0,16},{4,20},{8,24},{12,28},{16,0},{20,4},{24,8},{28,12},{1,17},{... | collective-permute-start | bytes 110600 | tf_op jit(solution)/shard_map/ppermute | solution.py:56
  20.2 8.8 %collective-permute-done.5 = bf16[16,8,144]{2,0,1:T(8,128)(2,1)S(1)} collective-permute-done((bf16[16,8,144]{2,0,1:T(8,128)(2,1)S(1)}, bf16[16,8,144]{2,0,1:T(8,128)(2,1)S(1)}, u32[]{:S(2)}, u32[]{:S(2)}) %collective-permute-start.5) | collective-permute-done | bytes 36896 | tf_op jit(solution)/shard_map/ppermute | solution.py:56
  30.5 2.1 collective-permute-start.9
  32.6 6.0 %collective-permute-done.8 = f32[6,16,288]{2,1,0:T(8,128)S(1)} collective-permute-done((f32[6,16,288]{2,1,0:T(8,128)S(1)}, f32[6,16,288]{2,1,0:T(8,128)S(1)}, u32[]{:S(2)}, u32[]{:S(2)}) %collective-permute-start.8) | collective-permute-done | bytes 110624 | tf_op jit(solution)/shard_map/ppermute | solution.py:56
  39.2 3.3 %collective-permute-done.9.refs_3_ = bf16[144,1152]{1,0:T(8,128)(2,1)S(1)} collective-permute-done((bf16[144,1152]{1,0:T(8,128)(2,1)S(1)}, bf16[144,1152]{1,0:T(8,128)(2,1)S(1)}, u32[]{:S(2)}, u32[]{:S(2)}) %collective-permute-start.9) | collective-permute-done | bytes 331808 | tf_op jit(solution)/shard_map/ppermute | solution.py:118
  47.4 5.2 %collective-permute-done.11 = f32[6,4,288]{2,1,0:T(4,128)S(1)} collective-permute-done((f32[6,4,288]{2,1,0:T(4,128)S(1)}, f32[6,4,288]{2,1,0:T(4,128)S(1)}, u32[]{:S(2)}, u32[]{:S(2)}) %collective-permute-start.11) | collective-permute-done | bytes 27680 | tf_op jit(solution)/shard_map/ppermute | solution.py:56
  62.2 2.0 collective-permute-start.23
  65.9 3.2 %project.1 = (bf16[512,1152]{1,0:T(8,128)(2,1)S(1)}, bf16[512,864]{1,0:T(8,128)(2,1)S(1)}) custom-call(bf16[144,1152]{1,0:T(8,128)(2,1)S(1)} %concatenate.41.refs_0_, bf16[144,1152]{1,0:T(8,128)(2,1)S(1)} %collective-permute-done.3.refs_1_, bf16[144,1152]{1,0:T(8,128)(2,1)S(1)} %collective-permute-done.6.refs_2_, ...), custom_call_target="tpu_custom_call" | custom-call | bytes 1024 | tf_op jit(solution)/shard_map/project/pallas_call | solution.py:220
  69.2 5.6 %attend.1 = (bf16[512,288]{1,0:T(8,128)(2,1)S(1)}, f32[256,1152]{1,0:T(8,128)S(1)}, bf16[256,1152]{1,0:T(8,128)(2,1)S(1)}) custom-call(bf16[144,1152]{1,0:T(8,128)(2,1)S(1)} %concatenate.41.refs_0_, bf16[144,1152]{1,0:T(8,128)(2,1)S(1)} %collective-permute-done.3.refs_1_, bf16[144,1152]{1,0:T(8,128)(2,1)S(1)} %collective-permute-done.6.refs_2_, ...), custom_call_target="tpu_custom_call" | custom-call | bytes 1024 | tf_op jit(solution)/shard_map/attend/pallas_call | solution.py:220
  83.4 6.3 %collective-permute-done.28.refs_10_.refs_2_ = bf16[144,1152]{1,0:T(8,128)(2,1)S(1)} collective-permute-done((bf16[144,1152]{1,0:T(8,128)(2,1)}, bf16[144,1152]{1,0:T(8,128)(2,1)S(1)}, u32[]{:S(2)}, u32[]{:S(2)}) %collective-permute-start.28) | collective-permute-done | bytes 331808 | tf_op jit(solution)/shard_map/ppermute | solution.py:118
  91.3 5.7 %collective-permute-done.26.refs_3_ = bf16[144,1152]{1,0:T(8,128)(2,1)S(1)} collective-permute-done((bf16[144,1152]{1,0:T(8,128)(2,1)S(1)}, bf16[144,1152]{1,0:T(8,128)(2,1)S(1)}, u32[]{:S(2)}, u32[]{:S(2)}) %collective-permute-start.26) | collective-permute-done | bytes 331808 | tf_op jit(solution)/shard_map/ppermute | solution.py:118
  99.6 5.8 %collective-permute-done.30.refs_4_ = bf16[144,1152]{1,0:T(8,128)(2,1)S(1)} collective-permute-done((bf16[144,1152]{1,0:T(8,128)(2,1)S(1)}, bf16[144,1152]{1,0:T(8,128)(2,1)S(1)}, u32[]{:S(2)}, u32[]{:S(2)}) %collective-permute-start.30) | collective-permute-done | bytes 331808 | tf_op jit(solution)/shard_map/ppermute | solution.py:118
  108.1 7.8 %feed_forward.1 = (f32[512,1152]{1,0:T(8,128)S(1)}, bf16[512,1152]{1,0:T(8,128)(2,1)S(1)}, bf16[1152,1152]{1,0:T(8,128)(2,1)S(1)}, bf16[144,1152]{1,0:T(8,128)(2,1)S(1)}, bf16[144,1152]{1,0:T(8,128)(2,1)S(1)}) custom-call(bf16[144,1152]{1,0:T(8,128)(2,1)S(1)} %convert_element_type.37.refs_0_, bf16[144,1152]{1,0:T(8,128)(2,1)} %collective-permute-done.18.refs_1_, ...), custom_call_target="tpu_custom_call" | custom-call | bytes 1024 | tf_op jit(solution)/shard_map/feed_forward/pallas_call | solution.py:220
  119.2 8.4 %feed_back.1 = (bf16[512,1152]{1,0:T(8,128)(2,1)S(1)}, f32[256,1152]{1,0:T(8,128)S(1)}, bf16[256,1152]{1,0:T(8,128)(2,1)S(1)}) custom-call(bf16[144,1152]{1,0:T(8,128)(2,1)S(1)} %convert_element_type.37.refs_0_, bf16[144,1152]{1,0:T(8,128)(2,1)} %collective-permute-done.18.refs_1_, bf16[144,1152]{1,0:T(8,128)(2,1)S(1)} %collective-permute-done.22.refs_2_, ...), custom_call_target="tpu_custom_call" | custom-call | bytes 1024 | tf_op jit(solution)/shard_map/feed_back/pallas_call | solution.py:220
  133.0 3.9 %fc1_grad.1 = (bf16[1152,1152]{1,0:T(8,128)(2,1)S(1)}, bf16[144,1152]{1,0:T(8,128)(2,1)S(1)}, bf16[144,1152]{1,0:T(8,128)(2,1)S(1)}) custom-call(bf16[256,1152]{1,0:T(8,128)(2,1)S(1)} %get-tuple-element.267.refs_8_.here, bf16[256,1152]{1,0:T(8,128)(2,1)S(1)} %collective-permute-done.32.refs_9_.there, bf16[512,1152]{1,0:T(8,128)(2,1)S(1)} %get-tuple-element.286.pre), custom_call_target="tpu_custom_call" | custom-call | bytes 1024 | tf_op jit(solution)/shard_map/fc1_grad/pallas_call | solution.py:220
  139.0 2.7 %collective-permute-done.41.refs_0_ = bf16[144,1152]{1,0:T(8,128)(2,1)S(1)} collective-permute-done((bf16[144,1152]{1,0:T(8,128)(2,1)S(1)}, bf16[144,1152]{1,0:T(8,128)(2,1)S(1)}, u32[]{:S(2)}, u32[]{:S(2)}) %collective-permute-start.41) | collective-permute-done | bytes 331808 | tf_op jit(solution)/shard_map/ppermute | solution.py:118
  142.9 4.7 %collective-permute-done.39.refs_0_ = bf16[144,1152]{1,0:T(8,128)(2,1)S(1)} collective-permute-done((bf16[144,1152]{1,0:T(8,128)(2,1)S(1)}, bf16[144,1152]{1,0:T(8,128)(2,1)S(1)}, u32[]{:S(2)}, u32[]{:S(2)}) %collective-permute-start.39) | collective-permute-done | bytes 331808 | tf_op jit(solution)/shard_map/ppermute | solution.py:118
  151.5 4.4 %feed_out.1 = (f32[256,1152]{1,0:T(8,128)S(1)}, bf16[256,1152]{1,0:T(8,128)(2,1)S(1)}) custom-call(bf16[144,1152]{1,0:T(8,128)(2,1)S(1)} %bitcast_convert_fusion.refs_8_.refs_0_, bf16[144,1152]{1,0:T(8,128)(2,1)} %collective-permute-done.20.refs_9_.refs_1_, bf16[144,1152]{1,0:T(8,128)(2,1)S(1)} %collective-permute-done.28.refs_10_.refs_2_, ...), custom_call_target="tpu_custom_call" | custom-call | bytes 1024 | tf_op jit(solution)/shard_map/feed_out/pallas_call | solution.py:220
  164.5 10.7 %attention_back.1 = (bf16[1152,1152]{1,0:T(8,128)(2,1)S(1)}, f32[256,1152]{1,0:T(8,128)S(1)}, bf16[256,1152]{1,0:T(8,128)(2,1)S(1)}, bf16[144,1152]{1,0:T(8,128)(2,1)S(1)}, bf16[144,1152]{1,0:T(8,128)(2,1)S(1)}) custom-call(bf16[144,1152]{1,0:T(8,128)(2,1)S(1)} %concatenate.41.refs_0_, bf16[144,1152]{1,0:T(8,128)(2,1)S(1)} %copy-done.8, ...), custom_call_target="tpu_custom_call" | custom-call | bytes 1024 | tf_op jit(solution)/shard_map/attention_back/pallas_call | solution.py:220
  175.3 3.0 %collective-permute-done.50.refs_0_ = bf16[144,1152]{1,0:T(8,128)(2,1)S(1)} collective-permute-done((bf16[144,1152]{1,0:T(8,128)(2,1)S(1)}, bf16[144,1152]{1,0:T(8,128)(2,1)S(1)}, u32[]{:S(2)}, u32[]{:S(2)}) %collective-permute-start.50) | collective-permute-done | bytes 331808 | tf_op jit(solution)/shard_map/ppermute | solution.py:118
  189.6 2.1 collective-permute-done.53.refs_0_
  193.2 5.2 %collective-permute-done.55.refs_0_ = bf16[144,1152]{1,0:T(8,128)(2,1)S(1)} collective-permute-done((bf16[144,1152]{1,0:T(8,128)(2,1)S(1)}, bf16[144,1152]{1,0:T(8,128)(2,1)S(1)}, u32[]{:S(2)}, u32[]{:S(2)}) %collective-permute-start.55) | collective-permute-done | bytes 331808 | tf_op jit(solution)/shard_map/ppermute | solution.py:118
  213.8 10.6 %collective-permute-done.63 = bf16[6,16,288]{2,1,0:T(8,128)(2,1)S(1)} collective-permute-done((bf16[6,16,288]{2,1,0:T(8,128)(2,1)S(1)}, bf16[6,16,288]{2,1,0:T(8,128)(2,1)S(1)}, u32[]{:S(2)}, u32[]{:S(2)}) %collective-permute-start.63) | collective-permute-done | bytes 55328 | tf_op jit(solution)/shard_map/ppermute | solution.py:56
  225.2 2.0 collective-permute-start.70
  227.7 2.6 %place_kept.3 = bf16[4,256,1152]{2,1,0:T(8,128)(2,1)} custom-call(bf16[256,1152]{1,0:T(8,128)(2,1)S(1)} %get-tuple-element.388.here, bf16[256,1152]{1,0:T(8,128)(2,1)S(1)} %collective-permute-done.65.there, bf16[4,256,1152]{2,1,0:T(8,128)(2,1)S(1)} %copy-done.6, s32[4,1,128]{2,1,0:T(1,128)S(1)} %bitcast.60), custom_call_target="tpu_custom_call" | custom-call | bytes 1024 | tf_op jit(solution)/shard_map/place_kept/pallas_call | solution.py:768
  230.3 3.1 %place_kept.2 = f32[4,256,1152]{2,1,0:T(8,128)} custom-call(bf16[256,1152]{1,0:T(8,128)(2,1)S(1)} %get-tuple-element.386.here, bf16[256,1152]{1,0:T(8,128)(2,1)S(1)} %collective-permute-done.64.there, bf16[4,256,1152]{2,1,0:T(8,128)(2,1)S(1)} %copy-done.4, s32[4,1,128]{2,1,0:T(1,128)S(1)} %bitcast.61), custom_call_target="tpu_custom_call" | custom-call | bytes 1024 | tf_op jit(solution)/shard_map/place_kept/pallas_call | solution.py:768
  235.0 4.9 %step_attention.1 = (f32[3,144,288]{2,1,0:T(8,128)}, f32[3,144,288]{2,1,0:T(8,128)}, f32[3,144,288]{2,1,0:T(8,128)}, f32[144,288]{1,0:T(8,128)}, f32[144,288]{1,0:T(8,128)}, /*index=5*/f32[144,288]{1,0:T(8,128)}) custom-call(s32[1]{0:T(128)} %bitcast.7.index, s32[1]{0:T(128)S(6)} %copy.50.steps, bf16[144,1152]{1,0:T(8,128)(2,1)} %copy-done.35, ...), custom_call_target="tpu_custom_call" | custom-call | bytes 1024 | tf_op jit(solution)/shard_map/step_attention/pallas_call | solution.py:873
  241.3 5.3 %step_ada.1 = (f32[6,144,288]{2,1,0:T(8,128)}, f32[6,144,288]{2,1,0:T(8,128)}, f32[6,144,288]{2,1,0:T(8,128)}) custom-call(s32[1]{0:T(128)S(6)} %copy.50.steps, bf16[32,144]{1,0:T(8,128)(2,1)} %copy-done.30, bf16[6,32,288]{2,1,0:T(8,128)(2,1)} %copy-done.27, f32[6,144,288]{2,1,0:T(8,128)} %bitcast.54, f32[6,144,288]{2,1,0:T(8,128)} %bitcast.62, ...), custom_call_target="tpu_custom_call" | custom-call | bytes 1024 | tf_op jit(solution)/shard_map/step_ada/pallas_call | solution.py:899
  250.1 4.0 %step_fc1.1 = (f32[144,1152]{1,0:T(8,128)}, f32[144,1152]{1,0:T(8,128)}, f32[144,1152]{1,0:T(8,128)}) custom-call(s32[1]{0:T(128)} %bitcast.7.index, s32[1]{0:T(128)S(6)} %copy.50.steps, bf16[144,1152]{1,0:T(8,128)(2,1)} %copy-done.37, bf16[144,1152]{1,0:T(8,128)(2,1)} %copy-done.36, bf16[1152,1152]{1,0:T(8,128)(2,1)} %copy-done, f32[144,1152]{1,0:T(8,128)} %refs_3_.3, ...), custom_call_target="tpu_custom_call" | custom-call | bytes 1024 | tf_op jit(solution)/shard_map/step_fc1/pallas_call | solution.py:873
  (269 shorter events, 103.3 us)
Async XLA Ops:
  2.2 12.9 %collective-permute-start.3 = (bf16[144,1152]{1,0:T(8,128)(2,1)S(1)}, bf16[144,1152]{1,0:T(8,128)(2,1)S(1)}, u32[]{:S(2)}, u32[]{:S(2)}) collective-permute-start(bf16[144,1152]{1,0:T(8,128)(2,1)S(1)} %concatenate.41.refs_0_), channel_id=1, source_target_pairs={{0,8},{8,16},{16,24},{24,28},{28,20},{20,12},{12,4},{4,0},{1,9},{9... | collective-permute-start | bytes 995336 | tf_op jit(solution)/shard_map/ppermute | solution.py:118
  15.1 13.8 %collective-permute-start.6 = (bf16[144,1152]{1,0:T(8,128)(2,1)S(1)}, bf16[144,1152]{1,0:T(8,128)(2,1)S(1)}, u32[]{:S(2)}, u32[]{:S(2)}) collective-permute-start(bf16[144,1152]{1,0:T(8,128)(2,1)S(1)} %collective-permute-done.3.refs_1_), channel_id=1, source_target_pairs={{0,8},{8,16},{16,24},{24,28},{28,20},{20,12},{12,4},{4,0},{1,9},{9... | collective-permute-start | bytes 995336 | tf_op jit(solution)/shard_map/ppermute | solution.py:118
  17.1 11.9 %collective-permute-start.7 = (bf16[144,1152]{1,0:T(8,128)(2,1)S(1)}, bf16[144,1152]{1,0:T(8,128)(2,1)S(1)}, u32[]{:S(2)}, u32[]{:S(2)}) collective-permute-start(bf16[144,1152]{1,0:T(8,128)(2,1)S(1)} %collective-permute-done.4.refs_5_), channel_id=1, source_target_pairs={{8,0},{16,8},{24,16},{28,24},{20,28},{12,20},{4,12},{0,4},{9,1},{1... | collective-permute-start | bytes 995336 | tf_op jit(solution)/shard_map/ppermute | solution.py:118
  17.2 11.7 %collective-permute-start.5 = (bf16[16,8,144]{2,0,1:T(8,128)(2,1)S(1)}, bf16[16,8,144]{2,0,1:T(8,128)(2,1)S(1)}, u32[]{:S(2)}, u32[]{:S(2)}) collective-permute-start(bf16[16,8,144]{2,0,1:T(8,128)(2,1)S(1)} %pad_maximum_fusion.3), channel_id=1, source_target_pairs={{0,16},{4,20},{8,24},{12,28},{16,0},{20,4},{24,8},{28,12},{1,17},{... | collective-permute-start | bytes 110600 | tf_op jit(solution)/shard_map/ppermute | solution.py:56
  30.5 12.1 %collective-permute-start.9 = (bf16[144,1152]{1,0:T(8,128)(2,1)S(1)}, bf16[144,1152]{1,0:T(8,128)(2,1)S(1)}, u32[]{:S(2)}, u32[]{:S(2)}) collective-permute-start(bf16[144,1152]{1,0:T(8,128)(2,1)S(1)} %collective-permute-done.6.refs_2_), channel_id=1, source_target_pairs={{0,8},{8,16},{16,24},{24,28},{28,20},{20,12},{12,4},{4,0},{1,9},{9... | collective-permute-start | bytes 995336 | tf_op jit(solution)/shard_map/ppermute | solution.py:118
  42.6 11.4 %collective-permute-start.14 = (bf16[144,1152]{1,0:T(8,128)(2,1)S(1)}, bf16[144,1152]{1,0:T(8,128)(2,1)S(1)}, u32[]{:S(2)}, u32[]{:S(2)}) collective-permute-start(bf16[144,1152]{1,0:T(8,128)(2,1)S(1)} %collective-permute-done.9.refs_3_), channel_id=1, source_target_pairs={{0,8},{8,16},{16,24},{24,28},{28,20},{20,12},{12,4},{4,0},{1,9},{9... | collective-permute-start | bytes 995336 | tf_op jit(solution)/shard_map/ppermute | solution.py:118
  46.5 13.9 %collective-permute-start.18 = (bf16[144,1152]{1,0:T(8,128)(2,1)S(1)}, bf16[144,1152]{1,0:T(8,128)(2,1)}, u32[]{:S(2)}, u32[]{:S(2)}) collective-permute-start(bf16[144,1152]{1,0:T(8,128)(2,1)S(1)} %convert_element_type.37.refs_0_), channel_id=1, source_target_pairs={{0,8},{8,16},{16,24},{24,28},{28,20},{20,12},{12,4},{4,0},{1,9},{9... | collective-permute-start | bytes 995336 | tf_op jit(solution)/shard_map/ppermute | solution.py:118
  54.1 15.0 %collective-permute-start.20 = (bf16[144,1152]{1,0:T(8,128)(2,1)S(1)}, bf16[144,1152]{1,0:T(8,128)(2,1)}, u32[]{:S(2)}, u32[]{:S(2)}) collective-permute-start(bf16[144,1152]{1,0:T(8,128)(2,1)S(1)} %bitcast_convert_fusion.refs_8_.refs_0_), channel_id=1, source_target_pairs={{8,0},{16,8},{24,16},{28,24},{20,28},{12,20},{4,12},{0,4},{9,1},{1... | collective-permute-start | bytes 995336 | tf_op jit(solution)/shard_map/ppermute | solution.py:118
  58.2 10.9 %collective-permute-start.21 = (bf16[144,1152]{1,0:T(8,128)(2,1)S(1)}, bf16[144,1152]{1,0:T(8,128)(2,1)S(1)}, u32[]{:S(2)}, u32[]{:S(2)}) collective-permute-start(bf16[144,1152]{1,0:T(8,128)(2,1)S(1)} %bitcast_convert_fusion.refs_8_.refs_0_), channel_id=1, source_target_pairs={{0,8},{8,16},{16,24},{24,28},{28,20},{20,12},{12,4},{4,0},{1,9},{9... | collective-permute-start | bytes 995336 | tf_op jit(solution)/shard_map/ppermute | solution.py:118
  62.2 12.6 %collective-permute-start.22 = (bf16[144,1152]{1,0:T(8,128)(2,1)}, bf16[144,1152]{1,0:T(8,128)(2,1)S(1)}, u32[]{:S(2)}, u32[]{:S(2)}) collective-permute-start(bf16[144,1152]{1,0:T(8,128)(2,1)} %collective-permute-done.18.refs_1_), channel_id=1, source_target_pairs={{0,8},{8,16},{16,24},{24,28},{28,20},{20,12},{12,4},{4,0},{1,9},{9... | collective-permute-start | bytes 995336 | tf_op jit(solution)/shard_map/ppermute | solution.py:118
  62.2 12.6 %collective-permute-start.23 = (bf16[144,1152]{1,0:T(8,128)(2,1)}, bf16[144,1152]{1,0:T(8,128)(2,1)S(1)}, u32[]{:S(2)}, u32[]{:S(2)}) collective-permute-start(bf16[144,1152]{1,0:T(8,128)(2,1)} %collective-permute-done.19.refs_5_), channel_id=1, source_target_pairs={{8,0},{16,8},{24,16},{28,24},{20,28},{12,20},{4,12},{0,4},{9,1},{1... | collective-permute-start | bytes 995336 | tf_op jit(solution)/shard_map/ppermute | solution.py:118
  77.1 19.9 %collective-permute-start.25 = (bf16[256,1152]{1,0:T(8,128)(2,1)S(1)}, bf16[256,1152]{1,0:T(8,128)(2,1)S(1)}, u32[]{:S(2)}, u32[]{:S(2)}) collective-permute-start(bf16[256,1152]{1,0:T(8,128)(2,1)S(1)} %add_convert_fusion.3.own.attn_own), channel_id=1, source_target_pairs={{0,2},{1,3},{2,0},{3,1},{4,6},{5,7},{6,4},{7,5},{8,10},{9,11},{10,... | collective-permute-start | bytes 1769480 | tf_op jit(solution)/shard_map/ppermute | solution.py:39
  78.8 10.9 %collective-permute-start.28 = (bf16[144,1152]{1,0:T(8,128)(2,1)}, bf16[144,1152]{1,0:T(8,128)(2,1)S(1)}, u32[]{:S(2)}, u32[]{:S(2)}) collective-permute-start(bf16[144,1152]{1,0:T(8,128)(2,1)} %collective-permute-done.20.refs_9_.refs_1_), channel_id=1, source_target_pairs={{8,0},{16,8},{24,16},{28,24},{20,28},{12,20},{4,12},{0,4},{9,1},{1... | collective-permute-start | bytes 995336 | tf_op jit(solution)/shard_map/ppermute | solution.py:118
  80.6 10.7 %collective-permute-start.29 = (bf16[144,1152]{1,0:T(8,128)(2,1)S(1)}, bf16[144,1152]{1,0:T(8,128)(2,1)S(1)}, u32[]{:S(2)}, u32[]{:S(2)}) collective-permute-start(bf16[144,1152]{1,0:T(8,128)(2,1)S(1)} %collective-permute-done.21.refs_13_.refs_5_), channel_id=1, source_target_pairs={{0,8},{8,16},{16,24},{24,28},{28,20},{20,12},{12,4},{4,0},{1,9},{9... | collective-permute-start | bytes 995336 | tf_op jit(solution)/shard_map/ppermute | solution.py:118
  80.8 16.1 %collective-permute-start.26 = (bf16[144,1152]{1,0:T(8,128)(2,1)S(1)}, bf16[144,1152]{1,0:T(8,128)(2,1)S(1)}, u32[]{:S(2)}, u32[]{:S(2)}) collective-permute-start(bf16[144,1152]{1,0:T(8,128)(2,1)S(1)} %collective-permute-done.22.refs_2_), channel_id=1, source_target_pairs={{0,8},{8,16},{16,24},{24,28},{28,20},{20,12},{12,4},{4,0},{1,9},{9... | collective-permute-start | bytes 995336 | tf_op jit(solution)/shard_map/ppermute | solution.py:118
  82.8 14.2 %collective-permute-start.27 = (bf16[144,1152]{1,0:T(8,128)(2,1)S(1)}, bf16[144,1152]{1,0:T(8,128)(2,1)S(1)}, u32[]{:S(2)}, u32[]{:S(2)}) collective-permute-start(bf16[144,1152]{1,0:T(8,128)(2,1)S(1)} %collective-permute-done.23.refs_6_), channel_id=1, source_target_pairs={{8,0},{16,8},{24,16},{28,24},{20,28},{12,20},{4,12},{0,4},{9,1},{1... | collective-permute-start | bytes 995336 | tf_op jit(solution)/shard_map/ppermute | solution.py:118
  129.8 18.3 %collective-permute-start.38 = (bf16[256,1152]{1,0:T(8,128)(2,1)S(1)}, bf16[256,1152]{1,0:T(8,128)(2,1)S(1)}, u32[]{:S(2)}, u32[]{:S(2)}) collective-permute-start(bf16[256,1152]{1,0:T(8,128)(2,1)S(1)} %add_convert_fusion.2.own), channel_id=1, source_target_pairs={{0,2},{1,3},{2,0},{3,1},{4,6},{5,7},{6,4},{7,5},{8,10},{9,11},{10,... | collective-permute-start | bytes 1769480 | tf_op jit(solution)/shard_map/ppermute | solution.py:39
  130.9 10.7 %collective-permute-start.41 = (bf16[144,1152]{1,0:T(8,128)(2,1)S(1)}, bf16[144,1152]{1,0:T(8,128)(2,1)S(1)}, u32[]{:S(2)}, u32[]{:S(2)}) collective-permute-start(bf16[144,1152]{1,0:T(8,128)(2,1)S(1)} %get-tuple-element.294), channel_id=1, source_target_pairs={{8,0},{16,8},{24,16},{28,24},{20,28},{12,20},{4,12},{0,4},{9,1},{1... | collective-permute-start | bytes 995336 | tf_op jit(solution)/shard_map/ppermute | solution.py:118
  136.9 10.7 %collective-permute-start.39 = (bf16[144,1152]{1,0:T(8,128)(2,1)S(1)}, bf16[144,1152]{1,0:T(8,128)(2,1)S(1)}, u32[]{:S(2)}, u32[]{:S(2)}) collective-permute-start(bf16[144,1152]{1,0:T(8,128)(2,1)S(1)} %get-tuple-element.289), channel_id=1, source_target_pairs={{8,0},{16,8},{24,16},{28,24},{20,28},{12,20},{4,12},{0,4},{9,1},{1... | collective-permute-start | bytes 995336 | tf_op jit(solution)/shard_map/ppermute | solution.py:118
  160.2 18.2 %collective-permute-start.47 = (bf16[256,1152]{1,0:T(8,128)(2,1)S(1)}, bf16[256,1152]{1,0:T(8,128)(2,1)S(1)}, u32[]{:S(2)}, u32[]{:S(2)}) collective-permute-start(bf16[256,1152]{1,0:T(8,128)(2,1)S(1)} %add_convert_fusion.1.own), channel_id=1, source_target_pairs={{0,2},{1,3},{2,0},{3,1},{4,6},{5,7},{6,4},{7,5},{8,10},{9,11},{10,... | collective-permute-start | bytes 1769480 | tf_op jit(solution)/shard_map/ppermute | solution.py:39
  161.6 13.6 %collective-permute-start.48 = (bf16[144,1152]{1,0:T(8,128)(2,1)S(1)}, bf16[144,1152]{1,0:T(8,128)(2,1)S(1)}, u32[]{:S(2)}, u32[]{:S(2)}) collective-permute-start(bf16[144,1152]{1,0:T(8,128)(2,1)S(1)} %get-tuple-element.334), channel_id=1, source_target_pairs={{8,0},{16,8},{24,16},{28,24},{20,28},{12,20},{4,12},{0,4},{9,1},{1... | collective-permute-start | bytes 995336 | tf_op jit(solution)/shard_map/ppermute | solution.py:118
  162.4 12.8 %collective-permute-start.49 = (bf16[144,1152]{1,0:T(8,128)(2,1)S(1)}, bf16[144,1152]{1,0:T(8,128)(2,1)S(1)}, u32[]{:S(2)}, u32[]{:S(2)}) collective-permute-start(bf16[144,1152]{1,0:T(8,128)(2,1)S(1)} %get-tuple-element.335), channel_id=1, source_target_pairs={{0,8},{8,16},{16,24},{24,28},{28,20},{20,12},{12,4},{4,0},{1,9},{9... | collective-permute-start | bytes 995336 | tf_op jit(solution)/shard_map/ppermute | solution.py:118
  163.7 14.6 %collective-permute-start.50 = (bf16[144,1152]{1,0:T(8,128)(2,1)S(1)}, bf16[144,1152]{1,0:T(8,128)(2,1)S(1)}, u32[]{:S(2)}, u32[]{:S(2)}) collective-permute-start(bf16[144,1152]{1,0:T(8,128)(2,1)S(1)} %add_blocks.12), channel_id=1, source_target_pairs={{8,0},{16,8},{24,16},{28,24},{20,28},{12,20},{4,12},{0,4},{9,1},{1... | collective-permute-start | bytes 995336 | tf_op jit(solution)/shard_map/ppermute | solution.py:118
  180.4 18.0 %collective-permute-start.52 = (bf16[256,1152]{1,0:T(8,128)(2,1)S(1)}, bf16[256,1152]{1,0:T(8,128)(2,1)S(1)}, u32[]{:S(2)}, u32[]{:S(2)}) collective-permute-start(bf16[256,1152]{1,0:T(8,128)(2,1)S(1)} %add_convert_fusion.own), channel_id=1, source_target_pairs={{0,2},{1,3},{2,0},{3,1},{4,6},{5,7},{6,4},{7,5},{8,10},{9,11},{10,... | collective-permute-start | bytes 1769480 | tf_op jit(solution)/shard_map/ppermute | solution.py:39
  183.5 14.9 %collective-permute-start.55 = (bf16[144,1152]{1,0:T(8,128)(2,1)S(1)}, bf16[144,1152]{1,0:T(8,128)(2,1)S(1)}, u32[]{:S(2)}, u32[]{:S(2)}) collective-permute-start(bf16[144,1152]{1,0:T(8,128)(2,1)S(1)} %get-tuple-element.362), channel_id=1, source_target_pairs={{8,0},{16,8},{24,16},{28,24},{20,28},{12,20},{4,12},{0,4},{9,1},{1... | collective-permute-start | bytes 995336 | tf_op jit(solution)/shard_map/ppermute | solution.py:118
  184.4 14.0 %collective-permute-start.56 = (bf16[144,1152]{1,0:T(8,128)(2,1)S(1)}, bf16[144,1152]{1,0:T(8,128)(2,1)S(1)}, u32[]{:S(2)}, u32[]{:S(2)}) collective-permute-start(bf16[144,1152]{1,0:T(8,128)(2,1)S(1)} %get-tuple-element.363), channel_id=1, source_target_pairs={{0,8},{8,16},{16,24},{24,28},{28,20},{20,12},{12,4},{4,0},{1,9},{9... | collective-permute-start | bytes 995336 | tf_op jit(solution)/shard_map/ppermute | solution.py:118
  198.4 11.3 %collective-permute-start.61 = (bf16[144,1152]{1,0:T(8,128)(2,1)S(1)}, bf16[144,1152]{1,0:T(8,128)(2,1)S(1)}, u32[]{:S(2)}, u32[]{:S(2)}) collective-permute-start(bf16[144,1152]{1,0:T(8,128)(2,1)S(1)} %get-tuple-element.372), channel_id=1, source_target_pairs={{0,8},{8,16},{16,24},{24,28},{28,20},{20,12},{12,4},{4,0},{1,9},{9... | collective-permute-start | bytes 995336 | tf_op jit(solution)/shard_map/ppermute | solution.py:118
  209.7 14.8 %collective-permute-start.64 = (bf16[256,1152]{1,0:T(8,128)(2,1)S(1)}, bf16[256,1152]{1,0:T(8,128)(2,1)S(1)}, u32[]{:S(2)}, u32[]{:S(2)}) collective-permute-start(bf16[256,1152]{1,0:T(8,128)(2,1)S(1)} %get-tuple-element.386.here), channel_id=1, source_target_pairs={{0,1},{1,0},{2,3},{3,2},{4,5},{5,4},{6,7},{7,6},{8,9},{9,8},{10,11... | collective-permute-start | bytes 1769480 | tf_op jit(solution)/shard_map/ppermute | solution.py:35
  209.8 14.7 %collective-permute-start.65 = (bf16[256,1152]{1,0:T(8,128)(2,1)S(1)}, bf16[256,1152]{1,0:T(8,128)(2,1)S(1)}, u32[]{:S(2)}, u32[]{:S(2)}) collective-permute-start(bf16[256,1152]{1,0:T(8,128)(2,1)S(1)} %get-tuple-element.388.here), channel_id=1, source_target_pairs={{0,1},{1,0},{2,3},{3,2},{4,5},{5,4},{6,7},{7,6},{8,9},{9,8},{10,11... | collective-permute-start | bytes 1769480 | tf_op jit(solution)/shard_map/ppermute | solution.py:35
  210.7 13.8 %collective-permute-start.66 = (bf16[144,1152]{1,0:T(8,128)(2,1)S(1)}, bf16[144,1152]{1,0:T(8,128)(2,1)S(1)}, u32[]{:S(2)}, u32[]{:S(2)}) collective-permute-start(bf16[144,1152]{1,0:T(8,128)(2,1)S(1)} %get-tuple-element.382), channel_id=1, source_target_pairs={{0,8},{8,16},{16,24},{24,28},{28,20},{20,12},{12,4},{4,0},{1,9},{9... | collective-permute-start | bytes 995336 | tf_op jit(solution)/shard_map/ppermute | solution.py:118
  212.0 12.5 %collective-permute-start.67 = (bf16[144,1152]{1,0:T(8,128)(2,1)S(1)}, bf16[144,1152]{1,0:T(8,128)(2,1)S(1)}, u32[]{:S(2)}, u32[]{:S(2)}) collective-permute-start(bf16[144,1152]{1,0:T(8,128)(2,1)S(1)} %get-tuple-element.383), channel_id=1, source_target_pairs={{8,0},{16,8},{24,16},{28,24},{20,28},{12,20},{4,12},{0,4},{9,1},{1... | collective-permute-start | bytes 995336 | tf_op jit(solution)/shard_map/ppermute | solution.py:118
  212.8 11.6 %collective-permute-start.63 = (bf16[6,16,288]{2,1,0:T(8,128)(2,1)S(1)}, bf16[6,16,288]{2,1,0:T(8,128)(2,1)S(1)}, u32[]{:S(2)}, u32[]{:S(2)}) collective-permute-start(bf16[6,16,288]{2,1,0:T(8,128)(2,1)S(1)} %pad_maximum_fusion.2), channel_id=1, source_target_pairs={{0,16},{4,20},{8,24},{12,28},{16,0},{20,4},{24,8},{28,12},{1,17},{... | collective-permute-start | bytes 165896 | tf_op jit(solution)/shard_map/ppermute | solution.py:56
  (83 other events, 885.8 us)

commit v3 on v2

--- a/solution.py
+++ b/solution.py
@@ -1282,7 +1282,7 @@
         return values, kept_grad, kept_out, *there, *sums
 
     mod_grad_all, kept_grad, kept_out, grad_there, kept_there, *sums = tick(
-        last_spread, (attn_sums, "ab")
+        last_spread, (attn_sums, "ab+")
     )
     if ring:
         fc1_sums.finish("a", sums)

time: 256 us -> 255 us (level)
  transfers between devices with their start and end apart: 76 -> 76, of which waited for: 36 -> 36; matrix products, arithmetic and copies ran while one was open for 0% -> 0% of each run, Pallas kernels for 29% -> 30%
where the time goes in v3:
time: 255 us
  waiting for transfers between devices  93.8 us (37%)
  Pallas kernels  75.7 us (30%)
  starting transfers between devices  72.2 us (28%)
  local copies, waits for them, and re-layouts  7.56 us (3%)
  other arithmetic  3.03 us (1%)
    pallas_call x15, Pallas kernels, run(): pl.pallas_call(kernel, out_shape=[jax.ShapeDtypeStruct(shape, dtype) for...  50.8 us
    ppermute x42, waiting for transfers between devices, hop(): return lax.ppermute(values, 'dp', clockwise if direction > 0 else backward)  48.1 us
    ppermute x42, starting transfers between devices, hop(): return lax.ppermute(values, 'dp', clockwise if direction > 0 else backward)  43.1 us
    ppermute x16, waiting for transfers between devices, swap_dp(): return lax.ppermute(values, 'dp', [(i, i ^ bit) for i in range(size)])  35 us
    ppermute x16, starting transfers between devices, swap_dp(): return lax.ppermute(values, 'dp', [(i, i ^ bit) for i in range(size)])  19.5 us
    pallas_call x3, Pallas kernels, step_weights(): pl.pallas_call(partial(kernel, rate, len(given)), grid_spec=pltpu.Prefetc...  10.7 us
    ppermute x11, waiting for transfers between devices, swap_core(): return lax.ppermute(values, 'mp', [(j, j ^ 1) for j in range(4)])  9.09 us
    ppermute x6, starting transfers between devices, swap_x(): return lax.ppermute(values, 'mp', [(j, j ^ 2) for j in range(4)])  7.51 us
  transfers between devices with their start and end apart: 76, of which 36 were waited for; matrix products, arithmetic and copies ran while one was open for 0% of the time, Pallas kernels for 30%

profile of v3, /device:TPU:0, one launch (start us, length us, event | category | flops | bytes accessed | tf_op | source)
XLA Modules:
  0.0 254.8 jit_solution(5681488115806772014)
XLA Ops:
  2.2 3.1 %collective-permute-start.3 = (bf16[144,1152]{1,0:T(8,128)(2,1)S(1)}, bf16[144,1152]{1,0:T(8,128)(2,1)S(1)}, u32[]{:S(2)}, u32[]{:S(2)}) collective-permute-start(bf16[144,1152]{1,0:T(8,128)(2,1)S(1)} %concatenate.41.refs_0_), channel_id=1, source_target_pairs={{0,8},{8,16},{16,24},{24,28},{28,20},{20,12},{12,4},{4,0},{1,9},{9... | collective-permute-start | bytes 995336 | tf_op jit(solution)/shard_map/ppermute | solution.py:118
  5.4 2.0 collective-permute-start
  10.7 2.1 first_norm.1
  17.2 2.9 %collective-permute-start.5 = (bf16[16,8,144]{2,0,1:T(8,128)(2,1)S(1)}, bf16[16,8,144]{2,0,1:T(8,128)(2,1)S(1)}, u32[]{:S(2)}, u32[]{:S(2)}) collective-permute-start(bf16[16,8,144]{2,0,1:T(8,128)(2,1)S(1)} %pad_maximum_fusion.3), channel_id=1, source_target_pairs={{0,16},{4,20},{8,24},{12,28},{16,0},{20,4},{24,8},{28,12},{1,17},{... | collective-permute-start | bytes 110600 | tf_op jit(solution)/shard_map/ppermute | solution.py:56
  20.2 8.8 %collective-permute-done.5 = bf16[16,8,144]{2,0,1:T(8,128)(2,1)S(1)} collective-permute-done((bf16[16,8,144]{2,0,1:T(8,128)(2,1)S(1)}, bf16[16,8,144]{2,0,1:T(8,128)(2,1)S(1)}, u32[]{:S(2)}, u32[]{:S(2)}) %collective-permute-start.5) | collective-permute-done | bytes 36896 | tf_op jit(solution)/shard_map/ppermute | solution.py:56
  30.5 2.1 collective-permute-start.9
  32.6 6.0 %collective-permute-done.8 = f32[6,16,288]{2,1,0:T(8,128)S(1)} collective-permute-done((f32[6,16,288]{2,1,0:T(8,128)S(1)}, f32[6,16,288]{2,1,0:T(8,128)S(1)}, u32[]{:S(2)}, u32[]{:S(2)}) %collective-permute-start.8) | collective-permute-done | bytes 110624 | tf_op jit(solution)/shard_map/ppermute | solution.py:56
  39.2 3.3 %collective-permute-done.9.refs_3_ = bf16[144,1152]{1,0:T(8,128)(2,1)S(1)} collective-permute-done((bf16[144,1152]{1,0:T(8,128)(2,1)S(1)}, bf16[144,1152]{1,0:T(8,128)(2,1)S(1)}, u32[]{:S(2)}, u32[]{:S(2)}) %collective-permute-start.9) | collective-permute-done | bytes 331808 | tf_op jit(solution)/shard_map/ppermute | solution.py:118
  47.4 5.2 %collective-permute-done.11 = f32[6,4,288]{2,1,0:T(4,128)S(1)} collective-permute-done((f32[6,4,288]{2,1,0:T(4,128)S(1)}, f32[6,4,288]{2,1,0:T(4,128)S(1)}, u32[]{:S(2)}, u32[]{:S(2)}) %collective-permute-start.11) | collective-permute-done | bytes 27680 | tf_op jit(solution)/shard_map/ppermute | solution.py:56
  62.2 2.0 collective-permute-start.23
  65.9 3.2 %project.1 = (bf16[512,1152]{1,0:T(8,128)(2,1)S(1)}, bf16[512,864]{1,0:T(8,128)(2,1)S(1)}) custom-call(bf16[144,1152]{1,0:T(8,128)(2,1)S(1)} %concatenate.41.refs_0_, bf16[144,1152]{1,0:T(8,128)(2,1)S(1)} %collective-permute-done.3.refs_1_, bf16[144,1152]{1,0:T(8,128)(2,1)S(1)} %collective-permute-done.6.refs_2_, ...), custom_call_target="tpu_custom_call" | custom-call | bytes 1024 | tf_op jit(solution)/shard_map/project/pallas_call | solution.py:220
  69.2 5.6 %attend.1 = (bf16[512,288]{1,0:T(8,128)(2,1)S(1)}, f32[256,1152]{1,0:T(8,128)S(1)}, bf16[256,1152]{1,0:T(8,128)(2,1)S(1)}) custom-call(bf16[144,1152]{1,0:T(8,128)(2,1)S(1)} %concatenate.41.refs_0_, bf16[144,1152]{1,0:T(8,128)(2,1)S(1)} %collective-permute-done.3.refs_1_, bf16[144,1152]{1,0:T(8,128)(2,1)S(1)} %collective-permute-done.6.refs_2_, ...), custom_call_target="tpu_custom_call" | custom-call | bytes 1024 | tf_op jit(solution)/shard_map/attend/pallas_call | solution.py:220
  83.4 6.3 %collective-permute-done.28.refs_10_.refs_2_ = bf16[144,1152]{1,0:T(8,128)(2,1)S(1)} collective-permute-done((bf16[144,1152]{1,0:T(8,128)(2,1)}, bf16[144,1152]{1,0:T(8,128)(2,1)S(1)}, u32[]{:S(2)}, u32[]{:S(2)}) %collective-permute-start.28) | collective-permute-done | bytes 331808 | tf_op jit(solution)/shard_map/ppermute | solution.py:118
  91.3 5.7 %collective-permute-done.26.refs_3_ = bf16[144,1152]{1,0:T(8,128)(2,1)S(1)} collective-permute-done((bf16[144,1152]{1,0:T(8,128)(2,1)S(1)}, bf16[144,1152]{1,0:T(8,128)(2,1)S(1)}, u32[]{:S(2)}, u32[]{:S(2)}) %collective-permute-start.26) | collective-permute-done | bytes 331808 | tf_op jit(solution)/shard_map/ppermute | solution.py:118
  99.6 5.8 %collective-permute-done.30.refs_4_ = bf16[144,1152]{1,0:T(8,128)(2,1)S(1)} collective-permute-done((bf16[144,1152]{1,0:T(8,128)(2,1)S(1)}, bf16[144,1152]{1,0:T(8,128)(2,1)S(1)}, u32[]{:S(2)}, u32[]{:S(2)}) %collective-permute-start.30) | collective-permute-done | bytes 331808 | tf_op jit(solution)/shard_map/ppermute | solution.py:118
  108.1 7.8 %feed_forward.1 = (f32[512,1152]{1,0:T(8,128)S(1)}, bf16[512,1152]{1,0:T(8,128)(2,1)S(1)}, bf16[1152,1152]{1,0:T(8,128)(2,1)S(1)}, bf16[144,1152]{1,0:T(8,128)(2,1)S(1)}, bf16[144,1152]{1,0:T(8,128)(2,1)S(1)}) custom-call(bf16[144,1152]{1,0:T(8,128)(2,1)S(1)} %convert_element_type.37.refs_0_, bf16[144,1152]{1,0:T(8,128)(2,1)} %collective-permute-done.18.refs_1_, ...), custom_call_target="tpu_custom_call" | custom-call | bytes 1024 | tf_op jit(solution)/shard_map/feed_forward/pallas_call | solution.py:220
  119.2 8.4 %feed_back.1 = (bf16[512,1152]{1,0:T(8,128)(2,1)S(1)}, f32[256,1152]{1,0:T(8,128)S(1)}, bf16[256,1152]{1,0:T(8,128)(2,1)S(1)}) custom-call(bf16[144,1152]{1,0:T(8,128)(2,1)S(1)} %convert_element_type.37.refs_0_, bf16[144,1152]{1,0:T(8,128)(2,1)} %collective-permute-done.18.refs_1_, bf16[144,1152]{1,0:T(8,128)(2,1)S(1)} %collective-permute-done.22.refs_2_, ...), custom_call_target="tpu_custom_call" | custom-call | bytes 1024 | tf_op jit(solution)/shard_map/feed_back/pallas_call | solution.py:220
  133.0 3.9 %fc1_grad.1 = (bf16[1152,1152]{1,0:T(8,128)(2,1)S(1)}, bf16[144,1152]{1,0:T(8,128)(2,1)S(1)}, bf16[144,1152]{1,0:T(8,128)(2,1)S(1)}) custom-call(bf16[256,1152]{1,0:T(8,128)(2,1)S(1)} %get-tuple-element.267.refs_8_.here, bf16[256,1152]{1,0:T(8,128)(2,1)S(1)} %collective-permute-done.32.refs_9_.there, bf16[512,1152]{1,0:T(8,128)(2,1)S(1)} %get-tuple-element.286.pre), custom_call_target="tpu_custom_call" | custom-call | bytes 1024 | tf_op jit(solution)/shard_map/fc1_grad/pallas_call | solution.py:220
  139.0 2.7 %collective-permute-done.41.refs_0_ = bf16[144,1152]{1,0:T(8,128)(2,1)S(1)} collective-permute-done((bf16[144,1152]{1,0:T(8,128)(2,1)S(1)}, bf16[144,1152]{1,0:T(8,128)(2,1)S(1)}, u32[]{:S(2)}, u32[]{:S(2)}) %collective-permute-start.41) | collective-permute-done | bytes 331808 | tf_op jit(solution)/shard_map/ppermute | solution.py:118
  142.9 4.7 %collective-permute-done.39.refs_0_ = bf16[144,1152]{1,0:T(8,128)(2,1)S(1)} collective-permute-done((bf16[144,1152]{1,0:T(8,128)(2,1)S(1)}, bf16[144,1152]{1,0:T(8,128)(2,1)S(1)}, u32[]{:S(2)}, u32[]{:S(2)}) %collective-permute-start.39) | collective-permute-done | bytes 331808 | tf_op jit(solution)/shard_map/ppermute | solution.py:118
  151.5 4.4 %feed_out.1 = (f32[256,1152]{1,0:T(8,128)S(1)}, bf16[256,1152]{1,0:T(8,128)(2,1)S(1)}) custom-call(bf16[144,1152]{1,0:T(8,128)(2,1)S(1)} %bitcast_convert_fusion.refs_8_.refs_0_, bf16[144,1152]{1,0:T(8,128)(2,1)} %collective-permute-done.20.refs_9_.refs_1_, bf16[144,1152]{1,0:T(8,128)(2,1)S(1)} %collective-permute-done.28.refs_10_.refs_2_, ...), custom_call_target="tpu_custom_call" | custom-call | bytes 1024 | tf_op jit(solution)/shard_map/feed_out/pallas_call | solution.py:220
  164.5 10.7 %attention_back.1 = (bf16[1152,1152]{1,0:T(8,128)(2,1)S(1)}, f32[256,1152]{1,0:T(8,128)S(1)}, bf16[256,1152]{1,0:T(8,128)(2,1)S(1)}, bf16[144,1152]{1,0:T(8,128)(2,1)S(1)}, bf16[144,1152]{1,0:T(8,128)(2,1)S(1)}) custom-call(bf16[144,1152]{1,0:T(8,128)(2,1)S(1)} %concatenate.41.refs_0_, bf16[144,1152]{1,0:T(8,128)(2,1)S(1)} %copy-done.8, ...), custom_call_target="tpu_custom_call" | custom-call | bytes 1024 | tf_op jit(solution)/shard_map/attention_back/pallas_call | solution.py:220
  175.3 3.0 %collective-permute-done.50.refs_0_ = bf16[144,1152]{1,0:T(8,128)(2,1)S(1)} collective-permute-done((bf16[144,1152]{1,0:T(8,128)(2,1)S(1)}, bf16[144,1152]{1,0:T(8,128)(2,1)S(1)}, u32[]{:S(2)}, u32[]{:S(2)}) %collective-permute-start.50) | collective-permute-done | bytes 331808 | tf_op jit(solution)/shard_map/ppermute | solution.py:118
  189.6 2.1 collective-permute-done.53.refs_0_
  193.2 5.2 %collective-permute-done.55.refs_0_ = bf16[144,1152]{1,0:T(8,128)(2,1)S(1)} collective-permute-done((bf16[144,1152]{1,0:T(8,128)(2,1)S(1)}, bf16[144,1152]{1,0:T(8,128)(2,1)S(1)}, u32[]{:S(2)}, u32[]{:S(2)}) %collective-permute-start.55) | collective-permute-done | bytes 331808 | tf_op jit(solution)/shard_map/ppermute | solution.py:118
  213.8 10.6 %collective-permute-done.63 = bf16[6,16,288]{2,1,0:T(8,128)(2,1)S(1)} collective-permute-done((bf16[6,16,288]{2,1,0:T(8,128)(2,1)S(1)}, bf16[6,16,288]{2,1,0:T(8,128)(2,1)S(1)}, u32[]{:S(2)}, u32[]{:S(2)}) %collective-permute-start.63) | collective-permute-done | bytes 55328 | tf_op jit(solution)/shard_map/ppermute | solution.py:56
  224.8 2.0 collective-permute-start.70
  227.3 2.6 %place_kept.3 = bf16[4,256,1152]{2,1,0:T(8,128)(2,1)} custom-call(bf16[256,1152]{1,0:T(8,128)(2,1)S(1)} %get-tuple-element.388.here, bf16[256,1152]{1,0:T(8,128)(2,1)S(1)} %collective-permute-done.65.there, bf16[4,256,1152]{2,1,0:T(8,128)(2,1)S(1)} %copy-done.6, s32[4,1,128]{2,1,0:T(1,128)S(1)} %bitcast.60), custom_call_target="tpu_custom_call" | custom-call | bytes 1024 | tf_op jit(solution)/shard_map/place_kept/pallas_call | solution.py:768
  229.9 3.1 %place_kept.2 = f32[4,256,1152]{2,1,0:T(8,128)} custom-call(bf16[256,1152]{1,0:T(8,128)(2,1)S(1)} %get-tuple-element.386.here, bf16[256,1152]{1,0:T(8,128)(2,1)S(1)} %collective-permute-done.64.there, bf16[4,256,1152]{2,1,0:T(8,128)(2,1)S(1)} %copy-done.4, s32[4,1,128]{2,1,0:T(1,128)S(1)} %bitcast.61), custom_call_target="tpu_custom_call" | custom-call | bytes 1024 | tf_op jit(solution)/shard_map/place_kept/pallas_call | solution.py:768
  234.6 4.9 %step_attention.1 = (f32[3,144,288]{2,1,0:T(8,128)}, f32[3,144,288]{2,1,0:T(8,128)}, f32[3,144,288]{2,1,0:T(8,128)}, f32[144,288]{1,0:T(8,128)}, f32[144,288]{1,0:T(8,128)}, /*index=5*/f32[144,288]{1,0:T(8,128)}) custom-call(s32[1]{0:T(128)} %bitcast.7.index, s32[1]{0:T(128)S(6)} %copy.50.steps, bf16[144,1152]{1,0:T(8,128)(2,1)} %copy-done.35, ...), custom_call_target="tpu_custom_call" | custom-call | bytes 1024 | tf_op jit(solution)/shard_map/step_attention/pallas_call | solution.py:873
  240.9 5.3 %step_ada.1 = (f32[6,144,288]{2,1,0:T(8,128)}, f32[6,144,288]{2,1,0:T(8,128)}, f32[6,144,288]{2,1,0:T(8,128)}) custom-call(s32[1]{0:T(128)S(6)} %copy.50.steps, bf16[32,144]{1,0:T(8,128)(2,1)} %copy-done.30, bf16[6,32,288]{2,1,0:T(8,128)(2,1)} %copy-done.27, f32[6,144,288]{2,1,0:T(8,128)} %bitcast.54, f32[6,144,288]{2,1,0:T(8,128)} %bitcast.62, ...), custom_call_target="tpu_custom_call" | custom-call | bytes 1024 | tf_op jit(solution)/shard_map/step_ada/pallas_call | solution.py:899
  249.8 4.0 %step_fc1.1 = (f32[144,1152]{1,0:T(8,128)}, f32[144,1152]{1,0:T(8,128)}, f32[144,1152]{1,0:T(8,128)}) custom-call(s32[1]{0:T(128)} %bitcast.7.index, s32[1]{0:T(128)S(6)} %copy.50.steps, bf16[144,1152]{1,0:T(8,128)(2,1)} %copy-done.37, bf16[144,1152]{1,0:T(8,128)(2,1)} %copy-done.36, bf16[1152,1152]{1,0:T(8,128)(2,1)} %copy-done, f32[144,1152]{1,0:T(8,128)} %refs_3_.3, ...), custom_call_target="tpu_custom_call" | custom-call | bytes 1024 | tf_op jit(solution)/shard_map/step_fc1/pallas_call | solution.py:873
  (269 shorter events, 102.9 us)
Async XLA Ops:
  2.2 12.9 %collective-permute-start.3 = (bf16[144,1152]{1,0:T(8,128)(2,1)S(1)}, bf16[144,1152]{1,0:T(8,128)(2,1)S(1)}, u32[]{:S(2)}, u32[]{:S(2)}) collective-permute-start(bf16[144,1152]{1,0:T(8,128)(2,1)S(1)} %concatenate.41.refs_0_), channel_id=1, source_target_pairs={{0,8},{8,16},{16,24},{24,28},{28,20},{20,12},{12,4},{4,0},{1,9},{9... | collective-permute-start | bytes 995336 | tf_op jit(solution)/shard_map/ppermute | solution.py:118
  15.1 13.8 %collective-permute-start.6 = (bf16[144,1152]{1,0:T(8,128)(2,1)S(1)}, bf16[144,1152]{1,0:T(8,128)(2,1)S(1)}, u32[]{:S(2)}, u32[]{:S(2)}) collective-permute-start(bf16[144,1152]{1,0:T(8,128)(2,1)S(1)} %collective-permute-done.3.refs_1_), channel_id=1, source_target_pairs={{0,8},{8,16},{16,24},{24,28},{28,20},{20,12},{12,4},{4,0},{1,9},{9... | collective-permute-start | bytes 995336 | tf_op jit(solution)/shard_map/ppermute | solution.py:118
  17.1 11.9 %collective-permute-start.7 = (bf16[144,1152]{1,0:T(8,128)(2,1)S(1)}, bf16[144,1152]{1,0:T(8,128)(2,1)S(1)}, u32[]{:S(2)}, u32[]{:S(2)}) collective-permute-start(bf16[144,1152]{1,0:T(8,128)(2,1)S(1)} %collective-permute-done.4.refs_5_), channel_id=1, source_target_pairs={{8,0},{16,8},{24,16},{28,24},{20,28},{12,20},{4,12},{0,4},{9,1},{1... | collective-permute-start | bytes 995336 | tf_op jit(solution)/shard_map/ppermute | solution.py:118
  17.2 11.7 %collective-permute-start.5 = (bf16[16,8,144]{2,0,1:T(8,128)(2,1)S(1)}, bf16[16,8,144]{2,0,1:T(8,128)(2,1)S(1)}, u32[]{:S(2)}, u32[]{:S(2)}) collective-permute-start(bf16[16,8,144]{2,0,1:T(8,128)(2,1)S(1)} %pad_maximum_fusion.3), channel_id=1, source_target_pairs={{0,16},{4,20},{8,24},{12,28},{16,0},{20,4},{24,8},{28,12},{1,17},{... | collective-permute-start | bytes 110600 | tf_op jit(solution)/shard_map/ppermute | solution.py:56
  30.5 12.1 %collective-permute-start.9 = (bf16[144,1152]{1,0:T(8,128)(2,1)S(1)}, bf16[144,1152]{1,0:T(8,128)(2,1)S(1)}, u32[]{:S(2)}, u32[]{:S(2)}) collective-permute-start(bf16[144,1152]{1,0:T(8,128)(2,1)S(1)} %collective-permute-done.6.refs_2_), channel_id=1, source_target_pairs={{0,8},{8,16},{16,24},{24,28},{28,20},{20,12},{12,4},{4,0},{1,9},{9... | collective-permute-start | bytes 995336 | tf_op jit(solution)/shard_map/ppermute | solution.py:118
  42.6 11.4 %collective-permute-start.14 = (bf16[144,1152]{1,0:T(8,128)(2,1)S(1)}, bf16[144,1152]{1,0:T(8,128)(2,1)S(1)}, u32[]{:S(2)}, u32[]{:S(2)}) collective-permute-start(bf16[144,1152]{1,0:T(8,128)(2,1)S(1)} %collective-permute-done.9.refs_3_), channel_id=1, source_target_pairs={{0,8},{8,16},{16,24},{24,28},{28,20},{20,12},{12,4},{4,0},{1,9},{9... | collective-permute-start | bytes 995336 | tf_op jit(solution)/shard_map/ppermute | solution.py:118
  46.5 13.9 %collective-permute-start.18 = (bf16[144,1152]{1,0:T(8,128)(2,1)S(1)}, bf16[144,1152]{1,0:T(8,128)(2,1)}, u32[]{:S(2)}, u32[]{:S(2)}) collective-permute-start(bf16[144,1152]{1,0:T(8,128)(2,1)S(1)} %convert_element_type.37.refs_0_), channel_id=1, source_target_pairs={{0,8},{8,16},{16,24},{24,28},{28,20},{20,12},{12,4},{4,0},{1,9},{9... | collective-permute-start | bytes 995336 | tf_op jit(solution)/shard_map/ppermute | solution.py:118
  54.1 15.0 %collective-permute-start.20 = (bf16[144,1152]{1,0:T(8,128)(2,1)S(1)}, bf16[144,1152]{1,0:T(8,128)(2,1)}, u32[]{:S(2)}, u32[]{:S(2)}) collective-permute-start(bf16[144,1152]{1,0:T(8,128)(2,1)S(1)} %bitcast_convert_fusion.refs_8_.refs_0_), channel_id=1, source_target_pairs={{8,0},{16,8},{24,16},{28,24},{20,28},{12,20},{4,12},{0,4},{9,1},{1... | collective-permute-start | bytes 995336 | tf_op jit(solution)/shard_map/ppermute | solution.py:118
  58.2 10.9 %collective-permute-start.21 = (bf16[144,1152]{1,0:T(8,128)(2,1)S(1)}, bf16[144,1152]{1,0:T(8,128)(2,1)S(1)}, u32[]{:S(2)}, u32[]{:S(2)}) collective-permute-start(bf16[144,1152]{1,0:T(8,128)(2,1)S(1)} %bitcast_convert_fusion.refs_8_.refs_0_), channel_id=1, source_target_pairs={{0,8},{8,16},{16,24},{24,28},{28,20},{20,12},{12,4},{4,0},{1,9},{9... | collective-permute-start | bytes 995336 | tf_op jit(solution)/shard_map/ppermute | solution.py:118
  62.2 12.6 %collective-permute-start.22 = (bf16[144,1152]{1,0:T(8,128)(2,1)}, bf16[144,1152]{1,0:T(8,128)(2,1)S(1)}, u32[]{:S(2)}, u32[]{:S(2)}) collective-permute-start(bf16[144,1152]{1,0:T(8,128)(2,1)} %collective-permute-done.18.refs_1_), channel_id=1, source_target_pairs={{0,8},{8,16},{16,24},{24,28},{28,20},{20,12},{12,4},{4,0},{1,9},{9... | collective-permute-start | bytes 995336 | tf_op jit(solution)/shard_map/ppermute | solution.py:118
  62.2 12.6 %collective-permute-start.23 = (bf16[144,1152]{1,0:T(8,128)(2,1)}, bf16[144,1152]{1,0:T(8,128)(2,1)S(1)}, u32[]{:S(2)}, u32[]{:S(2)}) collective-permute-start(bf16[144,1152]{1,0:T(8,128)(2,1)} %collective-permute-done.19.refs_5_), channel_id=1, source_target_pairs={{8,0},{16,8},{24,16},{28,24},{20,28},{12,20},{4,12},{0,4},{9,1},{1... | collective-permute-start | bytes 995336 | tf_op jit(solution)/shard_map/ppermute | solution.py:118
  77.1 19.9 %collective-permute-start.25 = (bf16[256,1152]{1,0:T(8,128)(2,1)S(1)}, bf16[256,1152]{1,0:T(8,128)(2,1)S(1)}, u32[]{:S(2)}, u32[]{:S(2)}) collective-permute-start(bf16[256,1152]{1,0:T(8,128)(2,1)S(1)} %add_convert_fusion.3.own.attn_own), channel_id=1, source_target_pairs={{0,2},{1,3},{2,0},{3,1},{4,6},{5,7},{6,4},{7,5},{8,10},{9,11},{10,... | collective-permute-start | bytes 1769480 | tf_op jit(solution)/shard_map/ppermute | solution.py:39
  78.8 10.9 %collective-permute-start.28 = (bf16[144,1152]{1,0:T(8,128)(2,1)}, bf16[144,1152]{1,0:T(8,128)(2,1)S(1)}, u32[]{:S(2)}, u32[]{:S(2)}) collective-permute-start(bf16[144,1152]{1,0:T(8,128)(2,1)} %collective-permute-done.20.refs_9_.refs_1_), channel_id=1, source_target_pairs={{8,0},{16,8},{24,16},{28,24},{20,28},{12,20},{4,12},{0,4},{9,1},{1... | collective-permute-start | bytes 995336 | tf_op jit(solution)/shard_map/ppermute | solution.py:118
  80.6 10.7 %collective-permute-start.29 = (bf16[144,1152]{1,0:T(8,128)(2,1)S(1)}, bf16[144,1152]{1,0:T(8,128)(2,1)S(1)}, u32[]{:S(2)}, u32[]{:S(2)}) collective-permute-start(bf16[144,1152]{1,0:T(8,128)(2,1)S(1)} %collective-permute-done.21.refs_13_.refs_5_), channel_id=1, source_target_pairs={{0,8},{8,16},{16,24},{24,28},{28,20},{20,12},{12,4},{4,0},{1,9},{9... | collective-permute-start | bytes 995336 | tf_op jit(solution)/shard_map/ppermute | solution.py:118
  80.8 16.1 %collective-permute-start.26 = (bf16[144,1152]{1,0:T(8,128)(2,1)S(1)}, bf16[144,1152]{1,0:T(8,128)(2,1)S(1)}, u32[]{:S(2)}, u32[]{:S(2)}) collective-permute-start(bf16[144,1152]{1,0:T(8,128)(2,1)S(1)} %collective-permute-done.22.refs_2_), channel_id=1, source_target_pairs={{0,8},{8,16},{16,24},{24,28},{28,20},{20,12},{12,4},{4,0},{1,9},{9... | collective-permute-start | bytes 995336 | tf_op jit(solution)/shard_map/ppermute | solution.py:118
  82.8 14.2 %collective-permute-start.27 = (bf16[144,1152]{1,0:T(8,128)(2,1)S(1)}, bf16[144,1152]{1,0:T(8,128)(2,1)S(1)}, u32[]{:S(2)}, u32[]{:S(2)}) collective-permute-start(bf16[144,1152]{1,0:T(8,128)(2,1)S(1)} %collective-permute-done.23.refs_6_), channel_id=1, source_target_pairs={{8,0},{16,8},{24,16},{28,24},{20,28},{12,20},{4,12},{0,4},{9,1},{1... | collective-permute-start | bytes 995336 | tf_op jit(solution)/shard_map/ppermute | solution.py:118
  129.8 18.3 %collective-permute-start.38 = (bf16[256,1152]{1,0:T(8,128)(2,1)S(1)}, bf16[256,1152]{1,0:T(8,128)(2,1)S(1)}, u32[]{:S(2)}, u32[]{:S(2)}) collective-permute-start(bf16[256,1152]{1,0:T(8,128)(2,1)S(1)} %add_convert_fusion.2.own), channel_id=1, source_target_pairs={{0,2},{1,3},{2,0},{3,1},{4,6},{5,7},{6,4},{7,5},{8,10},{9,11},{10,... | collective-permute-start | bytes 1769480 | tf_op jit(solution)/shard_map/ppermute | solution.py:39
  130.9 10.7 %collective-permute-start.41 = (bf16[144,1152]{1,0:T(8,128)(2,1)S(1)}, bf16[144,1152]{1,0:T(8,128)(2,1)S(1)}, u32[]{:S(2)}, u32[]{:S(2)}) collective-permute-start(bf16[144,1152]{1,0:T(8,128)(2,1)S(1)} %get-tuple-element.294), channel_id=1, source_target_pairs={{8,0},{16,8},{24,16},{28,24},{20,28},{12,20},{4,12},{0,4},{9,1},{1... | collective-permute-start | bytes 995336 | tf_op jit(solution)/shard_map/ppermute | solution.py:118
  136.9 10.7 %collective-permute-start.39 = (bf16[144,1152]{1,0:T(8,128)(2,1)S(1)}, bf16[144,1152]{1,0:T(8,128)(2,1)S(1)}, u32[]{:S(2)}, u32[]{:S(2)}) collective-permute-start(bf16[144,1152]{1,0:T(8,128)(2,1)S(1)} %get-tuple-element.289), channel_id=1, source_target_pairs={{8,0},{16,8},{24,16},{28,24},{20,28},{12,20},{4,12},{0,4},{9,1},{1... | collective-permute-start | bytes 995336 | tf_op jit(solution)/shard_map/ppermute | solution.py:118
  160.2 18.2 %collective-permute-start.47 = (bf16[256,1152]{1,0:T(8,128)(2,1)S(1)}, bf16[256,1152]{1,0:T(8,128)(2,1)S(1)}, u32[]{:S(2)}, u32[]{:S(2)}) collective-permute-start(bf16[256,1152]{1,0:T(8,128)(2,1)S(1)} %add_convert_fusion.1.own), channel_id=1, source_target_pairs={{0,2},{1,3},{2,0},{3,1},{4,6},{5,7},{6,4},{7,5},{8,10},{9,11},{10,... | collective-permute-start | bytes 1769480 | tf_op jit(solution)/shard_map/ppermute | solution.py:39
  161.6 13.6 %collective-permute-start.48 = (bf16[144,1152]{1,0:T(8,128)(2,1)S(1)}, bf16[144,1152]{1,0:T(8,128)(2,1)S(1)}, u32[]{:S(2)}, u32[]{:S(2)}) collective-permute-start(bf16[144,1152]{1,0:T(8,128)(2,1)S(1)} %get-tuple-element.334), channel_id=1, source_target_pairs={{8,0},{16,8},{24,16},{28,24},{20,28},{12,20},{4,12},{0,4},{9,1},{1... | collective-permute-start | bytes 995336 | tf_op jit(solution)/shard_map/ppermute | solution.py:118
  162.4 12.8 %collective-permute-start.49 = (bf16[144,1152]{1,0:T(8,128)(2,1)S(1)}, bf16[144,1152]{1,0:T(8,128)(2,1)S(1)}, u32[]{:S(2)}, u32[]{:S(2)}) collective-permute-start(bf16[144,1152]{1,0:T(8,128)(2,1)S(1)} %get-tuple-element.335), channel_id=1, source_target_pairs={{0,8},{8,16},{16,24},{24,28},{28,20},{20,12},{12,4},{4,0},{1,9},{9... | collective-permute-start | bytes 995336 | tf_op jit(solution)/shard_map/ppermute | solution.py:118
  163.7 14.6 %collective-permute-start.50 = (bf16[144,1152]{1,0:T(8,128)(2,1)S(1)}, bf16[144,1152]{1,0:T(8,128)(2,1)S(1)}, u32[]{:S(2)}, u32[]{:S(2)}) collective-permute-start(bf16[144,1152]{1,0:T(8,128)(2,1)S(1)} %add_blocks.12), channel_id=1, source_target_pairs={{8,0},{16,8},{24,16},{28,24},{20,28},{12,20},{4,12},{0,4},{9,1},{1... | collective-permute-start | bytes 995336 | tf_op jit(solution)/shard_map/ppermute | solution.py:118
  180.4 18.0 %collective-permute-start.52 = (bf16[256,1152]{1,0:T(8,128)(2,1)S(1)}, bf16[256,1152]{1,0:T(8,128)(2,1)S(1)}, u32[]{:S(2)}, u32[]{:S(2)}) collective-permute-start(bf16[256,1152]{1,0:T(8,128)(2,1)S(1)} %add_convert_fusion.own), channel_id=1, source_target_pairs={{0,2},{1,3},{2,0},{3,1},{4,6},{5,7},{6,4},{7,5},{8,10},{9,11},{10,... | collective-permute-start | bytes 1769480 | tf_op jit(solution)/shard_map/ppermute | solution.py:39
  183.5 14.9 %collective-permute-start.55 = (bf16[144,1152]{1,0:T(8,128)(2,1)S(1)}, bf16[144,1152]{1,0:T(8,128)(2,1)S(1)}, u32[]{:S(2)}, u32[]{:S(2)}) collective-permute-start(bf16[144,1152]{1,0:T(8,128)(2,1)S(1)} %get-tuple-element.362), channel_id=1, source_target_pairs={{8,0},{16,8},{24,16},{28,24},{20,28},{12,20},{4,12},{0,4},{9,1},{1... | collective-permute-start | bytes 995336 | tf_op jit(solution)/shard_map/ppermute | solution.py:118
  184.4 14.0 %collective-permute-start.56 = (bf16[144,1152]{1,0:T(8,128)(2,1)S(1)}, bf16[144,1152]{1,0:T(8,128)(2,1)S(1)}, u32[]{:S(2)}, u32[]{:S(2)}) collective-permute-start(bf16[144,1152]{1,0:T(8,128)(2,1)S(1)} %get-tuple-element.363), channel_id=1, source_target_pairs={{0,8},{8,16},{16,24},{24,28},{28,20},{20,12},{12,4},{4,0},{1,9},{9... | collective-permute-start | bytes 995336 | tf_op jit(solution)/shard_map/ppermute | solution.py:118
  198.4 11.3 %collective-permute-start.61 = (bf16[144,1152]{1,0:T(8,128)(2,1)S(1)}, bf16[144,1152]{1,0:T(8,128)(2,1)S(1)}, u32[]{:S(2)}, u32[]{:S(2)}) collective-permute-start(bf16[144,1152]{1,0:T(8,128)(2,1)S(1)} %get-tuple-element.372), channel_id=1, source_target_pairs={{0,8},{8,16},{16,24},{24,28},{28,20},{20,12},{12,4},{4,0},{1,9},{9... | collective-permute-start | bytes 995336 | tf_op jit(solution)/shard_map/ppermute | solution.py:118
  209.7 15.1 %collective-permute-start.64 = (bf16[256,1152]{1,0:T(8,128)(2,1)S(1)}, bf16[256,1152]{1,0:T(8,128)(2,1)S(1)}, u32[]{:S(2)}, u32[]{:S(2)}) collective-permute-start(bf16[256,1152]{1,0:T(8,128)(2,1)S(1)} %get-tuple-element.386.here), channel_id=1, source_target_pairs={{0,1},{1,0},{2,3},{3,2},{4,5},{5,4},{6,7},{7,6},{8,9},{9,8},{10,11... | collective-permute-start | bytes 1769480 | tf_op jit(solution)/shard_map/ppermute | solution.py:35
  209.8 15.0 %collective-permute-start.65 = (bf16[256,1152]{1,0:T(8,128)(2,1)S(1)}, bf16[256,1152]{1,0:T(8,128)(2,1)S(1)}, u32[]{:S(2)}, u32[]{:S(2)}) collective-permute-start(bf16[256,1152]{1,0:T(8,128)(2,1)S(1)} %get-tuple-element.388.here), channel_id=1, source_target_pairs={{0,1},{1,0},{2,3},{3,2},{4,5},{5,4},{6,7},{7,6},{8,9},{9,8},{10,11... | collective-permute-start | bytes 1769480 | tf_op jit(solution)/shard_map/ppermute | solution.py:35
  210.7 13.8 %collective-permute-start.66 = (bf16[144,1152]{1,0:T(8,128)(2,1)S(1)}, bf16[144,1152]{1,0:T(8,128)(2,1)S(1)}, u32[]{:S(2)}, u32[]{:S(2)}) collective-permute-start(bf16[144,1152]{1,0:T(8,128)(2,1)S(1)} %get-tuple-element.382), channel_id=1, source_target_pairs={{0,8},{8,16},{16,24},{24,28},{28,20},{20,12},{12,4},{4,0},{1,9},{9... | collective-permute-start | bytes 995336 | tf_op jit(solution)/shard_map/ppermute | solution.py:118
  212.0 12.8 %collective-permute-start.67 = (bf16[144,1152]{1,0:T(8,128)(2,1)S(1)}, bf16[144,1152]{1,0:T(8,128)(2,1)S(1)}, u32[]{:S(2)}, u32[]{:S(2)}) collective-permute-start(bf16[144,1152]{1,0:T(8,128)(2,1)S(1)} %get-tuple-element.383), channel_id=1, source_target_pairs={{8,0},{16,8},{24,16},{28,24},{20,28},{12,20},{4,12},{0,4},{9,1},{1... | collective-permute-start | bytes 995336 | tf_op jit(solution)/shard_map/ppermute | solution.py:118
  212.8 11.6 %collective-permute-start.63 = (bf16[6,16,288]{2,1,0:T(8,128)(2,1)S(1)}, bf16[6,16,288]{2,1,0:T(8,128)(2,1)S(1)}, u32[]{:S(2)}, u32[]{:S(2)}) collective-permute-start(bf16[6,16,288]{2,1,0:T(8,128)(2,1)S(1)} %pad_maximum_fusion.2), channel_id=1, source_target_pairs={{0,16},{4,20},{8,24},{12,28},{16,0},{20,4},{24,8},{28,12},{1,17},{... | collective-permute-start | bytes 165896 | tf_op jit(solution)/shard_map/ppermute | solution.py:56
  (83 other events, 889.2 us)
